TPU v7x, 32 devices: a whole 2x2x4 slice. The times are simulated.
32 devices in a mesh: dp: 8 (over z, y), tensor: 4 (over x, core).
Axes of the slice: x: 2, y: 2, z: 4, core: 2. Of those that a mesh axis runs over, the one named last changes fastest.
Arguments:
- noisy_latents: bfloat16 [16, 256, 16], P('dp'), may hold values from -6 to 6
- noise_target: float32 [16, 256, 16], P('dp'), may hold values from -6 to 6
- timesteps: int32 [16], P('dp'), may hold values from 0 to 999
- labels: int32 [16], P('dp'), may hold values from 0 to 999
- owners: int32 [39], replicated, may hold values from 0 to 7, as said below
- step_count: int32 [1], replicated, may hold values from 2 to 20
- master_bank: float32 [64, 1024, 1024], P('dp', None, 'tensor'), may hold values from -0.1875 to 0.1875
- momentum_bank: float32 [64, 1024, 1024], P('dp', None, 'tensor'), may hold values from -0.0024414062 to 0.0024414062
- embed_tables: float32 [1288, 1024], P(None, 'tensor'), may hold values from -0.75 to 0.75
- embed_first: float32 [1288, 1024], P(None, 'tensor'), may hold values from -0.0024414062 to 0.0024414062
- embed_second: float32 [1288, 1024], P(None, 'tensor'), may hold values from 2.4414062e-08 to 9.765625e-08
Outputs:
- loss: float32 [], replicated
- master_new: float32 [64, 1024, 1024], P('dp', None, 'tensor')
- momentum_new: float32 [64, 1024, 1024], P('dp', None, 'tensor')
- embed_new: float32 [1288, 1024], P(None, 'tensor')
- first_new: float32 [1288, 1024], P(None, 'tensor')
- second_new: float32 [1288, 1024], P(None, 'tensor')
Inputs may be any that keep to these rules, and one draw needn't show every extreme that they name: `owners`: each index of dp owns at most 8 units, and one owns exactly 8.
All inputs are finite; a program needn't handle non-finite values.
Results may differ from a plain program's by a relative error of at most 0.0089.
Values may be sent and summed in bfloat16 or wider, within the bound.
No kernel may reach another device: no remote copies, remote signals or barrier semaphores. Data moves between devices by JAX's collectives and lax.ppermute only.
A program may use at most 384 MiB of HBM per device.

v0:
```python
import functools
import math

import jax
import jax.numpy as jnp
import numpy as np
from jax import lax
from jax.experimental import pallas as pl
from jax.experimental.pallas import tpu as pltpu
from jax.sharding import PartitionSpec as P

D = 1024
HEAD_DIM = 64
FREQ = 256
CLASSES = 1000
GRID = 16
LAYERS = 2
BIG = 12
N_BIG = BIG * LAYERS
SMALL_ROWS = 16
SHIFT_F, SCALE_F, TIME_AT = 0, 1, 6 * LAYERS + 2


def small_at(layer, i):
    first = 2 + 6 * (LAYERS - 1 - layer)
    return first + (4, 5, 3, 1, 2, 0)[i]


NS_COEF = (3.4445, -4.775, 2.0315)
LR_MUON = 0.5
LR_ADAM = 0.02
WEIGHT_DECAY = 0.1
SCORE_SCALE = 1.0 / math.sqrt(HEAD_DIM)
HIGHEST_PREC = lax.Precision.HIGHEST

F32 = jnp.float32
BF16 = jnp.bfloat16
SCOPE = 16
GELU_C = math.sqrt(2.0 / math.pi)
GROUPS = ((0, 4), (4, 12), (12, 16), (16, 24))


def unit_tables():
    big, small = [], []
    for u in range(18 * LAYERS):
        layer, place = divmod(u, 18)
        big.append(layer * BIG + place if place < BIG else -1)
        small.append(-1 if place < BIG else small_at(layer, place - BIG))
    return np.array(big + [-1] * 3), np.array(small + [TIME_AT, SHIFT_F, SCALE_F])


BIG_OF, SMALL_OF = unit_tables()


def params(limit, **more):
    return pltpu.CompilerParams(vmem_limit_bytes=limit * 1024 * 1024, **more)


SMEM_SPEC = pl.BlockSpec(memory_space=pltpu.SMEM)
VMEM_SPEC = pl.BlockSpec(memory_space=pltpu.VMEM)


def in_hbm(values):
    return pltpu.with_memory_space_constraint(values, pltpu.HBM)


def dot(a, b):
    return lax.dot_general(a, b, (((1,), (0,)), ((), ())), preferred_element_type=F32)


def dot_nt(a, b):
    return lax.dot_general(a, b, (((1,), (1,)), ((), ())), preferred_element_type=F32)


def dot_tn(a, b):
    return lax.dot_general(a, b, (((0,), (0,)), ((), ())), preferred_element_type=F32)


def shape(dims, kind):
    return jax.ShapeDtypeStruct(dims, kind)


ISSUED = []


def order(values, after):
    if not after:
        return values
    flat, tree = jax.tree.flatten(values)
    tied = lax.optimization_barrier(tuple(flat) + tuple(after))
    return jax.tree.unflatten(tree, tied[: len(flat)])


def drive(work, line):
    ISSUED.clear()
    try:
        value = next(work)
        while True:
            after = tuple(ISSUED)
            ISSUED.clear()
            value = work.send(order(value, line(after)))
    except StopIteration as end:
        return end.value


def together(*works):
    ends, flying = [None] * len(works), {}

    def go(i, step):
        try:
            flying[i] = step()
        except StopIteration as end:
            flying.pop(i, None)
            ends[i] = end.value

    for i, work in enumerate(works):
        go(i, lambda: next(work))
    while flying:
        got = yield dict(flying)
        for i in list(got):
            go(i, lambda: works[i].send(got[i]))
    return ends


def finish(work, value):
    try:
        work.send(value)
    except StopIteration as end:
        return end.value
    raise AssertionError


def flip(values, axis, bit, size):
    ISSUED.append(values)
    got = lax.ppermute(values, axis, [(i, i ^ bit) for i in range(size)])
    if axis == "tensor" and values.size < 2**16:
        ISSUED.append(got)
    return got


def is_at(flag, value, ndim):
    return flag.reshape((1,) * ndim) == value


def pick(low, high, place, other=False):
    return jnp.where(is_at(place, 1 if other else 0, low.ndim), low, high)


def own_latents(values, axis, data, n_data):
    n_lat = values.shape[axis]
    dims = values.shape[:axis] + (n_lat * n_data,) + values.shape[axis + 1 :]
    at = lax.broadcasted_iota(jnp.int32, dims, axis)
    first = data.reshape((1,) * len(dims)) * n_lat
    placed = jnp.zeros(dims, values.dtype)
    for l in range(n_lat):
        placed = jnp.where(at == first + l, lax.slice_in_dim(values, l, l + 1, axis=axis), placed)
    return placed


def dp_sum(values, n_data):
    bit = 1
    while bit < n_data:
        values = values + (yield flip(values, "dp", bit, n_data))
        bit *= 2
    return values


def dp_rows(values, n_data):
    bit = 1
    while bit < n_data:
        values = jnp.concatenate([values, (yield flip(values, "dp", bit, n_data))], 0)
        bit *= 2
    return values


def core_flip(values):
    return flip(values, "tensor", 1, 4)


def x_flip(values):
    return flip(values, "tensor", 2, 4)


def gather_tokens(own):
    beside, across = yield (core_flip(own), x_flip(own))
    return own, beside, across, core_flip(across)


def gather_columns(own, chip, core):
    beside, across = yield (core_flip(own), x_flip(own))
    corner = core_flip(across)
    at_core = [is_at(core, i, own.ndim) for i in range(2)]
    at_chip = [is_at(chip, i, own.ndim) for i in range(2)]
    near = [jnp.where(at_core[i], own, beside) for i in range(2)]
    far = [jnp.where(at_core[i], across, corner) for i in range(2)]
    parts = [jnp.where(at_chip[i], near[j], far[j]) for i in range(2) for j in range(2)]
    return jnp.concatenate(parts, -1)


def scatter_tokens(keep, send):
    got = core_flip(send)
    far = (keep[1] + got[1].astype(F32)).astype(BF16)
    return keep, got, (yield x_flip(far))


def core_columns(values, core, other=False):
    size = values.shape[-1] // 4
    block = [lax.slice_in_dim(values, j * size, (j + 1) * size, axis=values.ndim - 1) for j in range(4)]
    return [pick(block[2 * x], block[2 * x + 1], core, other) for x in range(2)]


def core_columns_sum(values, core):
    got = core_flip(jnp.concatenate(core_columns(values, core, True), -1))
    size = got.shape[-1] // 2
    return [
        mine + lax.slice_in_dim(got, x * size, (x + 1) * size, axis=got.ndim - 1)
        for x, mine in enumerate(core_columns(values, core))
    ]


def own_columns_sum(values, chip, core):
    mine = core_columns_sum(values, core)
    return pick(*mine, chip) + (yield x_flip(pick(*mine, chip, True)))


def sum_of_columns(values, chip, core, n_data):
    return (yield from dp_sum((yield from own_columns_sum(values, chip, core)), n_data))


def ring_order(n_data):
    return [0, 2, 4, 6, 7, 5, 3, 1] if n_data == 8 else list(range(n_data))


def sched_kernel(steps, depth, n_data, place_ref, own_ref, next_ref, out_ref):
    lane = lax.broadcasted_iota(jnp.int32, (n_data, 128), 1)
    row = lax.broadcasted_iota(jnp.int32, (n_data, 128), 0)
    far = jnp.int32(999)
    out_lane = lax.broadcasted_iota(jnp.int32, (1, 128), 1)

    def step(t, carry):
        line = jnp.full((1, 128), -1, jnp.int32)
        after = []
        for way in range(2):
            have, sent, *coming = carry[way]
            place = place_ref[way]
            before = jnp.where(place == 0, n_data - 1, place - 1)
            open_now = have * (1 - sent) * (1 - next_ref[way])
            first = jnp.min(jnp.where(open_now > 0, lane, far), axis=1, keepdims=True)
            chosen = (lane == first).astype(jnp.int32)
            first = jnp.broadcast_to(first, (n_data, 128))
            for k, who in enumerate((place, before)):
                index = jnp.min(jnp.where(row == who, first, far), axis=0, keepdims=True)
                index = jnp.where(index == far, -1, index)
                line = jnp.where(out_lane == 2 * way + k, index, line)
            coming = list(coming) + [pltpu.roll(chosen, 1, 0)]
            after.append((have + coming[0], sent + chosen, *coming[1:]))
        out_ref[pl.ds(t, 1), :] = line
        return tuple(after)

    none = jnp.zeros((n_data, 128), jnp.int32)
    lax.fori_loop(0, steps, step, tuple((own_ref[way], none) + (none,) * (depth - 1) for way in range(2)))


def ring_schedule(owners_big, n_data, steps, depth, my_data):
    order = np.array(ring_order(n_data))
    place_of = np.argsort(order)
    place = jnp.sum(jnp.where(jnp.arange(n_data) == my_data, place_of, 0)).astype(jnp.int32)
    at = jnp.arange(n_data)[:, None]
    owner_place = jnp.sum(jnp.where(owners_big[:, None] == jnp.arange(n_data)[None], place_of[None], 0), 1)
    owner_place = jnp.concatenate([owner_place, jnp.full((128 - N_BIG,), -9, owner_place.dtype)])[None]
    back_place = jnp.where(owner_place >= 0, n_data - 1 - owner_place, -9)
    own = jnp.stack([at == owner_place, at == back_place]).astype(jnp.int32)
    follow = (at + 1) % n_data
    nxt = jnp.stack([follow == owner_place, follow == back_place]).astype(jnp.int32)
    out = pl.pallas_call(
        functools.partial(sched_kernel, steps, depth, n_data),
        out_shape=shape((steps, 128), jnp.int32),
        in_specs=[
            pl.BlockSpec(memory_space=pltpu.SMEM),
            pl.BlockSpec(memory_space=pltpu.VMEM),
            pl.BlockSpec(memory_space=pltpu.VMEM),
        ],
        out_specs=pl.BlockSpec(memory_space=pltpu.VMEM),
        name="ring_schedule",
    )(jnp.stack([place, n_data - 1 - place]), own, nxt)
    return out[:, :4]


def spread_init_kernel(slots_ref, bank_ref, out_ref, wide, sem):
    big_ref = [slots_ref[0, s] for s in range(bank_ref.shape[0])]
    n_slots = bank_ref.shape[0]
    for s in range(n_slots):
        copy = pltpu.make_async_copy(bank_ref.at[s], wide.at[s], sem.at[s])
        pl.when(big_ref[s] >= 0)(copy.start)
    for s in range(n_slots):
        copy = pltpu.make_async_copy(bank_ref.at[s], wide.at[s], sem.at[s])
        pl.when(big_ref[s] >= 0)(copy.wait)

        @pl.when(big_ref[s] >= 0)
        def _(s=s):
            out_ref[jnp.maximum(big_ref[s], 0)] = wide[s].astype(BF16)


def spread_init(big_slots, master_bank):
    n_slots, rows, columns = master_bank.shape
    return pl.pallas_call(
        spread_init_kernel,
        out_shape=pltpu.VMEM((N_BIG + BIG, rows, columns), BF16),
        in_specs=[SMEM_SPEC, pl.BlockSpec(memory_space=pltpu.HBM)],
        out_specs=VMEM_SPEC,
        scratch_shapes=[
            pltpu.VMEM((n_slots, rows, columns), F32),
            pltpu.SemaphoreType.DMA((n_slots,)),
        ],
        compiler_params=params(SCOPE),
        name="own_weights",
    )(big_slots, in_hbm(master_bank))


def spread_kernel(places, fetch_at, tab_ref, got, held, out):
    half = held.shape[1] // 2
    for way in range(2):
        rows = pl.ds(way * half, half)
        for k, t in enumerate(places):
            unit = tab_ref[t, 2 * way + 1]

            @pl.when(unit >= 0)
            def _():
                held[jnp.maximum(unit, 0), rows] = got[2 * k + way][...]

        if fetch_at is not None:
            out[way][...] = held[jnp.maximum(tab_ref[fetch_at, 2 * way], 0), rows]


def ring_step(name, tab, held, got, sends, body, work=None, mail=(), mail_rows=0, keep_rows=0):
    rows, columns = held.shape[1:]
    extra, more, operands, shapes, scratch = (tuple(work) + ([],))[:5] if work else ("", None, [], [], [])
    specs = [value[1] if isinstance(value, tuple) else VMEM_SPEC for value in operands]
    operands = [value[0] if isinstance(value, tuple) else value for value in operands]
    operands, specs = list(mail) + list(operands), [VMEM_SPEC] * len(mail) + specs
    n, m, k = len(got), len(operands), len(mail)
    kept = 2 if keep_rows else 0
    shapes = [pltpu.VMEM((keep_rows, columns), BF16)] * kept + list(shapes)

    def kernel(tab_ref, *refs):
        out = refs[n + 1 + m :]
        if body is not None:
            body(tab_ref, refs[:n], out[0], out[1 : 1 + sends], *([refs[n + 1 : n + 1 + k]] if k else []))
        for way in range(kept):
            out[1 + sends + way][...] = refs[way][refs[way].shape[0] - keep_rows :]
        if more is not None:
            more(out[0], *refs[n + 1 + k : n + 1 + m], *out[1 + sends + kept :])

    res = pl.pallas_call(
        kernel,
        out_shape=[pltpu.VMEM(held.shape, held.dtype)] + [pltpu.VMEM((rows // 2 + mail_rows, columns), BF16)] * sends
        + list(shapes),
        in_specs=[SMEM_SPEC] + [VMEM_SPEC] * (n + 1) + specs,
        out_specs=[VMEM_SPEC] * (1 + sends + len(shapes)),
        scratch_shapes=scratch,
        input_output_aliases={1 + n: 0},
        compiler_params=params(SCOPE),
        name=name + extra,
    )(tab, *got, held, *operands)
    return res[0], list(res[1 : 1 + sends]), list(res[1 + sends :])


def ring_perms(n_data):
    order = ring_order(n_data)
    ahead = [(order[i], order[(i + 1) % n_data]) for i in range(n_data)]
    return ahead, [(b, a) for a, b in ahead]


class Spreader:
    def __init__(self, tab, held, n_data, steps, depth):
        self.tab, self.n_data, self.steps, self.depth = tab, n_data, steps, depth
        self.perms = ring_perms(n_data)
        self.held = held
        self.got = {}
        self.at = 0

    def last(self, g):
        return GROUPS[g][1] - 1 + (self.n_data - 2) * self.depth

    def step(self, after=()):
        self.work(None, after)
        return self.sent

    def work(self, work, after=()):
        t = self.at
        self.sent = ()
        if t > self.steps:
            return []
        fetch_at = t if t < self.steps else None
        places = [t - self.depth] if fetch_at is not None else list(range(self.steps - self.depth, self.steps))
        places = [p for p in places if p >= 0]
        self.held, sends, results = ring_step(
            "spread_step",
            order(self.tab, after),
            self.held,
            [value for p in places for value in self.got.pop(p)],
            0 if fetch_at is None else 2,
            functools.partial(spread_kernel, places, fetch_at),
            work,
        )
        if fetch_at is not None:
            self.got[t] = [lax.ppermute(sends[way], "dp", self.perms[way]) for way in range(2)]
        self.at += 1
        self.sent = tuple(sends) + tuple(self.got.get(t - 1, ()))
        return order(results, tuple(self.got.get(t - 1, ())))

    def prepare(self, g):
        while self.at < min(self.last(g) + self.depth, self.steps):
            self.step()


def reduce_kernel(place_at, fetch_at, mail, tab_ref, got, held, out, own=()):
    half = held.shape[1] // 2
    if mail:
        for way in range(2):
            out[way][half:] = own[0][...] if mail == "own" else got[way][half:]
    for way in range(2):
        rows = pl.ds(way * half, half)
        if place_at is not None:
            unit = tab_ref[place_at, 2 * way]

            @pl.when(unit >= 0)
            def _():
                at = BIG + jnp.maximum(unit, 0)
                held[at, rows] = (held[at, rows].astype(F32) + got[way][:half].astype(F32)).astype(BF16)

        out[way][:half] = held[BIG + jnp.maximum(tab_ref[fetch_at, 2 * way + 1], 0), rows]


class Reducer:
    def __init__(self, tab, n_data, steps, depth):
        self.tab, self.n_data, self.steps, self.depth = tab, n_data, steps, depth
        self.perms = [p for p in reversed(ring_perms(n_data))]
        self.held = None
        self.ready = N_BIG
        self.mail = {}
        self.come = {}
        self.got = {}
        self.at = 0

    def lowest(self, k):
        return (self.steps - 1 - k) - (self.n_data - 2) * self.depth

    def step(self, after=()):
        k = self.at
        self.sent = ()
        if k < self.steps and max(self.lowest(k), 0) >= self.ready:
            self.work(None, after)
        return self.sent

    def work(self, work, after=()):
        k = self.at
        self.sent = ()
        tab = order(self.tab, after)
        if k >= self.steps or max(self.lowest(k), 0) < self.ready:
            self.held, unused, results = ring_step("layer_", tab, self.held, [], 0, None, work)
            return results
        place_at = self.steps - 1 - (k - self.depth) if k >= self.depth else None
        payload, hops = self.mail.get(k, (None, 0))
        mail = None if payload is None else "own" if hops == 0 else "pass"
        keep_rows = self.mail[k - self.depth][0].shape[0] if k - self.depth in self.mail else 0
        self.held, sends, results = ring_step(
            "reduce_step",
            tab,
            self.held,
            self.got.get(k - self.depth, []),
            2,
            functools.partial(reduce_kernel, place_at, self.steps - 1 - k, mail),
            work,
            [payload] if mail == "own" else [],
            0 if payload is None else payload.shape[0],
            keep_rows,
        )
        if keep_rows:
            self.come[k - self.depth], results = results[:2], results[2:]
        self.got[k] = [lax.ppermute(sends[way], "dp", self.perms[way]) for way in range(2)]
        self.at += 1
        self.sent = tuple(sends) + tuple(self.got.get(k - 1, ()))
        return order(results, tuple(self.got.get(k - 1, ())))

    def gather(self, payload, place):
        far = self.n_data // 2
        start, last = self.at, self.at + (far - 1) * self.depth
        assert last + self.depth < self.steps
        for j in range(far):
            self.mail[start + j * self.depth] = (payload, j)
        while self.at <= last + self.depth:
            yield ()
        come = [[self.come[start + j * self.depth][way] for j in range(far)] for way in range(2)]
        come = order(come, self.sent)
        at = [payload] + come[0][: far - 1] + come[1][::-1]
        everyone = []
        for d in range(self.n_data):
            ahead = ring_order(self.n_data).index(d) - place.reshape((1, 1))
            ahead = jnp.where(ahead < 0, ahead + self.n_data, ahead)
            value = at[0]
            for i in range(1, self.n_data):
                value = jnp.where(ahead == i, at[i], value)
            everyone.append(value)
        return everyone

    def drain(self):
        while self.at < self.steps:
            self.step()

    def last(self):
        return [self.got[self.steps - 1 - t][way] for t in range(self.depth) for way in range(2)]


def past(kernel, operands, beside):
    n, m = len(operands), len(beside)
    return lambda *refs: kernel(*refs[:n], *refs[n + m :])


def split_rows(total, keep_ref, send_ref):
    rows = total.shape[0] // 4
    for i in range(2):
        keep_ref[i] = total[2 * i * rows : (2 * i + 1) * rows]
        send_ref[i] = total[(2 * i + 1) * rows : (2 * i + 2) * rows].astype(BF16)


def part_shapes(rows, width):
    return [shape((2, rows // 4, width), F32), shape((2, rows // 4, width), BF16)]


def joined(refs):
    return jnp.concatenate([r[...] for r in refs], 0)


def softmax_parts(q, k):
    scores = dot_nt(q, k) * SCORE_SCALE
    expo = jnp.exp(scores - jnp.max(scores, -1, keepdims=True))
    return expo / jnp.sum(expo, -1, keepdims=True)


def attention_kernel(n_lat, base, w_ref, x0, x1, x2, x3, qkv_ref, mixed_ref, keep_ref, send_ref):
    x = joined((x0, x1, x2, x3))
    for j in range(3):
        qkv_ref[j] = dot(x, w_ref[base + j]).astype(BF16)
    toks = x.shape[0] // n_lat
    heads = w_ref.shape[2] // HEAD_DIM
    for l in range(n_lat):
        rows = slice(l * toks, (l + 1) * toks)
        outs = []
        for h in range(heads):
            cols = slice(h * HEAD_DIM, (h + 1) * HEAD_DIM)
            q, k, v = (qkv_ref[j, rows, cols] for j in range(3))
            outs.append(dot(softmax_parts(q, k).astype(BF16), v))
        mixed_ref[rows, :] = jnp.concatenate(outs, 1).astype(BF16)
    split_rows(dot_nt(mixed_ref[...], w_ref[base + 3]), keep_ref, send_ref)


def attention(x, columns, base, n_lat):
    rows, width = 4 * x[0].shape[0], x[0].shape[1]
    shapes = [shape((3, rows, columns), BF16), shape((rows, columns), BF16)] + part_shapes(rows, width)
    return "_attention", functools.partial(attention_kernel, n_lat, base), x, shapes


def gelu(x):
    return 0.5 * x * (1.0 + jnp.tanh(GELU_C * (x + 0.044715 * x * x * x)))


def gelu_grad(x):
    t = jnp.tanh(GELU_C * (x + 0.044715 * x * x * x))
    return 0.5 * (1.0 + t) + 0.5 * x * (1.0 - t * t) * (GELU_C * (1.0 + 3 * 0.044715 * x * x))


def mlp_kernel(base, w_ref, x0, x1, x2, x3, hidden_ref, active_ref, keep_ref, send_ref):
    x = joined((x0, x1, x2, x3))
    total = None
    for j in range(4):
        hidden = dot(x, w_ref[base + j])
        hidden_ref[j] = hidden
        active = gelu(hidden).astype(BF16)
        active_ref[j] = active
        part = dot_nt(active, w_ref[base + 4 + j])
        total = part if total is None else total + part
    split_rows(total, keep_ref, send_ref)


def mlp(x, columns, base):
    rows, width = 4 * x[0].shape[0], x[0].shape[1]
    shapes = [shape((4, rows, columns), F32), shape((4, rows, columns), BF16)] + part_shapes(rows, width)
    return "_mlp", functools.partial(mlp_kernel, base), x, shapes


def mlp_back_kernel(base, w_ref, d0, d1, d2, d3, hidden_ref, dh_ref, keep_ref, send_ref):
    d = joined((d0, d1, d2, d3))
    total = None
    for j in range(4):
        dh = (gelu_grad(hidden_ref[j]) * dot(d, w_ref[base + 4 + j])).astype(BF16)
        dh_ref[j] = dh
        part = dot_nt(dh, w_ref[base + j])
        total = part if total is None else total + part
    split_rows(total, keep_ref, send_ref)


def mlp_back(d, hidden, base):
    rows, width = 4 * d[0].shape[0], d[0].shape[1]
    shapes = [shape(hidden.shape, BF16)] + part_shapes(rows, width)
    return "_mlp_back", functools.partial(mlp_back_kernel, base), [*d, hidden], shapes


def attention_back_kernel(n_lat, base, w_ref, d0, d1, d2, d3, qkv_ref, dqkv_ref, keep_ref, send_ref):
    d_mixed = dot(joined((d0, d1, d2, d3)), w_ref[base + 3]).astype(BF16)
    toks = d_mixed.shape[0] // n_lat
    heads = w_ref.shape[2] // HEAD_DIM
    for l in range(n_lat):
        rows = slice(l * toks, (l + 1) * toks)
        outs = [[], [], []]
        for h in range(heads):
            cols = slice(h * HEAD_DIM, (h + 1) * HEAD_DIM)
            q, k, v = (qkv_ref[j, rows, cols] for j in range(3))
            do = d_mixed[rows, cols]
            probs = softmax_parts(q, k)
            d_probs = dot_nt(do, v)
            d_scores = probs * (d_probs - jnp.sum(probs * d_probs, -1, keepdims=True))
            d_scores = d_scores.astype(BF16)
            outs[0].append(dot(d_scores, k) * SCORE_SCALE)
            outs[1].append(dot_tn(d_scores, q) * SCORE_SCALE)
            outs[2].append(dot_tn(probs.astype(BF16), do))
        for j in range(3):
            dqkv_ref[j, rows, :] = jnp.concatenate(outs[j], 1).astype(BF16)
    total = sum(dot_nt(dqkv_ref[j], w_ref[base + j]) for j in range(3))
    split_rows(total, keep_ref, send_ref)


def attention_back(d, qkv, base, n_lat):
    rows, width = 4 * d[0].shape[0], d[0].shape[1]
    shapes = [shape(qkv.shape, BF16)] + part_shapes(rows, width)
    return "_attention_back", functools.partial(attention_back_kernel, n_lat, base), [*d, qkv], shapes


def weight_grad_kernel(counts, n_lat, base, out_ref, *refs):
    n = len(counts)
    lefts, rights, (mean_ref, sum_ref) = refs[: 4 * n], refs[4 * n : 5 * n], refs[-2:]
    at = 0
    for k, count in enumerate(counts):
        a = joined(lefts[4 * k : 4 * k + 4])
        toks = a.shape[0] // n_lat

        def rows_of(x, scale):
            parts = [
                jnp.sum(x[l * toks : (l + 1) * toks].astype(F32), 0, keepdims=True) * scale for l in range(n_lat)
            ]
            return jnp.concatenate(parts + [jnp.zeros((8 - n_lat, x.shape[1]), F32)], 0).astype(BF16)

        mean = rows_of(a, 1.0 / toks)
        mean_ref[k] = mean.astype(F32)
        for j in range(count):
            b = rights[k][j]
            total = rows_of(b, 1.0)
            sum_ref[at] = total.astype(F32)
            out_ref[BIG + base + at] = (dot_tn(a, b) - dot_tn(mean, total)).astype(BF16)
            at += 1


def weight_grads(base, pairs, n_lat):
    counts = [right.shape[0] for _, right in pairs]
    width, columns = pairs[0][0][0].shape[1], pairs[0][1].shape[2]
    operands = [part for left, _ in pairs for part in left] + [right for _, right in pairs]
    shapes = [shape((len(pairs), 8, width), F32), shape((sum(counts), 8, columns), F32)]
    return "_weight_grads", functools.partial(weight_grad_kernel, counts, n_lat, base), operands, shapes


def small_weights(small_ref, bank_ref, wide, sem, use):
    units = [small_ref[s] for s in range(bank_ref.shape[0])]
    ours = [(unit >= 0) & (unit != TIME_AT) for unit in units]
    copies = [pltpu.make_async_copy(bank_ref.at[s], wide.at[s], sem.at[s]) for s in range(len(units))]
    for s, copy in enumerate(copies):
        pl.when(ours[s])(copy.start)
    for s, copy in enumerate(copies):

        @pl.when(ours[s])
        def _(s=s, copy=copy):
            copy.wait()
            use(jnp.maximum(units[s], 0), wide[s].astype(BF16))


def modulation_kernel(held_ref, small_ref, cond_ref, bank_ref, out_ref, wide, sem):
    out_ref[...] = jnp.zeros_like(out_ref)

    def use(unit, weight):
        out_ref[unit] = dot(cond_ref[...], weight)

    small_weights(small_ref, bank_ref, wide, sem, use)


def bank_scratch(bank):
    return [pltpu.VMEM(bank.shape, F32), pltpu.SemaphoreType.DMA((bank.shape[0],))]


def modulations(small_slots, cond_in, bank):
    operands = [(small_slots, SMEM_SPEC), cond_in, (in_hbm(bank), pl.BlockSpec(memory_space=pltpu.HBM))]
    shapes = [shape((SMALL_ROWS, cond_in.shape[0], bank.shape[2]), F32)]
    return "_modulations", modulation_kernel, operands, shapes, bank_scratch(bank)


def cond_back_kernel(held_ref, small_ref, d_ref, bank_ref, out_ref, wide, sem):
    out_ref[...] = jnp.zeros_like(out_ref)

    def use(unit, weight):
        out_ref[...] += dot_nt(d_ref[unit], weight)

    small_weights(small_ref, bank_ref, wide, sem, use)


def cond_back(small_slots, d_small, bank):
    operands = [(small_slots, SMEM_SPEC), d_small, (in_hbm(bank), pl.BlockSpec(memory_space=pltpu.HBM))]
    return "_cond_back", cond_back_kernel, operands, [shape((d_small.shape[1], bank.shape[1]), F32)], bank_scratch(bank)


def halves(x):
    high = x.astype(BF16)
    return high, (x - high.astype(F32)).astype(BF16)


def newton_sweep_coarse(x):
    xh = x.astype(BF16)
    gram = dot_tn(xh, xh)
    gh = gram.astype(BF16)
    poly = NS_COEF[1] * gram + NS_COEF[2] * dot(gh, gh)
    return NS_COEF[0] * x + dot(xh, poly.astype(BF16))


def newton_sweep(x):
    xh, xl = halves(x)
    cross = dot_tn(xh, xl)
    gram = dot_tn(xh, xh) + (cross + cross.T)
    gh, gl = halves(gram)
    cross = dot(gh, gl)
    square = dot(gh, gh) + (cross + cross.T)
    ph, pl_ = halves(NS_COEF[1] * gram + NS_COEF[2] * square)
    return NS_COEF[0] * x + (dot(xh, ph) + (dot(xl, ph) + dot(xh, pl_)))


def newton_kernel(n_last, big_ref, left_ref, right_ref, tab_ref, a_ref, b_ref, bank_ref, mom_ref, *refs):
    held, got = refs[0], refs[1 : 1 + n_last]
    new_ref, mom_new_ref, grad, sem = refs[1 + n_last :]
    s = pl.program_id(0)
    unit, left, right = big_ref[s], left_ref[s], right_ref[s]
    half = got[0].shape[0]

    @pl.when(right < 0)
    def _():
        new_ref[...] = bank_ref[...]
        mom_new_ref[...] = mom_ref[...]

    @pl.when(right >= 0)
    def _():
        copy = pltpu.make_async_copy(held.at[BIG + jnp.maximum(unit, 0)], grad, sem.at[0])
        pl.when(unit >= 0)(copy.start)
        mom_new_ref[0] = 0.5 * mom_ref[0] + dot_tn(
            a_ref[jnp.maximum(left, 0)], b_ref[jnp.maximum(right, 0)]
        )
        pl.when(unit >= 0)(copy.wait)

        @pl.when(unit >= 0)
        def _():
            mom_new_ref[0] += grad[...].astype(F32)

        for i in range(n_last):
            rows = slice((i % 2) * half, (i % 2 + 1) * half)

            @pl.when((tab_ref[i // 2, 2 * (i % 2)] == unit) & (unit >= 0))
            def _(i=i, rows=rows):
                mom_new_ref[0, rows] += got[i][...].astype(F32)

        block = mom_new_ref[0]
        norm = jnp.sqrt(jnp.sum(block * block)) + 1e-07
        x = block / norm
        for sweep in range(5):
            x = newton_sweep_coarse(x) if sweep < 3 else newton_sweep(x)
        new_ref[0] = bank_ref[0] - LR_MUON * x


def optimizer(big_slots, left_slots, right_slots, tab, a_all, b_all, master, momentum, held, got):
    n_slots, rows, columns = master.shape
    block = pl.BlockSpec((1, rows, columns), lambda s, *t: (s, 0, 0))
    return pl.pallas_call(
        functools.partial(newton_kernel, len(got)),
        grid_spec=pltpu.PrefetchScalarGridSpec(
            num_scalar_prefetch=4,
            grid=(n_slots,),
            in_specs=[
                pl.BlockSpec(a_all.shape, lambda s, *t: (0, 0, 0)),
                pl.BlockSpec(b_all.shape, lambda s, *t: (0, 0, 0)),
                block,
                block,
            ]
            + [pl.BlockSpec(memory_space=pl.ANY)]
            + [pl.BlockSpec(g.shape, lambda s, *t: (0, 0)) for g in got],
            out_specs=[block, block],
            scratch_shapes=[pltpu.VMEM((rows, columns), BF16), pltpu.SemaphoreType.DMA((1,))],
        ),
        out_shape=[shape(master.shape, F32), shape(momentum.shape, F32)],
        compiler_params=params(SCOPE, dimension_semantics=("arbitrary",)),
        name="optimizer",
    )(big_slots, left_slots, right_slots, tab, a_all, b_all, in_hbm(master), in_hbm(momentum), held, *got)


def layer_norm(values):
    centered = values - jnp.mean(values, -1, keepdims=True)
    inv_std = lax.rsqrt(jnp.mean(centered * centered, -1, keepdims=True) + 1e-06)
    return centered * inv_std, inv_std


def norm_back(grad_out, normed, inv_std):
    return inv_std * (
        grad_out
        - jnp.mean(grad_out, -1, keepdims=True)
        - normed * jnp.mean(grad_out * normed, -1, keepdims=True)
    )


def added(keep_ref, got_ref, far_ref):
    return keep_ref[0] + got_ref[0].astype(F32) + far_ref[...].astype(F32)


def row_of(mods_ref, at):
    return mods_ref[at : at + 1, :]


def enter_kernel(at, noisy_ref, patch_ref, place_ref, mods_ref, stream_ref, inner_ref, normed_ref, inv_ref):
    stream = dot(noisy_ref[...], patch_ref[...]) + place_ref[...]
    stream_ref[...] = stream
    normed, inv = layer_norm(stream)
    inner_ref[...] = (normed * (1.0 + row_of(mods_ref, at[1])) + row_of(mods_ref, at[0])).astype(BF16)
    normed_ref[...] = normed
    inv_ref[...] = jnp.broadcast_to(inv, inv_ref.shape)


def enter(noisy, patch, places, mods, at):
    rows, width = places.shape
    full = shape((rows, width), F32)
    return pl.pallas_call(
        functools.partial(enter_kernel, at),
        out_shape=[full, shape((rows, width), BF16), full, shape((rows, 128), F32)],
        compiler_params=params(SCOPE),
        name="enter",
    )(noisy, patch, places, mods)


def residual_kernel(
    at, keep_ref, got_ref, far_ref, stream_ref, mods_ref, part_ref, next_ref, inner_ref, normed_ref, inv_ref
):
    part = added(keep_ref, got_ref, far_ref)
    part_ref[...] = part
    stream = stream_ref[...] + row_of(mods_ref, at[0]) * part
    next_ref[...] = stream
    normed, inv = layer_norm(stream)
    inner_ref[...] = (normed * (1.0 + row_of(mods_ref, at[2])) + row_of(mods_ref, at[1])).astype(BF16)
    normed_ref[...] = normed
    inv_ref[...] = jnp.broadcast_to(inv, inv_ref.shape)


def residual(parts, stream, mods, at):
    rows, width = stream.shape
    full = shape((rows, width), F32)
    return pl.pallas_call(
        functools.partial(residual_kernel, at),
        out_shape=[full, full, shape((rows, width), BF16), full, shape((rows, 128), F32)],
        compiler_params=params(SCOPE),
        name="residual",
    )(*parts, stream, mods)


def leave_kernel(
    at,
    count_all,
    keep_ref,
    got_ref,
    far_ref,
    stream_ref,
    mods_ref,
    head_ref,
    target_ref,
    grad_ref,
    next_ref,
    rows_ref,
    edge_ref,
):
    branch = added(keep_ref, got_ref, far_ref)
    gate, shift, scale = (row_of(mods_ref, i) for i in at)
    normed, inv = layer_norm(stream_ref[...] + gate * branch)
    inner = (normed * (1.0 + scale) + shift).astype(BF16)
    head = head_ref[...]
    error = dot_nt(inner, head) - target_ref[...]
    d_output = (2.0 * error / count_all).astype(BF16)
    d_inner = dot(d_output, head)
    grad = norm_back(d_inner * (1.0 + scale), normed, inv)
    grad_ref[...] = grad
    next_ref[...] = (gate * grad).astype(BF16)
    rows_ref[...] = jnp.zeros_like(rows_ref)
    rows_ref[0:1, :] = jnp.sum(d_inner, 0, keepdims=True)
    rows_ref[1:2, :] = jnp.sum(d_inner * normed, 0, keepdims=True)
    rows_ref[2:3, :] = jnp.sum(grad * branch, 0, keepdims=True)
    n_patch = head.shape[0]
    loss = jnp.sum(jnp.sum(error * error, 1, keepdims=True), 0, keepdims=True) / count_all
    edge_ref[:n_patch, :] = dot_tn(d_output, inner)
    edge_ref[n_patch:, :] = jnp.broadcast_to(loss, (8, edge_ref.shape[1]))


def leave(parts, stream, mods, head, target, at, count_all):
    rows, width = stream.shape
    return pl.pallas_call(
        functools.partial(leave_kernel, at, count_all),
        out_shape=[
            shape((rows, width), F32),
            shape((rows, width), BF16),
            shape((SMALL_ROWS, width), F32),
            shape((head.shape[0] + 8, width), F32),
        ],
        compiler_params=params(SCOPE),
        name="leave",
    )(*parts, stream, mods, head, target)


def back_kernel(
    at,
    gate_at,
    first,
    keep_ref,
    got_ref,
    far_ref,
    normed_ref,
    inv_ref,
    grad_ref,
    part_ref,
    mods_ref,
    rows_in_ref,
    out_ref,
    next_ref,
    rows_ref,
):
    d_inner = added(keep_ref, got_ref, far_ref)
    normed = normed_ref[...]
    inv = inv_ref[:, 0:1]
    grad = grad_ref[...] + norm_back(d_inner * (1.0 + row_of(mods_ref, at)), normed, inv)
    out_ref[...] = grad
    rows_ref[...] = rows_in_ref[...]
    rows_ref[first : first + 1, :] = jnp.sum(d_inner, 0, keepdims=True)
    rows_ref[first + 1 : first + 2, :] = jnp.sum(d_inner * normed, 0, keepdims=True)
    if gate_at is None:
        next_ref[...] = grad.astype(BF16)
    else:
        next_ref[...] = (row_of(mods_ref, gate_at) * grad).astype(BF16)
        rows_ref[first + 2 : first + 3, :] = jnp.sum(grad * part_ref[...], 0, keepdims=True)


def back(parts, normed, inv, grad, part, mods, rows_in, at, gate_at, first, beside):
    rows, width = grad.shape
    operands = (*parts, normed, inv, grad, part, mods, rows_in)
    return pl.pallas_call(
        past(functools.partial(back_kernel, at, gate_at, first), operands, beside),
        out_shape=[shape((rows, width), F32), shape((rows, width), BF16), shape(rows_in.shape, F32)],
        compiler_params=params(SCOPE),
        name="back",
    )(*operands, *beside)


def tables_kernel(n_patch, fix_ref, edge_ref, time_ref, class_ref, table_ref, first_ref, second_ref, *outs):
    new_ref, first_new_ref, second_new_ref = outs
    at = 0
    for ref, low, count in (
        (edge_ref, 0, n_patch),
        (time_ref, 0, FREQ),
        (class_ref, 0, CLASSES),
        (edge_ref, n_patch, n_patch),
    ):
        rows = slice(at, at + count)
        grad = ref[low : low + count, :]
        first = 0.5 * first_ref[rows, :] + 0.5 * grad
        second = 0.5 * second_ref[rows, :] + 0.5 * grad * grad
        first_new_ref[rows, :] = first
        second_new_ref[rows, :] = second
        new_ref[rows, :] = table_ref[rows, :] * (1.0 - LR_ADAM * WEIGHT_DECAY) - LR_ADAM * (
            first / fix_ref[0]
        ) / (jnp.sqrt(second / fix_ref[0]) + 1e-08)
        at += count


def update_tables(n_patch, bias_fix, edges, grad_time, grad_class, table, first, second):
    return pl.pallas_call(
        functools.partial(tables_kernel, n_patch),
        out_shape=[shape(table.shape, F32)] * 3,
        in_specs=[SMEM_SPEC] + [VMEM_SPEC] * 6,
        compiler_params=params(SCOPE),
        name="update_tables",
    )(bias_fix, edges, grad_time, grad_class, table, first, second)


def position_rows(first, rows):
    quarter = D // 4
    omega = jnp.exp(-math.log(10000.0) * jnp.arange(quarter, dtype=F32) / quarter)
    places = first + jnp.arange(rows, dtype=jnp.int32)
    rows_at = (places // GRID).astype(F32)[:, None] * omega[None]
    cols_at = (places % GRID).astype(F32)[:, None] * omega[None]
    return jnp.concatenate([jnp.sin(rows_at), jnp.cos(rows_at), jnp.sin(cols_at), jnp.cos(cols_at)], 1)


def time_features(timesteps):
    half_freq = FREQ // 2
    rates = jnp.exp(-math.log(10000.0) * jnp.arange(half_freq, dtype=F32) / half_freq)
    angles = timesteps.astype(F32)[:, None] * rates[None]
    return jnp.concatenate([jnp.cos(angles), jnp.sin(angles)], 1)


def shards(
    noisy_latents,
    noise_target,
    timesteps,
    labels,
    owners,
    step_count,
    master_bank,
    momentum_bank,
    embed_tables,
    embed_first,
    embed_second,
):
    n_lat, n_tok, n_patch = noisy_latents.shape
    n_slots, width, columns = master_bank.shape
    n_units = owners.shape[0]
    n_data = lax.axis_size("dp")
    my_data = lax.axis_index("dp")
    my_tensor = lax.axis_index("tensor")
    n_all = n_lat * n_data
    own_rows = n_lat * n_tok // 4
    count_all = float(n_all * n_tok * n_patch)
    depth = 2 if n_data <= 8 else 1
    steps = N_BIG + (n_data - 2) * depth

    unit_order = jnp.arange(n_units, dtype=jnp.int32)
    same_owner = owners[:, None] == owners[None, :]
    slot_of = jnp.sum((same_owner & (unit_order[None, :] < unit_order[:, None])).astype(jnp.int32), 1)
    mine = (owners[None, :] == my_data) & (
        slot_of[None, :] == jnp.arange(n_slots, dtype=jnp.int32)[:, None]
    )
    kind = [2 + 2 * g + (b >= low + (3, 4)[g % 2]) for g, (low, high) in enumerate(GROUPS) for b in range(low, high)]
    slot_tables = np.stack(
        [
            BIG_OF,
            SMALL_OF,
            np.where(BIG_OF >= 0, np.array(kind)[BIG_OF], np.where(SMALL_OF == TIME_AT, 1, 0)),
            np.where(BIG_OF >= 0, SMALL_ROWS + BIG_OF, SMALL_OF),
        ]
    )
    slots = jnp.sum(jnp.where(mine[None], jnp.asarray(slot_tables + 1, jnp.int32)[:, None], 0), 2) - 1
    owners_big = jnp.concatenate([owners[18 * l : 18 * l + BIG] for l in range(LAYERS)])
    tab = ring_schedule(owners_big, n_data, steps, depth, my_data)

    def flag(value):
        return jnp.asarray(value, jnp.int32).reshape(1)

    first_row = my_tensor * own_rows
    early = dict(
        slots=slots,
        chip=flag(my_tensor // 2),
        core=flag(my_tensor % 2),
        data=flag(my_data),
        place=flag(jnp.sum(jnp.where(jnp.arange(n_data) == my_data, np.argsort(ring_order(n_data)), 0))),
        bits=[flag((my_data // (1 << i)) % 2) for i in range((n_data - 1).bit_length())],
        time_mine=flag(owners[18 * LAYERS] == my_data),
        time_w2=lax.dynamic_index_in_dim(master_bank, slot_of[18 * LAYERS], 0, keepdims=False).astype(BF16),
        noisy=lax.dynamic_slice_in_dim(noisy_latents.reshape(n_lat * n_tok, n_patch), first_row, own_rows, 0),
        target=lax.dynamic_slice_in_dim(noise_target.reshape(n_lat * n_tok, n_patch), first_row, own_rows, 0),
        places=position_rows(first_row % n_tok, own_rows),
        ids=jnp.stack([timesteps, labels], 1),
        bias_fix=1.0 - jnp.power(0.5, step_count.astype(F32)),
        tab=tab,
        edge_cols=jnp.concatenate(
            [embed_tables[:n_patch], embed_tables[n_patch + FREQ + CLASSES :]], 0
        ).astype(BF16),
        time_w1=embed_tables[n_patch : n_patch + FREQ].astype(BF16),
        class_w=embed_tables[n_patch + FREQ : n_patch + FREQ + CLASSES].astype(BF16),
    )
    flat, tree = jax.tree.flatten(early)
    early = jax.tree.unflatten(tree, lax.optimization_barrier(tuple(flat)))
    chip, core, data, time_w2, noisy_own = (early[k] for k in ("chip", "core", "data", "time_w2", "noisy"))
    tab = early["tab"]
    big_slots, small_slots, left_slots, right_slots = (early["slots"][i] for i in range(4))
    spread = Spreader(tab, spread_init(early["slots"], master_bank), n_data, steps, depth)
    spread.step()
    ring = Reducer(tab, n_data, steps, depth)

    def conditioning():
        ids, edge_rows = yield from together(
            dp_sum(own_latents(early["ids"], 0, data, n_data), n_data),
            gather_columns(early["edge_cols"], chip, core),
        )
        features = time_features(ids[:, 0]).astype(BF16)
        time_one = jnp.dot(features, early["time_w1"], preferred_element_type=F32)
        time_act = yield from gather_columns(jax.nn.silu(time_one).astype(BF16), chip, core)
        second = jnp.dot(time_act, time_w2, preferred_element_type=F32)
        second = yield from dp_sum(jnp.where(is_at(early["time_mine"], 1, 2), second, 0.0), n_data)
        onehot = ids[:, 1:2] == jnp.arange(CLASSES, dtype=jnp.int32)[None]
        condition = second + jnp.dot(onehot.astype(BF16), early["class_w"], preferred_element_type=F32)
        cond_in = yield from gather_columns(jax.nn.silu(condition).astype(BF16), chip, core)
        (mods,) = spread.work(modulations(small_slots, cond_in, master_bank), ISSUED)
        ISSUED.clear()
        bit = n_data // 2
        while bit:
            half = mods.shape[1] // 2
            sides = mods[:, :half], mods[:, half:]
            side = early["bits"][bit.bit_length() - 1]
            mods = pick(*sides, side) + (yield flip(pick(*sides, side, True), "dp", bit, n_data))
            bit //= 2
        latents = mods[:, 0], mods[:, 1]
        across = yield x_flip(pick(*latents, chip, True))
        own = pick(*latents, chip)
        pair = [pick(own, across, chip), pick(across, own, chip)]
        beside = core_flip(jnp.concatenate(pair, 1))
        beside = [beside[:, x * columns : (x + 1) * columns] for x in range(2)]
        blocks = [pick(one, two, core) for x in range(2) for one, two in ((pair[x], beside[x]), (beside[x], pair[x]))]
        return edge_rows, features, time_one, time_act, onehot, condition, cond_in, jnp.concatenate(blocks, 1)

    def forward():
        cond = yield from conditioning()
        edge_rows, mods = cond[0], cond[-1]
        stream, inner, normed, inv = enter(
            noisy_own, edge_rows[:n_patch], early["places"], mods, (small_at(0, 0), small_at(0, 1))
        )
        kept = []
        for layer in range(LAYERS):
            inner = yield from gather_tokens(inner)
            spread.prepare(2 * layer)
            qkv, mixed, keep, send = spread.work(attention(inner, columns, BIG * layer, n_lat))
            parts = yield from scatter_tokens(keep, send)
            attended, stream, inner_mid, normed_mid, inv_mid = residual(
                parts, stream, mods, tuple(small_at(layer, i) for i in (2, 3, 4))
            )
            inner_mid = yield from gather_tokens(inner_mid)
            spread.prepare(2 * layer + 1)
            hidden, active, keep, send = spread.work(mlp(inner_mid, columns, BIG * layer + 4))
            parts = yield from scatter_tokens(keep, send)
            kept.append([inner, normed, inv, qkv, mixed, attended, inner_mid, normed_mid, inv_mid, hidden, active])
            if layer + 1 < LAYERS:
                branch, stream, inner, normed, inv = residual(
                    parts,
                    stream,
                    mods,
                    (small_at(layer, 5), small_at(layer + 1, 0), small_at(layer + 1, 1)),
                )
                kept[-1].append(branch)
        return cond, kept, parts, stream

    cond, kept, parts_last, stream_last = drive(forward(), spread.step)
    edge_rows, features, time_one, time_act, onehot, condition, cond_in, mods = cond
    ring.held = spread.held

    def backward():
        grad, d_branch, rows, edge_head = leave(
            parts_last,
            stream_last,
            mods,
            edge_rows[n_patch:],
            early["target"],
            (small_at(LAYERS - 1, 5), SHIFT_F, SCALE_F),
            count_all,
        )
        lefts, rights = {}, {}
        for layer in reversed(range(LAYERS)):
            inner, normed, inv, qkv, mixed, attended, inner_mid, normed_mid, inv_mid, hidden, active = kept[layer][:11]
            d_branch = yield from gather_tokens(d_branch)
            d_hidden, keep, send = ring.work(mlp_back(d_branch, hidden, BIG * layer + 4))
            work = scatter_tokens(keep, send)
            flying = next(work)
            lefts[2 * layer + 1], rights[2 * layer + 1] = ring.work(
                weight_grads(BIG * layer + 4, [(inner_mid, d_hidden), (d_branch, active)], n_lat), ISSUED
            )
            ring.ready = BIG * layer + 4
            parts = finish(work, order(flying, (lefts[2 * layer + 1],) + ring.sent))
            grad, d_attended, rows = back(
                parts,
                normed_mid,
                inv_mid,
                grad,
                attended,
                mods,
                rows,
                small_at(layer, 4),
                small_at(layer, 2),
                small_at(layer, 3),
                [ring.held],
            )
            d_attended = yield from gather_tokens(d_attended)
            d_qkv, keep, send = ring.work(attention_back(d_attended, qkv, BIG * layer, n_lat))
            work = scatter_tokens(keep, send)
            flying = next(work)
            lefts[2 * layer], rights[2 * layer] = ring.work(
                weight_grads(BIG * layer, [(inner, d_qkv), (d_attended, mixed[None])], n_lat), ISSUED
            )
            ring.ready = BIG * layer
            parts = finish(work, order(flying, (lefts[2 * layer],) + ring.sent))
            below = kept[layer - 1][11] if layer else normed
            grad, d_branch, rows = back(
                parts,
                normed,
                inv,
                grad,
                below,
                mods,
                rows,
                small_at(layer, 1),
                small_at(layer - 1, 5) if layer else None,
                small_at(layer, 0),
                [ring.held],
            )
        return (yield from cond_backward(rows, d_branch, edge_head, lefts, rights))

    def cond_backward(rows, d_stream, edge_head, lefts, rights):
        mine = core_columns_sum(rows, core)
        near, far = pick(*mine, chip), (yield x_flip(pick(*mine, chip, True)))
        own = [pick(near, far, chip).astype(BF16), pick(far, near, chip).astype(BF16)]
        if n_data == 8:
            latents = yield from ring.gather(jnp.concatenate(own, 0), early["place"])
            d_small = jnp.stack([v[l * SMALL_ROWS : (l + 1) * SMALL_ROWS] for v in latents for l in range(n_lat)], 1)
        else:
            d_small = yield from dp_sum(own_latents(jnp.stack(own, 1), 1, data, n_data), n_data)
        (d_cond,) = ring.work(cond_back(small_slots, d_small, master_bank), ISSUED)
        ISSUED.clear()
        d_cond = yield from own_columns_sum(d_cond, chip, core)
        if n_data == 8:
            parts = yield from ring.gather(jnp.concatenate(halves(d_cond), 0), early["place"])
            d_cond = sum(p[:n_all].astype(F32) + p[n_all:].astype(F32) for p in parts)
        else:
            d_cond = yield from dp_sum(d_cond, n_data)
        unused, silu_pull = jax.vjp(jax.nn.silu, condition)
        d_condition = silu_pull(d_cond)[0]
        d_second = d_condition.astype(BF16)
        grad_class = lax.dot_general(
            onehot.astype(F32), d_condition, (((0,), (0,)), ((), ())), precision=HIGHEST_PREC
        )
        d_time_act = lax.dot_general(d_second, time_w2, (((1,), (1,)), ((), ())), preferred_element_type=F32)
        d_time_act = jnp.where(is_at(early["time_mine"], 1, 2), d_time_act, 0.0)
        grad_patch = lax.dot_general(noisy_own, d_stream, (((0,), (0,)), ((), ())), preferred_element_type=F32)
        sums = yield from own_columns_sum(jnp.concatenate([d_time_act, grad_patch, edge_head], 0), chip, core)
        ring.drain()
        sums, (a_rows, b_rows) = yield from together(
            dp_sum(order(sums, ring.last()), n_data), factor_rows(lefts, rights, ring.last())
        )
        d_time_act, edges = sums[:n_all], sums[n_all:]
        unused, time_pull = jax.vjp(jax.nn.silu, time_one)
        d_time_one = time_pull(d_time_act)[0].astype(BF16)
        grad_time_one = lax.dot_general(
            features, d_time_one, (((0,), (0,)), ((), ())), preferred_element_type=F32
        )
        return d_small, d_second, grad_class, grad_time_one, edges, (a_rows, b_rows)

    def factor_rows(lefts, rights, after):
        a_rows = jnp.concatenate([lefts[g][:, :n_lat] for g in range(len(GROUPS))], 0).transpose(1, 0, 2)
        b_rows = jnp.concatenate([rights[g][:, :n_lat] for g in range(len(GROUPS))], 0).transpose(1, 0, 2)
        n_left = a_rows.shape[1]
        packed = jnp.concatenate(
            [a_rows[:, :, j * columns : (j + 1) * columns] for j in range(4)] + [b_rows], 1
        ).astype(BF16)
        packed = yield from dp_rows(order(packed, after), n_data)
        a_rows = jnp.concatenate([packed[:, j * n_left : (j + 1) * n_left] for j in range(4)], 2)
        return a_rows.transpose(1, 0, 2), packed[:, 4 * n_left :].transpose(1, 0, 2)

    d_small, d_second, grad_class, grad_time_one, edges, (a_rows, b_rows) = drive(backward(), ring.step)
    loss = edges[2 * n_patch, 0]
    a_all = jnp.concatenate([cond_in[None], time_act[None], a_rows], 0)
    small_rows = jnp.where(jnp.arange(SMALL_ROWS)[:, None, None] == TIME_AT, d_second[None], d_small)
    b_all = jnp.concatenate([small_rows, b_rows], 0)
    master_new, momentum_new = optimizer(
        big_slots, left_slots, right_slots, tab, a_all, b_all, master_bank, momentum_bank, ring.held, ring.last()
    )
    embed_new, first_new, second_new = update_tables(
        n_patch, early["bias_fix"], edges, grad_time_one, grad_class, embed_tables, embed_first, embed_second
    )
    return (loss, master_new, momentum_new, embed_new, first_new, second_new)


def solution(mesh):
    placed = (
        P("dp", None, None),
        P("dp", None, None),
        P("dp"),
        P("dp"),
        P(),
        P(),
        P("dp", None, "tensor"),
        P("dp", None, "tensor"),
        P(None, "tensor"),
        P(None, "tensor"),
        P(None, "tensor"),
    )
    return jax.shard_map(
        shards,
        mesh=mesh,
        in_specs=placed,
        out_specs=(
            P(),
            P("dp", None, "tensor"),
            P("dp", None, "tensor"),
            P(None, "tensor"),
            P(None, "tensor"),
            P(None, "tensor"),
        ),
        check_vma=False,
    )
```

profile of v0, /device:TPU:0, one launch (start us, length us, event | category | flops | bytes accessed | tf_op | source)
XLA Modules:
  0.0 687.5 jit_solution(7695481368602392442)
XLA Ops:
  20.7 7.5 %ring_schedule.1 = s32[36,128]{1,0:T(8,128)} custom-call(s32[2]{0:T(128)} %pad_add_fusion.1.place_ref, s32[2,8,128]{2,1,0:T(8,128)} %add_convert_fusion.8.own_ref, s32[2,8,128]{2,1,0:T(8,128)} %add_convert_fusion.9.next_ref), custom_call_target="tpu_custom_call" | custom-call | tf_op jit(solution)/shard_map/ring_schedule/pallas_call | solution.py:275
  28.8 2.6 collective-permute-start.2
  31.3 2.9 own_weights.1.refs_0_
  42.0 2.4 collective-permute-done
  55.8 4.0 collective-permute-done.9
  62.0 2.5 collective-permute-done.13
  71.3 3.8 collective-permute-done.17
  81.5 5.2 collective-permute-done.20
  93.4 2.5 collective-permute-done.27
  99.7 2.4 spread_step_modulations.1
  102.2 2.1 collective-permute-start.34
  113.8 5.1 collective-permute-done.33
  130.8 3.2 collective-permute-done.42
  140.3 4.0 collective-permute-done.43.refs_0_
  149.9 3.6 collective-permute-done.51.refs_1_
  156.6 2.6 collective-permute-done.49.refs_1_
  159.2 15.4 %spread_step_attention.2 = (bf16[36,1024,256]{2,1,0:T(8,128)(2,1)S(1)}, bf16[512,256]{1,0:T(8,128)(2,1)S(1)}, bf16[512,256]{1,0:T(8,128)(2,1)S(1)}, bf16[3,512,2...) custom-call(s32[36,4]{1,0:T(8,128)S(1)} %bitcast.242, ...), custom_call_target="tpu_custom_call", output_to_operand_aliasing={{0}: (3, {})} | custom-call | tf_op jit(solution)/shard_map/spread_step_attention/pallas_call | solution.py:354
  180.5 3.3 collective-permute-done.59.refs_0_
  198.2 3.1 collective-permute-done.67.refs_0_
  206.9 3.6 collective-permute-done.66.refs_1_
  213.5 2.6 collective-permute-done.72.refs_1_
  221.6 3.9 spread_step_mlp.2
  231.4 3.4 collective-permute-done.80.refs_0_
  240.7 4.5 collective-permute-done.83.refs_5_
  248.2 4.3 spread_step_attention.3
  252.5 2.4 collective-permute-done.89.refs_0_
  261.2 3.4 collective-permute-done.95.refs_0_
  272.7 2.8 collective-permute-done.100.refs_1_
  282.2 2.6 collective-permute-done.98.refs_1_
  287.8 2.6 collective-permute-done.104.refs_1_
  293.8 2.2 collective-permute-done.102.refs_1_
  299.8 4.3 spread_step_mlp.3
  306.8 7.8 %collective-permute-done.111.far_ref = bf16[128,1024]{1,0:T(8,128)(2,1)S(1)} collective-permute-done((bf16[128,1024]{1,0:T(8,128)(2,1)S(1)}, bf16[128,1024]{1,0:T(8,128)(2,1)S(1)}, u32[]{:S(2)}, u32[]{:S(2)}) %collective-permute-start.111) | collective-permute-done | bytes 262176 | tf_op jit(solution)/shard_map/ppermute | solution.py:135
  316.2 7.0 %collective-permute-done.113.refs_3_.refs_7_ = bf16[128,1024]{1,0:T(8,128)(2,1)S(1)} collective-permute-done((bf16[128,1024]{1,0:T(8,128)(2,1)S(1)}, bf16[128,1024]{1,0:T(8,128)(2,1)S(1)}, u32[]{:S(2)}, u32[]{:S(2)}) %collective-permute-start.113) | collective-permute-done | bytes 262176 | tf_op jit(solution)/shard_map/ppermute | solution.py:135
  324.7 4.5 layer__mlp_back.1
  331.8 4.5 layer__weight_grads.1
  336.3 3.3 collective-permute-done.116.refs_2_
  341.7 7.2 %collective-permute-done.118.refs_3_.refs_9_ = bf16[128,1024]{1,0:T(8,128)(2,1)S(1)} collective-permute-done((bf16[128,1024]{1,0:T(8,128)(2,1)S(1)}, bf16[128,1024]{1,0:T(8,128)(2,1)S(1)}, u32[]{:S(2)}, u32[]{:S(2)}) %collective-permute-start.118) | collective-permute-done | bytes 262176 | tf_op jit(solution)/shard_map/ppermute | solution.py:135
  351.1 6.9 reduce_step_attention_back.2
  362.1 2.9 reduce_step_weight_grads.3
  365.0 3.1 collective-permute-done.126.refs_0_
  373.0 3.5 collective-permute-done.123.refs_0_
  377.2 3.1 collective-permute-done.129.refs_5_.refs_9_
  382.2 4.6 reduce_step_mlp_back.1
  392.4 4.5 reduce_step_weight_grads.4
  402.8 3.5 collective-permute-done.139.refs_0_
  406.7 3.3 collective-permute-done.138.refs_5_.refs_9_
  412.0 6.9 %reduce_step_attention_back.3 = (bf16[36,1024,256]{2,1,0:T(8,128)(2,1)S(1)}, bf16[512,256]{1,0:T(8,128)(2,1)S(1)}, bf16[512,256]{1,0:T(8,128)(2,1)S(1)}, bf16[3,...) custom-call(s32[36,4]{1,0:T(8,128)S(1)} %bitcast.271, ...), custom_call_target="tpu_custom_call", output_to_operand_aliasing={{0}: (3, {})} | custom-call | tf_op jit(solution)/shard_map/reduce_step_attention_back/pallas_call | solution.py:354
  421.8 3.3 reduce_step_weight_grads.5
  425.1 2.7 collective-permute-done.146.refs_0_
  433.5 3.1 collective-permute-done.149
  443.8 2.7 collective-permute-done.150.refs_0_
  500.5 2.5 reduce_step_cond_back.1
  508.3 3.2 collective-permute-done.175
  518.3 3.5 collective-permute-done.178.refs_0_
  525.3 2.4 collective-permute-done.176.refs_0_
  570.7 3.6 collective-permute-done.195
  580.9 3.7 collective-permute-done.200.refs_0_
  608.6 2.2 collective-permute-done.206.refs_1_
  618.3 2.6 collective-permute-done.211
  621.6 6.9 collective-permute-done.212
  629.6 2.7 update_tables.1
  632.3 5.4 collective-permute-done.215
  638.1 49.2 %optimizer.1 = (f32[8,1024,256]{2,1,0:T(8,128)}, f32[8,1024,256]{2,1,0:T(8,128)}) custom-call(s32[8]{0:T(128)S(1)} %get-tuple-element.945.big_ref, s32[8]{0:T(128)S(1)} %get-tuple-element.944.left_ref, s32[8]{0:T(128)S(1)} %get-tuple-element.943.right_ref, s32[36,4]{1,0:T(8,128)S(1)} %bitcast.300, bf16[10,16,1024]{2,1,0:T(8,128)(2,1)S(1)} %pad_maximum_fusion.1.a_ref, ...), custom_call_target="tpu_custom_call" | custom-call | tf_op jit(solution)/shard_map/optimizer/pallas_call | solution.py:785
  (682 shorter events, 373.0 us)
Async XLA Ops:
  28.3 10.8 %collective-permute-start.1 = (bf16[32,256]{1,0:T(8,128)(2,1)S(1)}, bf16[32,256]{1,0:T(8,128)(2,1)S(1)}, u32[]{:S(2)}, u32[]{:S(2)}) collective-permute-start(bf16[32,256]{1,0:T(8,128)(2,1)S(1)} %pad_maximum_fusion.29), channel_id=1, source_target_pairs={{0,1},{1,0},{2,3},{3,2},{4,5},{5,4},{6,7},{7,6},{8,9},{9,8},{10,11... | collective-permute-start | bytes 49160 | tf_op jit(solution)/shard_map/ppermute | solution.py:135
  28.8 10.3 %collective-permute-start.2 = (bf16[32,256]{1,0:T(8,128)(2,1)S(1)}, bf16[32,256]{1,0:T(8,128)(2,1)S(1)}, u32[]{:S(2)}, u32[]{:S(2)}) collective-permute-start(bf16[32,256]{1,0:T(8,128)(2,1)S(1)} %pad_maximum_fusion.29), channel_id=1, source_target_pairs={{0,2},{1,3},{2,0},{3,1},{4,6},{5,7},{6,4},{7,5},{8,10},{9,11},{10,... | collective-permute-start | bytes 49160 | tf_op jit(solution)/shard_map/ppermute | solution.py:135
  40.0 11.1 %collective-permute-start.7 = (bf16[512,256]{1,0:T(8,128)(2,1)S(1)}, bf16[512,256]{1,0:T(8,128)(2,1)S(1)}, u32[]{:S(2)}, u32[]{:S(2)}) collective-permute-start(bf16[512,256]{1,0:T(8,128)(2,1)S(1)} %get-tuple-element.464), channel_id=1, source_target_pairs={{0,8},{8,16},{16,24},{24,28},{28,20},{20,12},{12,4},{4,0},{1,9},{9... | collective-permute-start | bytes 786440 | tf_op jit(solution)/shard_map/ppermute | solution.py:407
  41.3 9.7 %collective-permute-start.8 = (bf16[512,256]{1,0:T(8,128)(2,1)S(1)}, bf16[512,256]{1,0:T(8,128)(2,1)S(1)}, u32[]{:S(2)}, u32[]{:S(2)}) collective-permute-start(bf16[512,256]{1,0:T(8,128)(2,1)S(1)} %get-tuple-element.465), channel_id=1, source_target_pairs={{8,0},{16,8},{24,16},{28,24},{20,28},{12,20},{4,12},{0,4},{9,1},{1... | collective-permute-start | bytes 786440 | tf_op jit(solution)/shard_map/ppermute | solution.py:407
  48.9 10.9 %collective-permute-start.10 = (bf16[512,256]{1,0:T(8,128)(2,1)S(1)}, bf16[512,256]{1,0:T(8,128)(2,1)S(1)}, u32[]{:S(2)}, u32[]{:S(2)}) collective-permute-start(bf16[512,256]{1,0:T(8,128)(2,1)S(1)} %get-tuple-element.472), channel_id=1, source_target_pairs={{0,8},{8,16},{16,24},{24,28},{28,20},{20,12},{12,4},{4,0},{1,9},{9... | collective-permute-start | bytes 786440 | tf_op jit(solution)/shard_map/ppermute | solution.py:407
  50.1 9.8 %collective-permute-start.11 = (bf16[512,256]{1,0:T(8,128)(2,1)S(1)}, bf16[512,256]{1,0:T(8,128)(2,1)S(1)}, u32[]{:S(2)}, u32[]{:S(2)}) collective-permute-start(bf16[512,256]{1,0:T(8,128)(2,1)S(1)} %get-tuple-element.473), channel_id=1, source_target_pairs={{8,0},{16,8},{24,16},{28,24},{20,28},{12,20},{4,12},{0,4},{9,1},{1... | collective-permute-start | bytes 786440 | tf_op jit(solution)/shard_map/ppermute | solution.py:407
  53.8 11.7 %collective-permute-start.14 = (bf16[512,256]{1,0:T(8,128)(2,1)S(1)}, bf16[512,256]{1,0:T(8,128)(2,1)S(1)}, u32[]{:S(2)}, u32[]{:S(2)}) collective-permute-start(bf16[512,256]{1,0:T(8,128)(2,1)S(1)} %get-tuple-element.477), channel_id=1, source_target_pairs={{0,8},{8,16},{16,24},{24,28},{28,20},{20,12},{12,4},{4,0},{1,9},{9... | collective-permute-start | bytes 786440 | tf_op jit(solution)/shard_map/ppermute | solution.py:407
  55.1 10.3 %collective-permute-start.15 = (bf16[512,256]{1,0:T(8,128)(2,1)S(1)}, bf16[512,256]{1,0:T(8,128)(2,1)S(1)}, u32[]{:S(2)}, u32[]{:S(2)}) collective-permute-start(bf16[512,256]{1,0:T(8,128)(2,1)S(1)} %get-tuple-element.478), channel_id=1, source_target_pairs={{8,0},{16,8},{24,16},{28,24},{20,28},{12,20},{4,12},{0,4},{9,1},{1... | collective-permute-start | bytes 786440 | tf_op jit(solution)/shard_map/ppermute | solution.py:407
  69.2 11.5 %collective-permute-start.21 = (bf16[512,256]{1,0:T(8,128)(2,1)S(1)}, bf16[512,256]{1,0:T(8,128)(2,1)S(1)}, u32[]{:S(2)}, u32[]{:S(2)}) collective-permute-start(bf16[512,256]{1,0:T(8,128)(2,1)S(1)} %get-tuple-element.490), channel_id=1, source_target_pairs={{0,8},{8,16},{16,24},{24,28},{28,20},{20,12},{12,4},{4,0},{1,9},{9... | collective-permute-start | bytes 786440 | tf_op jit(solution)/shard_map/ppermute | solution.py:407
  70.1 11.4 %collective-permute-start.22 = (bf16[512,256]{1,0:T(8,128)(2,1)S(1)}, bf16[512,256]{1,0:T(8,128)(2,1)S(1)}, u32[]{:S(2)}, u32[]{:S(2)}) collective-permute-start(bf16[512,256]{1,0:T(8,128)(2,1)S(1)} %get-tuple-element.491), channel_id=1, source_target_pairs={{8,0},{16,8},{24,16},{28,24},{20,28},{12,20},{4,12},{0,4},{9,1},{1... | collective-permute-start | bytes 786440 | tf_op jit(solution)/shard_map/ppermute | solution.py:407
  76.8 14.6 %collective-permute-start.24 = (bf16[512,256]{1,0:T(8,128)(2,1)S(1)}, bf16[512,256]{1,0:T(8,128)(2,1)S(1)}, u32[]{:S(2)}, u32[]{:S(2)}) collective-permute-start(bf16[512,256]{1,0:T(8,128)(2,1)S(1)} %get-tuple-element.495), channel_id=1, source_target_pairs={{0,8},{8,16},{16,24},{24,28},{28,20},{20,12},{12,4},{4,0},{1,9},{9... | collective-permute-start | bytes 786440 | tf_op jit(solution)/shard_map/ppermute | solution.py:407
  77.4 14.0 %collective-permute-start.25 = (bf16[512,256]{1,0:T(8,128)(2,1)S(1)}, bf16[512,256]{1,0:T(8,128)(2,1)S(1)}, u32[]{:S(2)}, u32[]{:S(2)}) collective-permute-start(bf16[512,256]{1,0:T(8,128)(2,1)S(1)} %get-tuple-element.496), channel_id=1, source_target_pairs={{8,0},{16,8},{24,16},{28,24},{20,28},{12,20},{4,12},{0,4},{9,1},{1... | collective-permute-start | bytes 786440 | tf_op jit(solution)/shard_map/ppermute | solution.py:407
  106.8 12.2 %collective-permute-start.33 = (f32[16,8,256]{2,0,1:T(8,128)S(1)}, f32[16,8,256]{2,0,1:T(8,128)S(1)}, u32[]{:S(2)}, u32[]{:S(2)}) collective-permute-start(f32[16,8,256]{2,0,1:T(8,128)S(1)} %slice_select_fusion), channel_id=1, source_target_pairs={{0,16},{4,20},{8,24},{12,28},{16,0},{20,4},{24,8},{28,12},{1,17},{... | collective-permute-start | bytes 393224 | tf_op jit(solution)/shard_map/ppermute | solution.py:135
  108.5 15.4 %collective-permute-start.37 = (bf16[512,256]{1,0:T(8,128)(2,1)S(1)}, bf16[512,256]{1,0:T(8,128)(2,1)S(1)}, u32[]{:S(2)}, u32[]{:S(2)}) collective-permute-start(bf16[512,256]{1,0:T(8,128)(2,1)S(1)} %get-tuple-element.516), channel_id=1, source_target_pairs={{0,8},{8,16},{16,24},{24,28},{28,20},{20,12},{12,4},{4,0},{1,9},{9... | collective-permute-start | bytes 786440 | tf_op jit(solution)/shard_map/ppermute | solution.py:407
  109.5 14.5 %collective-permute-start.38 = (bf16[512,256]{1,0:T(8,128)(2,1)S(1)}, bf16[512,256]{1,0:T(8,128)(2,1)S(1)}, u32[]{:S(2)}, u32[]{:S(2)}) collective-permute-start(bf16[512,256]{1,0:T(8,128)(2,1)S(1)} %get-tuple-element.517), channel_id=1, source_target_pairs={{8,0},{16,8},{24,16},{28,24},{20,28},{12,20},{4,12},{0,4},{9,1},{1... | collective-permute-start | bytes 786440 | tf_op jit(solution)/shard_map/ppermute | solution.py:407
  125.1 9.9 %collective-permute-start.45 = (bf16[512,256]{1,0:T(8,128)(2,1)S(1)}, bf16[512,256]{1,0:T(8,128)(2,1)S(1)}, u32[]{:S(2)}, u32[]{:S(2)}) collective-permute-start(bf16[512,256]{1,0:T(8,128)(2,1)S(1)} %get-tuple-element.528), channel_id=1, source_target_pairs={{0,8},{8,16},{16,24},{24,28},{28,20},{20,12},{12,4},{4,0},{1,9},{9... | collective-permute-start | bytes 786440 | tf_op jit(solution)/shard_map/ppermute | solution.py:407
  137.7 9.7 %collective-permute-start.52 = (bf16[128,1024]{1,0:T(8,128)(2,1)S(1)}, bf16[128,1024]{1,0:T(8,128)(2,1)S(1)}, u32[]{:S(2)}, u32[]{:S(2)}) collective-permute-start(bf16[128,1024]{1,0:T(8,128)(2,1)S(1)} %get-tuple-element.539.refs_3_), channel_id=1, source_target_pairs={{0,1},{1,0},{2,3},{3,2},{4,5},{5,4},{6,7},{7,6},{8,9},{9,8},{10,11... | collective-permute-start | bytes 786440 | tf_op jit(solution)/shard_map/ppermute | solution.py:135
  137.7 10.0 %collective-permute-start.53 = (bf16[128,1024]{1,0:T(8,128)(2,1)S(1)}, bf16[128,1024]{1,0:T(8,128)(2,1)S(1)}, u32[]{:S(2)}, u32[]{:S(2)}) collective-permute-start(bf16[128,1024]{1,0:T(8,128)(2,1)S(1)} %get-tuple-element.539.refs_3_), channel_id=1, source_target_pairs={{0,2},{1,3},{2,0},{3,1},{4,6},{5,7},{6,4},{7,5},{8,10},{9,11},{10,... | collective-permute-start | bytes 786440 | tf_op jit(solution)/shard_map/ppermute | solution.py:135
  139.3 10.6 %collective-permute-start.50 = (bf16[512,256]{1,0:T(8,128)(2,1)S(1)}, bf16[512,256]{1,0:T(8,128)(2,1)S(1)}, u32[]{:S(2)}, u32[]{:S(2)}) collective-permute-start(bf16[512,256]{1,0:T(8,128)(2,1)S(1)} %get-tuple-element.545), channel_id=1, source_target_pairs={{0,8},{8,16},{16,24},{24,28},{28,20},{20,12},{12,4},{4,0},{1,9},{9... | collective-permute-start | bytes 786440 | tf_op jit(solution)/shard_map/ppermute | solution.py:407
  145.7 10.9 %collective-permute-start.48 = (bf16[512,256]{1,0:T(8,128)(2,1)S(1)}, bf16[512,256]{1,0:T(8,128)(2,1)S(1)}, u32[]{:S(2)}, u32[]{:S(2)}) collective-permute-start(bf16[512,256]{1,0:T(8,128)(2,1)S(1)} %get-tuple-element.543), channel_id=1, source_target_pairs={{0,8},{8,16},{16,24},{24,28},{28,20},{20,12},{12,4},{4,0},{1,9},{9... | collective-permute-start | bytes 786440 | tf_op jit(solution)/shard_map/ppermute | solution.py:407
  147.3 11.8 %collective-permute-start.49 = (bf16[512,256]{1,0:T(8,128)(2,1)S(1)}, bf16[512,256]{1,0:T(8,128)(2,1)S(1)}, u32[]{:S(2)}, u32[]{:S(2)}) collective-permute-start(bf16[512,256]{1,0:T(8,128)(2,1)S(1)} %get-tuple-element.544), channel_id=1, source_target_pairs={{8,0},{16,8},{24,16},{28,24},{20,28},{12,20},{4,12},{0,4},{9,1},{1... | collective-permute-start | bytes 786440 | tf_op jit(solution)/shard_map/ppermute | solution.py:407
  147.8 11.4 %collective-permute-start.54 = (bf16[128,1024]{1,0:T(8,128)(2,1)S(1)}, bf16[128,1024]{1,0:T(8,128)(2,1)S(1)}, u32[]{:S(2)}, u32[]{:S(2)}) collective-permute-start(bf16[128,1024]{1,0:T(8,128)(2,1)S(1)} %collective-permute-done.53.refs_5_), channel_id=1, source_target_pairs={{0,1},{1,0},{2,3},{3,2},{4,5},{5,4},{6,7},{7,6},{8,9},{9,8},{10,11... | collective-permute-start | bytes 786440 | tf_op jit(solution)/shard_map/ppermute | solution.py:135
  154.5 20.1 %collective-permute-start.55 = (bf16[512,256]{1,0:T(8,128)(2,1)S(1)}, bf16[512,256]{1,0:T(8,128)(2,1)S(1)}, u32[]{:S(2)}, u32[]{:S(2)}) collective-permute-start(bf16[512,256]{1,0:T(8,128)(2,1)S(1)} %get-tuple-element.555), channel_id=1, source_target_pairs={{0,8},{8,16},{16,24},{24,28},{28,20},{20,12},{12,4},{4,0},{1,9},{9... | collective-permute-start | bytes 786440 | tf_op jit(solution)/shard_map/ppermute | solution.py:407
  155.5 19.1 %collective-permute-start.56 = (bf16[512,256]{1,0:T(8,128)(2,1)S(1)}, bf16[512,256]{1,0:T(8,128)(2,1)S(1)}, u32[]{:S(2)}, u32[]{:S(2)}) collective-permute-start(bf16[512,256]{1,0:T(8,128)(2,1)S(1)} %get-tuple-element.556), channel_id=1, source_target_pairs={{8,0},{16,8},{24,16},{28,24},{20,28},{12,20},{4,12},{0,4},{9,1},{1... | collective-permute-start | bytes 786440 | tf_op jit(solution)/shard_map/ppermute | solution.py:407
  178.4 11.0 %collective-permute-start.63 = (bf16[512,256]{1,0:T(8,128)(2,1)S(1)}, bf16[512,256]{1,0:T(8,128)(2,1)S(1)}, u32[]{:S(2)}, u32[]{:S(2)}) collective-permute-start(bf16[512,256]{1,0:T(8,128)(2,1)S(1)} %get-tuple-element.561), channel_id=1, source_target_pairs={{0,8},{8,16},{16,24},{24,28},{28,20},{20,12},{12,4},{4,0},{1,9},{9... | collective-permute-start | bytes 786440 | tf_op jit(solution)/shard_map/ppermute | solution.py:407
  179.5 11.0 %collective-permute-start.64 = (bf16[512,256]{1,0:T(8,128)(2,1)S(1)}, bf16[512,256]{1,0:T(8,128)(2,1)S(1)}, u32[]{:S(2)}, u32[]{:S(2)}) collective-permute-start(bf16[512,256]{1,0:T(8,128)(2,1)S(1)} %get-tuple-element.562), channel_id=1, source_target_pairs={{8,0},{16,8},{24,16},{28,24},{20,28},{12,20},{4,12},{0,4},{9,1},{1... | collective-permute-start | bytes 786440 | tf_op jit(solution)/shard_map/ppermute | solution.py:407
  191.4 9.8 %collective-permute-start.67 = (bf16[512,256]{1,0:T(8,128)(2,1)S(1)}, bf16[512,256]{1,0:T(8,128)(2,1)S(1)}, u32[]{:S(2)}, u32[]{:S(2)}) collective-permute-start(bf16[512,256]{1,0:T(8,128)(2,1)S(1)} %get-tuple-element.576), channel_id=1, source_target_pairs={{0,8},{8,16},{16,24},{24,28},{28,20},{20,12},{12,4},{4,0},{1,9},{9... | collective-permute-start | bytes 786440 | tf_op jit(solution)/shard_map/ppermute | solution.py:407
  191.7 10.3 %collective-permute-start.68 = (bf16[512,256]{1,0:T(8,128)(2,1)S(1)}, bf16[512,256]{1,0:T(8,128)(2,1)S(1)}, u32[]{:S(2)}, u32[]{:S(2)}) collective-permute-start(bf16[512,256]{1,0:T(8,128)(2,1)S(1)} %get-tuple-element.577), channel_id=1, source_target_pairs={{8,0},{16,8},{24,16},{28,24},{20,28},{12,20},{4,12},{0,4},{9,1},{1... | collective-permute-start | bytes 786440 | tf_op jit(solution)/shard_map/ppermute | solution.py:407
  193.5 10.7 %collective-permute-start.73 = (bf16[128,1024]{1,0:T(8,128)(2,1)S(1)}, bf16[128,1024]{1,0:T(8,128)(2,1)S(1)}, u32[]{:S(2)}, u32[]{:S(2)}) collective-permute-start(bf16[128,1024]{1,0:T(8,128)(2,1)S(1)} %get-tuple-element.567.refs_3_), channel_id=1, source_target_pairs={{0,1},{1,0},{2,3},{3,2},{4,5},{5,4},{6,7},{7,6},{8,9},{9,8},{10,11... | collective-permute-start | bytes 786440 | tf_op jit(solution)/shard_map/ppermute | solution.py:135
  203.0 10.5 %collective-permute-start.71 = (bf16[512,256]{1,0:T(8,128)(2,1)S(1)}, bf16[512,256]{1,0:T(8,128)(2,1)S(1)}, u32[]{:S(2)}, u32[]{:S(2)}) collective-permute-start(bf16[512,256]{1,0:T(8,128)(2,1)S(1)} %get-tuple-element.582), channel_id=1, source_target_pairs={{0,8},{8,16},{16,24},{24,28},{28,20},{20,12},{12,4},{4,0},{1,9},{9... | collective-permute-start | bytes 786440 | tf_op jit(solution)/shard_map/ppermute | solution.py:407
  204.3 11.8 %collective-permute-start.72 = (bf16[512,256]{1,0:T(8,128)(2,1)S(1)}, bf16[512,256]{1,0:T(8,128)(2,1)S(1)}, u32[]{:S(2)}, u32[]{:S(2)}) collective-permute-start(bf16[512,256]{1,0:T(8,128)(2,1)S(1)} %get-tuple-element.583), channel_id=1, source_target_pairs={{8,0},{16,8},{24,16},{28,24},{20,28},{12,20},{4,12},{0,4},{9,1},{1... | collective-permute-start | bytes 786440 | tf_op jit(solution)/shard_map/ppermute | solution.py:407
  205.1 14.1 %collective-permute-start.75 = (bf16[128,1024]{1,0:T(8,128)(2,1)S(1)}, bf16[128,1024]{1,0:T(8,128)(2,1)S(1)}, u32[]{:S(2)}, u32[]{:S(2)}) collective-permute-start(bf16[128,1024]{1,0:T(8,128)(2,1)S(1)} %collective-permute-done.74.refs_5_), channel_id=1, source_target_pairs={{0,1},{1,0},{2,3},{3,2},{4,5},{5,4},{6,7},{7,6},{8,9},{9,8},{10,11... | collective-permute-start | bytes 786440 | tf_op jit(solution)/shard_map/ppermute | solution.py:135
  229.4 10.6 %collective-permute-start.84 = (bf16[512,256]{1,0:T(8,128)(2,1)S(1)}, bf16[512,256]{1,0:T(8,128)(2,1)S(1)}, u32[]{:S(2)}, u32[]{:S(2)}) collective-permute-start(bf16[512,256]{1,0:T(8,128)(2,1)S(1)} %get-tuple-element.598), channel_id=1, source_target_pairs={{0,8},{8,16},{16,24},{24,28},{28,20},{20,12},{12,4},{4,0},{1,9},{9... | collective-permute-start | bytes 786440 | tf_op jit(solution)/shard_map/ppermute | solution.py:407
  230.3 10.3 %collective-permute-start.85 = (bf16[512,256]{1,0:T(8,128)(2,1)S(1)}, bf16[512,256]{1,0:T(8,128)(2,1)S(1)}, u32[]{:S(2)}, u32[]{:S(2)}) collective-permute-start(bf16[512,256]{1,0:T(8,128)(2,1)S(1)} %get-tuple-element.599), channel_id=1, source_target_pairs={{8,0},{16,8},{24,16},{28,24},{20,28},{12,20},{4,12},{0,4},{9,1},{1... | collective-permute-start | bytes 786440 | tf_op jit(solution)/shard_map/ppermute | solution.py:407
  238.0 10.2 %collective-permute-start.86 = (bf16[512,256]{1,0:T(8,128)(2,1)S(1)}, bf16[512,256]{1,0:T(8,128)(2,1)S(1)}, u32[]{:S(2)}, u32[]{:S(2)}) collective-permute-start(bf16[512,256]{1,0:T(8,128)(2,1)S(1)} %get-tuple-element.607), channel_id=1, source_target_pairs={{0,8},{8,16},{16,24},{24,28},{28,20},{20,12},{12,4},{4,0},{1,9},{9... | collective-permute-start | bytes 786440 | tf_op jit(solution)/shard_map/ppermute | solution.py:407
  259.2 10.7 %collective-permute-start.92 = (bf16[512,256]{1,0:T(8,128)(2,1)S(1)}, bf16[512,256]{1,0:T(8,128)(2,1)S(1)}, u32[]{:S(2)}, u32[]{:S(2)}) collective-permute-start(bf16[512,256]{1,0:T(8,128)(2,1)S(1)} %get-tuple-element.623), channel_id=1, source_target_pairs={{0,8},{8,16},{16,24},{24,28},{28,20},{20,12},{12,4},{4,0},{1,9},{9... | collective-permute-start | bytes 786440 | tf_op jit(solution)/shard_map/ppermute | solution.py:407
  259.6 11.1 %collective-permute-start.93 = (bf16[512,256]{1,0:T(8,128)(2,1)S(1)}, bf16[512,256]{1,0:T(8,128)(2,1)S(1)}, u32[]{:S(2)}, u32[]{:S(2)}) collective-permute-start(bf16[512,256]{1,0:T(8,128)(2,1)S(1)} %get-tuple-element.624), channel_id=1, source_target_pairs={{8,0},{16,8},{24,16},{28,24},{20,28},{12,20},{4,12},{0,4},{9,1},{1... | collective-permute-start | bytes 786440 | tf_op jit(solution)/shard_map/ppermute | solution.py:407
  269.2 10.2 %collective-permute-start.107 = (bf16[128,1024]{1,0:T(8,128)(2,1)S(1)}, bf16[128,1024]{1,0:T(8,128)(2,1)S(1)}, u32[]{:S(2)}, u32[]{:S(2)}) collective-permute-start(bf16[128,1024]{1,0:T(8,128)(2,1)S(1)} %get-tuple-element.629.refs_5_.refs_1_), channel_id=1, source_target_pairs={{0,1},{1,0},{2,3},{3,2},{4,5},{5,4},{6,7},{7,6},{8,9},{9,8},{10,11... | collective-permute-start | bytes 786440 | tf_op jit(solution)/shard_map/ppermute | solution.py:135
  269.9 10.5 %collective-permute-start.108 = (bf16[128,1024]{1,0:T(8,128)(2,1)S(1)}, bf16[128,1024]{1,0:T(8,128)(2,1)S(1)}, u32[]{:S(2)}, u32[]{:S(2)}) collective-permute-start(bf16[128,1024]{1,0:T(8,128)(2,1)S(1)} %get-tuple-element.629.refs_5_.refs_1_), channel_id=1, source_target_pairs={{0,2},{1,3},{2,0},{3,1},{4,6},{5,7},{6,4},{7,5},{8,10},{9,11},{10,... | collective-permute-start | bytes 786440 | tf_op jit(solution)/shard_map/ppermute | solution.py:135
  271.6 10.6 %collective-permute-start.97 = (bf16[512,256]{1,0:T(8,128)(2,1)S(1)}, bf16[512,256]{1,0:T(8,128)(2,1)S(1)}, u32[]{:S(2)}, u32[]{:S(2)}) collective-permute-start(bf16[512,256]{1,0:T(8,128)(2,1)S(1)} %get-tuple-element.633), channel_id=1, source_target_pairs={{0,8},{8,16},{16,24},{24,28},{28,20},{20,12},{12,4},{4,0},{1,9},{9... | collective-permute-start | bytes 786440 | tf_op jit(solution)/shard_map/ppermute | solution.py:407
  279.5 10.9 %collective-permute-start.104 = (bf16[512,256]{1,0:T(8,128)(2,1)S(1)}, bf16[512,256]{1,0:T(8,128)(2,1)S(1)}, u32[]{:S(2)}, u32[]{:S(2)}) collective-permute-start(bf16[512,256]{1,0:T(8,128)(2,1)S(1)} %get-tuple-element.642), channel_id=1, source_target_pairs={{8,0},{16,8},{24,16},{28,24},{20,28},{12,20},{4,12},{0,4},{9,1},{1... | collective-permute-start | bytes 786440 | tf_op jit(solution)/shard_map/ppermute | solution.py:407
  280.3 13.1 %collective-permute-start.109 = (bf16[128,1024]{1,0:T(8,128)(2,1)S(1)}, bf16[128,1024]{1,0:T(8,128)(2,1)S(1)}, u32[]{:S(2)}, u32[]{:S(2)}) collective-permute-start(bf16[128,1024]{1,0:T(8,128)(2,1)S(1)} %collective-permute-done.108.refs_7_.refs_3_), channel_id=1, source_target_pairs={{0,1},{1,0},{2,3},{3,2},{4,5},{5,4},{6,7},{7,6},{8,9},{9,8},{10,11... | collective-permute-start | bytes 786440 | tf_op jit(solution)/shard_map/ppermute | solution.py:135
  441.8 10.8 %collective-permute-start.156 = (bf16[544,256]{1,0:T(8,128)(2,1)S(1)}, bf16[544,256]{1,0:T(8,128)(2,1)S(1)}, u32[]{:S(2)}, u32[]{:S(2)}) collective-permute-start(bf16[544,256]{1,0:T(8,128)(2,1)S(1)} %get-tuple-element.771), channel_id=1, source_target_pairs={{8,0},{16,8},{24,16},{28,24},{20,28},{12,20},{4,12},{0,4},{9,1},{1... | collective-permute-start | bytes 835592 | tf_op jit(solution)/shard_map/ppermute | solution.py:481
  442.7 11.6 %collective-permute-start.157 = (bf16[544,256]{1,0:T(8,128)(2,1)S(1)}, bf16[544,256]{1,0:T(8,128)(2,1)S(1)}, u32[]{:S(2)}, u32[]{:S(2)}) collective-permute-start(bf16[544,256]{1,0:T(8,128)(2,1)S(1)} %get-tuple-element.772), channel_id=1, source_target_pairs={{0,8},{8,16},{16,24},{24,28},{28,20},{20,12},{12,4},{4,0},{1,9},{9... | collective-permute-start | bytes 835592 | tf_op jit(solution)/shard_map/ppermute | solution.py:481
  450.1 9.8 %collective-permute-start.155 = (bf16[512,256]{1,0:T(8,128)(2,1)S(1)}, bf16[512,256]{1,0:T(8,128)(2,1)S(1)}, u32[]{:S(2)}, u32[]{:S(2)}) collective-permute-start(bf16[512,256]{1,0:T(8,128)(2,1)S(1)} %get-tuple-element.770), channel_id=1, source_target_pairs={{0,8},{8,16},{16,24},{24,28},{28,20},{20,12},{12,4},{4,0},{1,9},{9... | collective-permute-start | bytes 786440 | tf_op jit(solution)/shard_map/ppermute | solution.py:481
  456.0 9.9 %collective-permute-start.161 = (bf16[544,256]{1,0:T(8,128)(2,1)S(1)}, bf16[544,256]{1,0:T(8,128)(2,1)S(1)}, u32[]{:S(2)}, u32[]{:S(2)}) collective-permute-start(bf16[544,256]{1,0:T(8,128)(2,1)S(1)} %get-tuple-element.778), channel_id=1, source_target_pairs={{0,8},{8,16},{16,24},{24,28},{28,20},{20,12},{12,4},{4,0},{1,9},{9... | collective-permute-start | bytes 835592 | tf_op jit(solution)/shard_map/ppermute | solution.py:481
  460.8 9.6 %collective-permute-start.158 = (bf16[512,256]{1,0:T(8,128)(2,1)S(1)}, bf16[512,256]{1,0:T(8,128)(2,1)S(1)}, u32[]{:S(2)}, u32[]{:S(2)}) collective-permute-start(bf16[512,256]{1,0:T(8,128)(2,1)S(1)} %get-tuple-element.775), channel_id=1, source_target_pairs={{8,0},{16,8},{24,16},{28,24},{20,28},{12,20},{4,12},{0,4},{9,1},{1... | collective-permute-start | bytes 786440 | tf_op jit(solution)/shard_map/ppermute | solution.py:481
  461.7 9.8 %collective-permute-start.159 = (bf16[512,256]{1,0:T(8,128)(2,1)S(1)}, bf16[512,256]{1,0:T(8,128)(2,1)S(1)}, u32[]{:S(2)}, u32[]{:S(2)}) collective-permute-start(bf16[512,256]{1,0:T(8,128)(2,1)S(1)} %get-tuple-element.776), channel_id=1, source_target_pairs={{0,8},{8,16},{16,24},{24,28},{28,20},{20,12},{12,4},{4,0},{1,9},{9... | collective-permute-start | bytes 786440 | tf_op jit(solution)/shard_map/ppermute | solution.py:481
  466.8 9.6 %collective-permute-start.164 = (bf16[544,256]{1,0:T(8,128)(2,1)S(1)}, bf16[544,256]{1,0:T(8,128)(2,1)S(1)}, u32[]{:S(2)}, u32[]{:S(2)}) collective-permute-start(bf16[544,256]{1,0:T(8,128)(2,1)S(1)} %get-tuple-element.783), channel_id=1, source_target_pairs={{8,0},{16,8},{24,16},{28,24},{20,28},{12,20},{4,12},{0,4},{9,1},{1... | collective-permute-start | bytes 835592 | tf_op jit(solution)/shard_map/ppermute | solution.py:481
  467.6 9.9 %collective-permute-start.165 = (bf16[544,256]{1,0:T(8,128)(2,1)S(1)}, bf16[544,256]{1,0:T(8,128)(2,1)S(1)}, u32[]{:S(2)}, u32[]{:S(2)}) collective-permute-start(bf16[544,256]{1,0:T(8,128)(2,1)S(1)} %get-tuple-element.784), channel_id=1, source_target_pairs={{0,8},{8,16},{16,24},{24,28},{28,20},{20,12},{12,4},{4,0},{1,9},{9... | collective-permute-start | bytes 835592 | tf_op jit(solution)/shard_map/ppermute | solution.py:481
  473.3 9.8 %collective-permute-start.163 = (bf16[512,256]{1,0:T(8,128)(2,1)S(1)}, bf16[512,256]{1,0:T(8,128)(2,1)S(1)}, u32[]{:S(2)}, u32[]{:S(2)}) collective-permute-start(bf16[512,256]{1,0:T(8,128)(2,1)S(1)} %get-tuple-element.782), channel_id=1, source_target_pairs={{0,8},{8,16},{16,24},{24,28},{28,20},{20,12},{12,4},{4,0},{1,9},{9... | collective-permute-start | bytes 786440 | tf_op jit(solution)/shard_map/ppermute | solution.py:481
  478.5 18.0 %collective-permute-start.168 = (bf16[544,256]{1,0:T(8,128)(2,1)S(1)}, bf16[544,256]{1,0:T(8,128)(2,1)S(1)}, u32[]{:S(2)}, u32[]{:S(2)}) collective-permute-start(bf16[544,256]{1,0:T(8,128)(2,1)S(1)} %get-tuple-element.789), channel_id=1, source_target_pairs={{8,0},{16,8},{24,16},{28,24},{20,28},{12,20},{4,12},{0,4},{9,1},{1... | collective-permute-start | bytes 835592 | tf_op jit(solution)/shard_map/ppermute | solution.py:481
  479.7 16.7 %collective-permute-start.169 = (bf16[544,256]{1,0:T(8,128)(2,1)S(1)}, bf16[544,256]{1,0:T(8,128)(2,1)S(1)}, u32[]{:S(2)}, u32[]{:S(2)}) collective-permute-start(bf16[544,256]{1,0:T(8,128)(2,1)S(1)} %get-tuple-element.790), channel_id=1, source_target_pairs={{0,8},{8,16},{16,24},{24,28},{28,20},{20,12},{12,4},{4,0},{1,9},{9... | collective-permute-start | bytes 835592 | tf_op jit(solution)/shard_map/ppermute | solution.py:481
  484.1 15.9 %collective-permute-start.166 = (bf16[512,256]{1,0:T(8,128)(2,1)S(1)}, bf16[512,256]{1,0:T(8,128)(2,1)S(1)}, u32[]{:S(2)}, u32[]{:S(2)}) collective-permute-start(bf16[512,256]{1,0:T(8,128)(2,1)S(1)} %get-tuple-element.787), channel_id=1, source_target_pairs={{8,0},{16,8},{24,16},{28,24},{20,28},{12,20},{4,12},{0,4},{9,1},{1... | collective-permute-start | bytes 786440 | tf_op jit(solution)/shard_map/ppermute | solution.py:481
  485.3 14.6 %collective-permute-start.167 = (bf16[512,256]{1,0:T(8,128)(2,1)S(1)}, bf16[512,256]{1,0:T(8,128)(2,1)S(1)}, u32[]{:S(2)}, u32[]{:S(2)}) collective-permute-start(bf16[512,256]{1,0:T(8,128)(2,1)S(1)} %get-tuple-element.788), channel_id=1, source_target_pairs={{0,8},{8,16},{16,24},{24,28},{28,20},{20,12},{12,4},{4,0},{1,9},{9... | collective-permute-start | bytes 786440 | tf_op jit(solution)/shard_map/ppermute | solution.py:481
  516.2 11.5 %collective-permute-start.176 = (bf16[544,256]{1,0:T(8,128)(2,1)S(1)}, bf16[544,256]{1,0:T(8,128)(2,1)S(1)}, u32[]{:S(2)}, u32[]{:S(2)}) collective-permute-start(bf16[544,256]{1,0:T(8,128)(2,1)S(1)} %get-tuple-element.819), channel_id=1, source_target_pairs={{8,0},{16,8},{24,16},{28,24},{20,28},{12,20},{4,12},{0,4},{9,1},{1... | collective-permute-start | bytes 835592 | tf_op jit(solution)/shard_map/ppermute | solution.py:481
  517.6 10.5 %collective-permute-start.177 = (bf16[544,256]{1,0:T(8,128)(2,1)S(1)}, bf16[544,256]{1,0:T(8,128)(2,1)S(1)}, u32[]{:S(2)}, u32[]{:S(2)}) collective-permute-start(bf16[544,256]{1,0:T(8,128)(2,1)S(1)} %get-tuple-element.820), channel_id=1, source_target_pairs={{0,8},{8,16},{16,24},{24,28},{28,20},{20,12},{12,4},{4,0},{1,9},{9... | collective-permute-start | bytes 835592 | tf_op jit(solution)/shard_map/ppermute | solution.py:481
  523.2 10.1 %collective-permute-start.182 = (bf16[512,256]{1,0:T(8,128)(2,1)S(1)}, bf16[512,256]{1,0:T(8,128)(2,1)S(1)}, u32[]{:S(2)}, u32[]{:S(2)}) collective-permute-start(bf16[512,256]{1,0:T(8,128)(2,1)S(1)} %get-tuple-element.826), channel_id=1, source_target_pairs={{8,0},{16,8},{24,16},{28,24},{20,28},{12,20},{4,12},{0,4},{9,1},{1... | collective-permute-start | bytes 786440 | tf_op jit(solution)/shard_map/ppermute | solution.py:481
  529.2 10.1 %collective-permute-start.180 = (bf16[544,256]{1,0:T(8,128)(2,1)S(1)}, bf16[544,256]{1,0:T(8,128)(2,1)S(1)}, u32[]{:S(2)}, u32[]{:S(2)}) collective-permute-start(bf16[544,256]{1,0:T(8,128)(2,1)S(1)} %get-tuple-element.824), channel_id=1, source_target_pairs={{8,0},{16,8},{24,16},{28,24},{20,28},{12,20},{4,12},{0,4},{9,1},{1... | collective-permute-start | bytes 835592 | tf_op jit(solution)/shard_map/ppermute | solution.py:481
  535.1 9.8 %collective-permute-start.186 = (bf16[512,256]{1,0:T(8,128)(2,1)S(1)}, bf16[512,256]{1,0:T(8,128)(2,1)S(1)}, u32[]{:S(2)}, u32[]{:S(2)}) collective-permute-start(bf16[512,256]{1,0:T(8,128)(2,1)S(1)} %get-tuple-element.833), channel_id=1, source_target_pairs={{8,0},{16,8},{24,16},{28,24},{20,28},{12,20},{4,12},{0,4},{9,1},{1... | collective-permute-start | bytes 786440 | tf_op jit(solution)/shard_map/ppermute | solution.py:481
  553.4 9.7 %collective-permute-start.188 = (bf16[544,256]{1,0:T(8,128)(2,1)S(1)}, bf16[544,256]{1,0:T(8,128)(2,1)S(1)}, u32[]{:S(2)}, u32[]{:S(2)}) collective-permute-start(bf16[544,256]{1,0:T(8,128)(2,1)S(1)} %get-tuple-element.841), channel_id=1, source_target_pairs={{8,0},{16,8},{24,16},{28,24},{20,28},{12,20},{4,12},{0,4},{9,1},{1... | collective-permute-start | bytes 835592 | tf_op jit(solution)/shard_map/ppermute | solution.py:481
  578.8 11.4 %collective-permute-start.198 = (bf16[512,256]{1,0:T(8,128)(2,1)S(1)}, bf16[512,256]{1,0:T(8,128)(2,1)S(1)}, u32[]{:S(2)}, u32[]{:S(2)}) collective-permute-start(bf16[512,256]{1,0:T(8,128)(2,1)S(1)} %get-tuple-element.867), channel_id=1, source_target_pairs={{8,0},{16,8},{24,16},{28,24},{20,28},{12,20},{4,12},{0,4},{9,1},{1... | collective-permute-start | bytes 786440 | tf_op jit(solution)/shard_map/ppermute | solution.py:481
  579.9 11.5 %collective-permute-start.199 = (bf16[512,256]{1,0:T(8,128)(2,1)S(1)}, bf16[512,256]{1,0:T(8,128)(2,1)S(1)}, u32[]{:S(2)}, u32[]{:S(2)}) collective-permute-start(bf16[512,256]{1,0:T(8,128)(2,1)S(1)} %get-tuple-element.868), channel_id=1, source_target_pairs={{0,8},{8,16},{16,24},{24,28},{28,20},{20,12},{12,4},{4,0},{1,9},{9... | collective-permute-start | bytes 786440 | tf_op jit(solution)/shard_map/ppermute | solution.py:481
  617.2 11.9 %collective-permute-start.214 = (bf16[4,56,256]{2,0,1:T(4,128)(2,1)S(1)}, bf16[4,56,256]{2,0,1:T(4,128)(2,1)S(1)}, u32[]{:S(2)}, u32[]{:S(2)}) collective-permute-start(bf16[4,56,256]{2,0,1:T(4,128)(2,1)S(1)} %pad_maximum_fusion.21), channel_id=1, source_target_pairs={{0,8},{4,12},{8,0},{12,4},{16,24},{20,28},{24,16},{28,20},{1,9},{5... | collective-permute-start | bytes 344072 | tf_op jit(solution)/shard_map/ppermute | solution.py:135
  (188 other events, 1723.8 us)
where the time goes:
time: 697 us; the launch traced here: 687 us
  waiting for transfers between devices  270 us (39%)
  Pallas kernels  199 us (29%)
  starting transfers between devices  178 us (26%)
  between operations  17.5 us (3%)
  other arithmetic  13.5 us (2%)
    ppermute x144, waiting for transfers between devices, work(): lax.ppermute(sends[way], 'dp', self.perms[way])  165 us
    ppermute x144, starting transfers between devices, work(): lax.ppermute(sends[way], 'dp', self.perms[way])  148 us
    pallas_call x75, Pallas kernels, ring_step(): pl.pallas_call(kernel, out_shape=[pltpu.VMEM(held.shape, held.dtype)] + [...  131 us
    ppermute x72, waiting for transfers between devices, flip(): got = lax.ppermute(values, axis, [(i, i ^ bit) for i in range(size)])  105 us
    pallas_call x1, Pallas kernels, optimizer(): pl.pallas_call(functools.partial(newton_kernel, len(got)), grid_spec=pltp...  49.2 us
    ppermute x72, starting transfers between devices, flip(): got = lax.ppermute(values, axis, [(i, i ^ bit) for i in range(size)])  29.7 us
  transfers between devices with their start and end apart: 216, of which 142 were waited for; matrix products, arithmetic and copies ran while one was open for 1% of the time, Pallas kernels for 19%

commit v1 on v0

--- a/solution.py
+++ b/solution.py
@@ -231,59 +231,85 @@
     return [0, 2, 4, 6, 7, 5, 3, 1] if n_data == 8 else list(range(n_data))
 
 
-def sched_kernel(steps, depth, n_data, place_ref, own_ref, next_ref, out_ref):
+def plan_kernel(n_units, n_slots, steps, depth, n_data, me_ref, owner_ref, table_ref, tab_ref, slot_ref):
+    me = me_ref[0]
+    place_of = [int(v) for v in np.argsort(ring_order(n_data))]
+    my_place = sum(jnp.where(me == d, place_of[d], 0) for d in range(n_data))
+    owner = owner_ref[...]
+    across = jnp.broadcast_to(owner, (128, 128))
+    before = lax.broadcasted_iota(jnp.int32, (128, 128), 0) < lax.broadcasted_iota(jnp.int32, (128, 128), 1)
+    slot = jnp.sum(jnp.where((across == across.T) & before, 1.0, 0.0), 0, keepdims=True)
+    mine = owner == me.astype(F32)
+    lane8 = lax.broadcasted_iota(jnp.int32, (8, 128), 1)
+    row8 = lax.broadcasted_iota(jnp.int32, (8, 128), 0)
+    result = jnp.full((8, 128), -1, jnp.int32)
+    for s in range(n_slots):
+        held = mine & (slot == s)
+        value = jnp.sum(jnp.where(held, table_ref[...], 0), 1, keepdims=True) - 1
+        result = jnp.where((lane8 == s) & (row8 < 4), value, result)
+    lane1 = lax.broadcasted_iota(jnp.int32, (1, 128), 1)
+    time = lane1 == 18 * LAYERS
+    time_slot = jnp.sum(jnp.where(time, slot, 0.0), 1, keepdims=True).astype(jnp.int32)
+    time_mine = jnp.sum(jnp.where(time & mine, 1.0, 0.0), 1, keepdims=True).astype(jnp.int32)
+    result = jnp.where((row8 == 4) & (lane8 == 0), time_slot, result)
+    result = jnp.where((row8 == 4) & (lane8 == 1), time_mine, result)
+    peers = jnp.full((1, 128), -1, jnp.int32)
+    place = jnp.full((1, 128), -9, jnp.int32)
+    for d in range(n_data):
+        ahead = place_of[d] - my_place
+        peers = jnp.where(lane1 == jnp.where(ahead < 0, ahead + n_data, ahead), d, peers)
+        place = jnp.where(owner == float(d), place_of[d], place)
+    slot_ref[...] = jnp.where(row8 == 5, peers, result)
+
+    big = jnp.where(lane1 < BIG, place, pltpu.roll(place, 128 - 6, 1))
+    big = jnp.where(lane1 < N_BIG, big, -9)
+    back = jnp.where(big >= 0, n_data - 1 - big, -9)
     lane = lax.broadcasted_iota(jnp.int32, (n_data, 128), 1)
     row = lax.broadcasted_iota(jnp.int32, (n_data, 128), 0)
+    follow = jnp.where(row == n_data - 1, 0, row + 1)
+    own = [(row == at).astype(jnp.int32) for at in (big, back)]
+    open_to = [(follow != at).astype(jnp.int32) for at in (big, back)]
+    spots = [my_place, n_data - 1 - my_place]
     far = jnp.int32(999)
-    out_lane = lax.broadcasted_iota(jnp.int32, (1, 128), 1)
 
     def step(t, carry):
         line = jnp.full((1, 128), -1, jnp.int32)
         after = []
         for way in range(2):
             have, sent, *coming = carry[way]
-            place = place_ref[way]
-            before = jnp.where(place == 0, n_data - 1, place - 1)
-            open_now = have * (1 - sent) * (1 - next_ref[way])
+            here = spots[way]
+            prior = jnp.where(here == 0, n_data - 1, here - 1)
+            open_now = have * (1 - sent) * open_to[way]
             first = jnp.min(jnp.where(open_now > 0, lane, far), axis=1, keepdims=True)
             chosen = (lane == first).astype(jnp.int32)
             first = jnp.broadcast_to(first, (n_data, 128))
-            for k, who in enumerate((place, before)):
+            for k, who in enumerate((here, prior)):
                 index = jnp.min(jnp.where(row == who, first, far), axis=0, keepdims=True)
                 index = jnp.where(index == far, -1, index)
-                line = jnp.where(out_lane == 2 * way + k, index, line)
+                line = jnp.where(lane1 == 2 * way + k, index, line)
             coming = list(coming) + [pltpu.roll(chosen, 1, 0)]
             after.append((have + coming[0], sent + chosen, *coming[1:]))
-        out_ref[pl.ds(t, 1), :] = line
+        tab_ref[pl.ds(t, 1), :] = line
         return tuple(after)
 
     none = jnp.zeros((n_data, 128), jnp.int32)
-    lax.fori_loop(0, steps, step, tuple((own_ref[way], none) + (none,) * (depth - 1) for way in range(2)))
-
-
-def ring_schedule(owners_big, n_data, steps, depth, my_data):
-    order = np.array(ring_order(n_data))
-    place_of = np.argsort(order)
-    place = jnp.sum(jnp.where(jnp.arange(n_data) == my_data, place_of, 0)).astype(jnp.int32)
-    at = jnp.arange(n_data)[:, None]
-    owner_place = jnp.sum(jnp.where(owners_big[:, None] == jnp.arange(n_data)[None], place_of[None], 0), 1)
-    owner_place = jnp.concatenate([owner_place, jnp.full((128 - N_BIG,), -9, owner_place.dtype)])[None]
-    back_place = jnp.where(owner_place >= 0, n_data - 1 - owner_place, -9)
-    own = jnp.stack([at == owner_place, at == back_place]).astype(jnp.int32)
-    follow = (at + 1) % n_data
-    nxt = jnp.stack([follow == owner_place, follow == back_place]).astype(jnp.int32)
-    out = pl.pallas_call(
-        functools.partial(sched_kernel, steps, depth, n_data),
-        out_shape=shape((steps, 128), jnp.int32),
-        in_specs=[
-            pl.BlockSpec(memory_space=pltpu.SMEM),
-            pl.BlockSpec(memory_space=pltpu.VMEM),
-            pl.BlockSpec(memory_space=pltpu.VMEM),
-        ],
-        out_specs=pl.BlockSpec(memory_space=pltpu.VMEM),
-        name="ring_schedule",
-    )(jnp.stack([place, n_data - 1 - place]), own, nxt)
-    return out[:, :4]
+    lax.fori_loop(0, steps, step, tuple((own[way], none) + (none,) * (depth - 1) for way in range(2)))
+
+
+def plan(owners, tables, n_slots, n_data, steps, depth, my_data):
+    n_units = owners.shape[0]
+    padded = jnp.pad(owners.astype(F32), (0, 128 - n_units), constant_values=-1.0)[None]
+    wide = np.zeros((8, 128), np.int32)
+    wide[: len(tables), :n_units] = tables + 1
+    tab, rows = pl.pallas_call(
+        functools.partial(plan_kernel, n_units, n_slots, steps, depth, n_data),
+        out_shape=[shape((steps, 128), jnp.int32), shape((8, 128), jnp.int32)],
+        in_specs=[SMEM_SPEC, VMEM_SPEC, VMEM_SPEC],
+        out_specs=[VMEM_SPEC, VMEM_SPEC],
+        compiler_params=params(SCOPE),
+        name="plan",
+    )(my_data.reshape(1), padded, jnp.asarray(wide))
+    return tab[:, :4], rows
 
 
 def spread_init_kernel(slots_ref, bank_ref, out_ref, wide, sem):
@@ -483,25 +509,20 @@
         self.sent = tuple(sends) + tuple(self.got.get(k - 1, ()))
         return order(results, tuple(self.got.get(k - 1, ())))
 
-    def gather(self, payload, place):
+    def gather(self, *payloads):
         far = self.n_data // 2
-        start, last = self.at, self.at + (far - 1) * self.depth
-        assert last + self.depth < self.steps
-        for j in range(far):
-            self.mail[start + j * self.depth] = (payload, j)
-        while self.at <= last + self.depth:
+        starts = [self.at + i for i in range(len(payloads))]
+        for start, payload in zip(starts, payloads):
+            for j in range(far):
+                self.mail[start + j * self.depth] = (payload, j)
+        last = starts[-1] + far * self.depth
+        assert len(payloads) <= self.depth and last < self.steps
+        while self.at <= last:
             yield ()
-        come = [[self.come[start + j * self.depth][way] for j in range(far)] for way in range(2)]
-        come = order(come, self.sent)
-        at = [payload] + come[0][: far - 1] + come[1][::-1]
         everyone = []
-        for d in range(self.n_data):
-            ahead = ring_order(self.n_data).index(d) - place.reshape((1, 1))
-            ahead = jnp.where(ahead < 0, ahead + self.n_data, ahead)
-            value = at[0]
-            for i in range(1, self.n_data):
-                value = jnp.where(ahead == i, at[i], value)
-            everyone.append(value)
+        for start, payload in zip(starts, payloads):
+            come = [[self.come[start + j * self.depth][way] for j in range(far)] for way in range(2)]
+            everyone.append(order([payload] + come[0][: far - 1] + come[1][::-1], self.sent))
         return everyone
 
     def drain(self):
@@ -701,18 +722,49 @@
     return "_modulations", modulation_kernel, operands, shapes, bank_scratch(bank)
 
 
-def cond_back_kernel(held_ref, small_ref, d_ref, bank_ref, out_ref, wide, sem):
+def cond_back_kernel(n_mail, held_ref, small_ref, peer_ref, *refs):
+    mail, (bank_ref, d_ref, out_ref, wide, sem) = refs[:n_mail], refs[n_mail:]
+    if n_mail == 1:
+        d_ref[...] = mail[0][...]
+    else:
+        n_lat = d_ref.shape[0] // n_mail
+        for i in range(n_mail):
+            for l in range(n_lat):
+                d_ref[peer_ref[i] * n_lat + l] = mail[i][l * SMALL_ROWS : (l + 1) * SMALL_ROWS]
     out_ref[...] = jnp.zeros_like(out_ref)
 
     def use(unit, weight):
-        out_ref[...] += dot_nt(d_ref[unit], weight)
+        d = d_ref[...].astype(F32)
+        d = jnp.sum(jnp.where(lax.broadcasted_iota(jnp.int32, d.shape, 1) == unit, d, 0.0), 1)
+        out_ref[...] += dot_nt(d.astype(BF16), weight)
 
     small_weights(small_ref, bank_ref, wide, sem, use)
 
 
-def cond_back(small_slots, d_small, bank):
-    operands = [(small_slots, SMEM_SPEC), d_small, (in_hbm(bank), pl.BlockSpec(memory_space=pltpu.HBM))]
-    return "_cond_back", cond_back_kernel, operands, [shape((d_small.shape[1], bank.shape[1]), F32)], bank_scratch(bank)
+def cond_back(small_slots, peers, mail, n_all, bank):
+    columns = bank.shape[2]
+    operands = [(small_slots, SMEM_SPEC), (peers, SMEM_SPEC)] + list(mail)
+    operands += [(in_hbm(bank), pl.BlockSpec(memory_space=pltpu.HBM))]
+    shapes = [shape((n_all, SMALL_ROWS, columns), BF16), shape((n_all, bank.shape[1]), F32)]
+    return "_cond_back", functools.partial(cond_back_kernel, len(mail)), operands, shapes, bank_scratch(bank)
+
+
+def mail_sum_kernel(n_mail, held_ref, peer_ref, *refs):
+    mail, (out_ref, whole) = refs[:n_mail], refs[n_mail:]
+    rows = out_ref.shape[0]
+    for i in range(n_mail):
+        whole[peer_ref[i]] = mail[i][:rows].astype(F32) + mail[i][rows:].astype(F32)
+    total = whole[0]
+    for i in range(1, n_mail):
+        total = total + whole[i]
+    out_ref[...] = total
+
+
+def mail_sum(peers, mail):
+    rows, columns = mail[0].shape[0] // 2, mail[0].shape[1]
+    scratch = [pltpu.VMEM((len(mail), rows, columns), F32)]
+    operands = [(peers, SMEM_SPEC)] + list(mail)
+    return "_mail_sum", functools.partial(mail_sum_kernel, len(mail)), operands, [shape((rows, columns), F32)], scratch
 
 
 def halves(x):
@@ -1026,7 +1078,6 @@
 ):
     n_lat, n_tok, n_patch = noisy_latents.shape
     n_slots, width, columns = master_bank.shape
-    n_units = owners.shape[0]
     n_data = lax.axis_size("dp")
     my_data = lax.axis_index("dp")
     my_tensor = lax.axis_index("tensor")
@@ -1036,12 +1087,6 @@
     depth = 2 if n_data <= 8 else 1
     steps = N_BIG + (n_data - 2) * depth
 
-    unit_order = jnp.arange(n_units, dtype=jnp.int32)
-    same_owner = owners[:, None] == owners[None, :]
-    slot_of = jnp.sum((same_owner & (unit_order[None, :] < unit_order[:, None])).astype(jnp.int32), 1)
-    mine = (owners[None, :] == my_data) & (
-        slot_of[None, :] == jnp.arange(n_slots, dtype=jnp.int32)[:, None]
-    )
     kind = [2 + 2 * g + (b >= low + (3, 4)[g % 2]) for g, (low, high) in enumerate(GROUPS) for b in range(low, high)]
     slot_tables = np.stack(
         [
@@ -1051,23 +1096,21 @@
             np.where(BIG_OF >= 0, SMALL_ROWS + BIG_OF, SMALL_OF),
         ]
     )
-    slots = jnp.sum(jnp.where(mine[None], jnp.asarray(slot_tables + 1, jnp.int32)[:, None], 0), 2) - 1
-    owners_big = jnp.concatenate([owners[18 * l : 18 * l + BIG] for l in range(LAYERS)])
-    tab = ring_schedule(owners_big, n_data, steps, depth, my_data)
+    tab, planned = plan(owners, slot_tables, n_slots, n_data, steps, depth, my_data)
 
     def flag(value):
         return jnp.asarray(value, jnp.int32).reshape(1)
 
     first_row = my_tensor * own_rows
     early = dict(
-        slots=slots,
+        slots=planned[:4, :n_slots],
+        peers=planned[5, :n_data],
         chip=flag(my_tensor // 2),
         core=flag(my_tensor % 2),
         data=flag(my_data),
-        place=flag(jnp.sum(jnp.where(jnp.arange(n_data) == my_data, np.argsort(ring_order(n_data)), 0))),
         bits=[flag((my_data // (1 << i)) % 2) for i in range((n_data - 1).bit_length())],
-        time_mine=flag(owners[18 * LAYERS] == my_data),
-        time_w2=lax.dynamic_index_in_dim(master_bank, slot_of[18 * LAYERS], 0, keepdims=False).astype(BF16),
+        time_mine=planned[4, 1:2],
+        time_w2=lax.dynamic_index_in_dim(master_bank, planned[4, 0], 0, keepdims=False).astype(BF16),
         noisy=lax.dynamic_slice_in_dim(noisy_latents.reshape(n_lat * n_tok, n_patch), first_row, own_rows, 0),
         target=lax.dynamic_slice_in_dim(noise_target.reshape(n_lat * n_tok, n_patch), first_row, own_rows, 0),
         places=position_rows(first_row % n_tok, own_rows),
@@ -1083,7 +1126,7 @@
     flat, tree = jax.tree.flatten(early)
     early = jax.tree.unflatten(tree, lax.optimization_barrier(tuple(flat)))
     chip, core, data, time_w2, noisy_own = (early[k] for k in ("chip", "core", "data", "time_w2", "noisy"))
-    tab = early["tab"]
+    tab, peers = early["tab"], early["peers"]
     big_slots, small_slots, left_slots, right_slots = (early["slots"][i] for i in range(4))
     spread = Spreader(tab, spread_init(early["slots"], master_bank), n_data, steps, depth)
     spread.step()
@@ -1219,16 +1262,21 @@
         near, far = pick(*mine, chip), (yield x_flip(pick(*mine, chip, True)))
         own = [pick(near, far, chip).astype(BF16), pick(far, near, chip).astype(BF16)]
         if n_data == 8:
-            latents = yield from ring.gather(jnp.concatenate(own, 0), early["place"])
-            d_small = jnp.stack([v[l * SMALL_ROWS : (l + 1) * SMALL_ROWS] for v in latents for l in range(n_lat)], 1)
+            first, *others = factor_rows(lefts, rights)
+            one, two = jnp.concatenate(own + [first], 0), jnp.concatenate(others, 0)
+            one, two = (jnp.pad(v, ((0, -len(v) % 96), (0, 0))) for v in (one, two))
+            latents, others = yield from ring.gather(one, two)
+            n_own, n_rows = n_lat * SMALL_ROWS, first.shape[0]
+            factors = [v[n_own : n_own + n_rows] for v in latents] + [v[:n_rows] for v in others]
+            factors = jnp.concatenate(factors, 0).reshape(n_all, n_rows, columns)
         else:
-            d_small = yield from dp_sum(own_latents(jnp.stack(own, 1), 1, data, n_data), n_data)
-        (d_cond,) = ring.work(cond_back(small_slots, d_small, master_bank), ISSUED)
+            latents = [(yield from dp_sum(own_latents(jnp.stack(own, 0), 0, data, n_data), n_data))]
+        d_small, d_cond = ring.work(cond_back(small_slots, peers, latents, n_all, master_bank), ISSUED)
         ISSUED.clear()
         d_cond = yield from own_columns_sum(d_cond, chip, core)
         if n_data == 8:
-            parts = yield from ring.gather(jnp.concatenate(halves(d_cond), 0), early["place"])
-            d_cond = sum(p[:n_all].astype(F32) + p[n_all:].astype(F32) for p in parts)
+            (parts,) = yield from ring.gather(jnp.concatenate(halves(d_cond), 0))
+            (d_cond,) = ring.work(mail_sum(peers, parts))
         else:
             d_cond = yield from dp_sum(d_cond, n_data)
         unused, silu_pull = jax.vjp(jax.nn.silu, condition)
@@ -1242,9 +1290,12 @@
         grad_patch = lax.dot_general(noisy_own, d_stream, (((0,), (0,)), ((), ())), preferred_element_type=F32)
         sums = yield from own_columns_sum(jnp.concatenate([d_time_act, grad_patch, edge_head], 0), chip, core)
         ring.drain()
-        sums, (a_rows, b_rows) = yield from together(
-            dp_sum(order(sums, ring.last()), n_data), factor_rows(lefts, rights, ring.last())
-        )
+        sums = yield from dp_sum(order(sums, ring.last()), n_data)
+        if n_data != 8:
+            factors = yield from dp_rows(jnp.stack(factor_rows(lefts, rights)), n_data)
+        n_left = sum(v.shape[0] for v in lefts.values())
+        a_rows = jnp.concatenate([factors[:, j * n_left : (j + 1) * n_left] for j in range(4)], 2).transpose(1, 0, 2)
+        b_rows = factors[:, 4 * n_left : 4 * n_left + N_BIG].transpose(1, 0, 2)
         d_time_act, edges = sums[:n_all], sums[n_all:]
         unused, time_pull = jax.vjp(jax.nn.silu, time_one)
         d_time_one = time_pull(d_time_act)[0].astype(BF16)
@@ -1253,21 +1304,20 @@
         )
         return d_small, d_second, grad_class, grad_time_one, edges, (a_rows, b_rows)
 
-    def factor_rows(lefts, rights, after):
-        a_rows = jnp.concatenate([lefts[g][:, :n_lat] for g in range(len(GROUPS))], 0).transpose(1, 0, 2)
-        b_rows = jnp.concatenate([rights[g][:, :n_lat] for g in range(len(GROUPS))], 0).transpose(1, 0, 2)
-        n_left = a_rows.shape[1]
-        packed = jnp.concatenate(
-            [a_rows[:, :, j * columns : (j + 1) * columns] for j in range(4)] + [b_rows], 1
-        ).astype(BF16)
-        packed = yield from dp_rows(order(packed, after), n_data)
-        a_rows = jnp.concatenate([packed[:, j * n_left : (j + 1) * n_left] for j in range(4)], 2)
-        return a_rows.transpose(1, 0, 2), packed[:, 4 * n_left :].transpose(1, 0, 2)
+    def factor_rows(lefts, rights):
+        a_rows = jnp.concatenate([lefts[g] for g in range(len(GROUPS))], 0)
+        b_rows = jnp.concatenate([rights[g] for g in range(len(GROUPS))], 0)
+        parts = []
+        for l in range(n_lat):
+            part = [a_rows[:, l, j * columns : (j + 1) * columns] for j in range(4)] + [b_rows[:, l]]
+            part = jnp.concatenate(part, 0).astype(BF16)
+            parts.append(jnp.pad(part, ((0, -len(part) % 32), (0, 0))))
+        return parts
 
     d_small, d_second, grad_class, grad_time_one, edges, (a_rows, b_rows) = drive(backward(), ring.step)
     loss = edges[2 * n_patch, 0]
     a_all = jnp.concatenate([cond_in[None], time_act[None], a_rows], 0)
-    small_rows = jnp.where(jnp.arange(SMALL_ROWS)[:, None, None] == TIME_AT, d_second[None], d_small)
+    small_rows = jnp.where(jnp.arange(SMALL_ROWS)[:, None, None] == TIME_AT, d_second[None], d_small.transpose(1, 0, 2))
     b_all = jnp.concatenate([small_rows, b_rows], 0)
     master_new, momentum_new = optimizer(
         big_slots, left_slots, right_slots, tab, a_all, b_all, master_bank, momentum_bank, ring.held, ring.last()

time: 697 us -> 678 us (0.973)
  between operations: 17.5 us -> 6.25 us
  Pallas kernels: 199 us -> 210 us
  other arithmetic: 13.5 us -> 5.88 us
    ppermute x144, waiting for transfers between devices: 165 us -> 178 us  [work(): lax.ppermute(sends[way], 'dp', self.perms[way])]
    ppermute x72 -> x69, waiting for transfers between devices: 105 us -> 93.4 us  [flip(): got = lax.ppermute(values, axis, [(i, i ^ bit) for i in range(size)])]
    pallas_call x1, Pallas kernels: 49.2 us -> 60.2 us  [optimizer(): pl.pallas_call(functools.partial(newton_kernel, len(got)), grid_spec=pltp...]
    ppermute x72 -> x69, starting transfers between devices: 29.7 us -> 25.9 us  [flip(): got = lax.ppermute(values, axis, [(i, i ^ bit) for i in range(size)])]
  transfers between devices with their start and end apart: 216 -> 213, of which waited for: 142 -> 139; matrix products, arithmetic and copies ran while one was open for 1% -> 1% of each run, Pallas kernels for 19% -> 28%
where the time goes in v1:
time: 678 us; the launch traced here: 675 us
  waiting for transfers between devices  272 us (40%)
  Pallas kernels  210 us (31%)
  starting transfers between devices  172 us (25%)
    ppermute x144, waiting for transfers between devices, work(): lax.ppermute(sends[way], 'dp', self.perms[way])  178 us
    ppermute x144, starting transfers between devices, work(): lax.ppermute(sends[way], 'dp', self.perms[way])  146 us
    pallas_call x75, Pallas kernels, ring_step(): pl.pallas_call(kernel, out_shape=[pltpu.VMEM(held.shape, held.dtype)] + [...  133 us
    ppermute x69, waiting for transfers between devices, flip(): got = lax.ppermute(values, axis, [(i, i ^ bit) for i in range(size)])  93.4 us
    pallas_call x1, Pallas kernels, optimizer(): pl.pallas_call(functools.partial(newton_kernel, len(got)), grid_spec=pltp...  60.2 us
    ppermute x69, starting transfers between devices, flip(): got = lax.ppermute(values, axis, [(i, i ^ bit) for i in range(size)])  25.9 us
  transfers between devices with their start and end apart: 213, of which 139 were waited for; matrix products, arithmetic and copies ran while one was open for 1% of the time, Pallas kernels for 28%

profile of v1, /device:TPU:0, one launch (start us, length us, event | category | flops | bytes accessed | tf_op | source)
XLA Modules:
  0.0 675.1 jit_solution(3966170997401908978)
XLA Ops:
  2.1 6.4 plan.1
  18.0 3.0 collective-permute-start.2
  21.0 3.2 own_weights.1.refs_0_
  31.7 2.6 collective-permute-done
  40.7 2.3 collective-permute-start.9
  46.0 3.8 collective-permute-done.9
  51.3 3.1 collective-permute-done.13
  61.6 4.1 collective-permute-done.17
  72.1 5.2 collective-permute-done.20
  83.4 3.1 collective-permute-done.27
  90.4 3.1 spread_step_modulations.1
  104.4 5.0 collective-permute-done.33
  117.6 2.5 collective-permute-done.39
  121.7 3.2 collective-permute-done.42
  131.0 4.2 collective-permute-done.43.refs_0_
  140.8 3.6 collective-permute-done.51.refs_1_
  147.5 2.6 collective-permute-done.49.refs_1_
  150.1 15.4 %spread_step_attention.2 = (bf16[36,1024,256]{2,1,0:T(8,128)(2,1)S(1)}, bf16[512,256]{1,0:T(8,128)(2,1)S(1)}, bf16[512,256]{1,0:T(8,128)(2,1)S(1)}, bf16[3,512,2...) custom-call(s32[36,4]{1,0:T(8,128)S(1)} %bitcast.145, ...), custom_call_target="tpu_custom_call", output_to_operand_aliasing={{0}: (3, {})} | custom-call | tf_op jit(solution)/shard_map/spread_step_attention/pallas_call | solution.py:380
  171.4 3.4 collective-permute-done.59.refs_0_
  188.5 3.1 collective-permute-done.67.refs_0_
  194.8 2.8 collective-permute-done.65.refs_0_
  197.5 3.3 collective-permute-done.66.refs_1_
  203.9 2.6 collective-permute-done.72.refs_1_
  212.1 3.9 spread_step_mlp.2
  221.9 3.4 collective-permute-done.80.refs_0_
  231.2 3.0 collective-permute-done.83.refs_5_
  238.4 4.3 spread_step_attention.3
  250.1 3.4 collective-permute-done.95.refs_0_
  260.9 4.5 collective-permute-done.99.refs_0_
  271.0 3.6 collective-permute-done.98.refs_1_
  277.6 2.6 collective-permute-done.104.refs_1_
  288.6 4.3 spread_step_mlp.3
  295.5 7.8 %collective-permute-done.111.far_ref = bf16[128,1024]{1,0:T(8,128)(2,1)S(1)} collective-permute-done((bf16[128,1024]{1,0:T(8,128)(2,1)S(1)}, bf16[128,1024]{1,0:T(8,128)(2,1)S(1)}, u32[]{:S(2)}, u32[]{:S(2)}) %collective-permute-start.111) | collective-permute-done | bytes 262176 | tf_op jit(solution)/shard_map/ppermute | solution.py:135
  304.9 7.0 %collective-permute-done.113.refs_3_.refs_7_ = bf16[128,1024]{1,0:T(8,128)(2,1)S(1)} collective-permute-done((bf16[128,1024]{1,0:T(8,128)(2,1)S(1)}, bf16[128,1024]{1,0:T(8,128)(2,1)S(1)}, u32[]{:S(2)}, u32[]{:S(2)}) %collective-permute-start.113) | collective-permute-done | bytes 262176 | tf_op jit(solution)/shard_map/ppermute | solution.py:135
  313.4 4.5 layer__mlp_back.1
  320.6 4.5 layer__weight_grads.1
  325.1 3.3 collective-permute-done.116.refs_2_
  330.4 6.1 collective-permute-done.118.refs_3_.refs_9_
  338.6 6.9 %reduce_step_attention_back.2 = (bf16[36,1024,256]{2,1,0:T(8,128)(2,1)S(1)}, bf16[512,256]{1,0:T(8,128)(2,1)S(1)}, bf16[512,256]{1,0:T(8,128)(2,1)S(1)}, bf16[3,...) custom-call(s32[36,4]{1,0:T(8,128)S(1)} %bitcast.168, ...), custom_call_target="tpu_custom_call", output_to_operand_aliasing={{0}: (1, {})} | custom-call | tf_op jit(solution)/shard_map/reduce_step_attention_back/pallas_call | solution.py:380
  349.0 2.9 reduce_step_weight_grads.3
  351.9 3.2 collective-permute-done.126.refs_0_
  359.8 3.6 collective-permute-done.123.refs_0_
  367.4 4.5 reduce_step_mlp_back.1
  372.0 2.1 collective-permute-done.131.refs_0_
  377.3 4.5 reduce_step_weight_grads.4
  387.6 3.6 collective-permute-done.139.refs_0_
  395.2 6.9 %reduce_step_attention_back.3 = (bf16[36,1024,256]{2,1,0:T(8,128)(2,1)S(1)}, bf16[512,256]{1,0:T(8,128)(2,1)S(1)}, bf16[512,256]{1,0:T(8,128)(2,1)S(1)}, bf16[3,...) custom-call(s32[36,4]{1,0:T(8,128)S(1)} %bitcast.174, ...), custom_call_target="tpu_custom_call", output_to_operand_aliasing={{0}: (3, {})} | custom-call | tf_op jit(solution)/shard_map/reduce_step_attention_back/pallas_call | solution.py:380
  405.2 3.3 reduce_step_weight_grads.5
  408.5 2.4 collective-permute-done.148.refs_0_
  417.0 3.2 collective-permute-done.151
  426.2 10.1 %collective-permute-done.154.refs_0_ = bf16[512,256]{1,0:T(8,128)(2,1)S(1)} collective-permute-done((bf16[512,256]{1,0:T(8,128)(2,1)S(1)}, bf16[512,256]{1,0:T(8,128)(2,1)S(1)}, u32[]{:S(2)}, u32[]{:S(2)}) %collective-permute-start.154) | collective-permute-done | bytes 262176 | tf_op jit(solution)/shard_map/ppermute | solution.py:507
  443.6 5.2 collective-permute-done.158.refs_0_
  495.7 3.2 reduce_step_cond_back.1
  503.8 3.2 collective-permute-done.175
  513.4 4.0 collective-permute-done.176.refs_0_
  521.2 2.2 collective-permute-done.182.refs_0_
  532.8 2.2 collective-permute-done.186.refs_0_
  571.3 3.7 collective-permute-done.199
  581.5 3.8 collective-permute-done.204.refs_0_
  597.7 2.4 collective-permute-done.206.refs_1_
  602.1 3.1 collective-permute-done.210
  606.2 3.4 collective-permute-done.211
  611.2 60.2 %optimizer.1 = (f32[8,1024,256]{2,1,0:T(8,128)}, f32[8,1024,256]{2,1,0:T(8,128)}) custom-call(s32[8]{0:T(128)S(1)} %get-tuple-element.1005.big_ref, s32[8]{0:T(128)S(1)} %get-tuple-element.1004.left_ref, s32[8]{0:T(128)S(1)} %get-tuple-element.1003.right_ref, s32[36,4]{1,0:T(8,128)S(1)} %bitcast.203, bf16[10,16,1024]{2,1,0:T(8,128)(2,1)S(1)} %pad_maximum_fusion.1.a_ref, ...), custom_call_target="tpu_custom_call" | custom-call | tf_op jit(solution)/shard_map/optimizer/pallas_call | solution.py:837
  672.2 2.7 update_tables.1
  (650 shorter events, 354.3 us)
Async XLA Ops:
  18.0 10.7 %collective-permute-start.2 = (bf16[32,256]{1,0:T(8,128)(2,1)S(1)}, bf16[32,256]{1,0:T(8,128)(2,1)S(1)}, u32[]{:S(2)}, u32[]{:S(2)}) collective-permute-start(bf16[32,256]{1,0:T(8,128)(2,1)S(1)} %pad_maximum_fusion.15), channel_id=1, source_target_pairs={{0,2},{1,3},{2,0},{3,1},{4,6},{5,7},{6,4},{7,5},{8,10},{9,11},{10,... | collective-permute-start | bytes 49160 | tf_op jit(solution)/shard_map/ppermute | solution.py:135
  29.7 10.9 %collective-permute-start.7 = (bf16[512,256]{1,0:T(8,128)(2,1)S(1)}, bf16[512,256]{1,0:T(8,128)(2,1)S(1)}, u32[]{:S(2)}, u32[]{:S(2)}) collective-permute-start(bf16[512,256]{1,0:T(8,128)(2,1)S(1)} %get-tuple-element.487), channel_id=1, source_target_pairs={{0,8},{8,16},{16,24},{24,28},{28,20},{20,12},{12,4},{4,0},{1,9},{9... | collective-permute-start | bytes 786440 | tf_op jit(solution)/shard_map/ppermute | solution.py:433
  37.8 12.0 %collective-permute-start.10 = (bf16[512,256]{1,0:T(8,128)(2,1)S(1)}, bf16[512,256]{1,0:T(8,128)(2,1)S(1)}, u32[]{:S(2)}, u32[]{:S(2)}) collective-permute-start(bf16[512,256]{1,0:T(8,128)(2,1)S(1)} %get-tuple-element.495), channel_id=1, source_target_pairs={{0,8},{8,16},{16,24},{24,28},{28,20},{20,12},{12,4},{4,0},{1,9},{9... | collective-permute-start | bytes 786440 | tf_op jit(solution)/shard_map/ppermute | solution.py:433
  38.8 11.1 %collective-permute-start.11 = (bf16[512,256]{1,0:T(8,128)(2,1)S(1)}, bf16[512,256]{1,0:T(8,128)(2,1)S(1)}, u32[]{:S(2)}, u32[]{:S(2)}) collective-permute-start(bf16[512,256]{1,0:T(8,128)(2,1)S(1)} %get-tuple-element.496), channel_id=1, source_target_pairs={{8,0},{16,8},{24,16},{28,24},{20,28},{12,20},{4,12},{0,4},{9,1},{1... | collective-permute-start | bytes 786440 | tf_op jit(solution)/shard_map/ppermute | solution.py:433
  43.9 11.5 %collective-permute-start.14 = (bf16[512,256]{1,0:T(8,128)(2,1)S(1)}, bf16[512,256]{1,0:T(8,128)(2,1)S(1)}, u32[]{:S(2)}, u32[]{:S(2)}) collective-permute-start(bf16[512,256]{1,0:T(8,128)(2,1)S(1)} %get-tuple-element.500), channel_id=1, source_target_pairs={{0,8},{8,16},{16,24},{24,28},{28,20},{20,12},{12,4},{4,0},{1,9},{9... | collective-permute-start | bytes 786440 | tf_op jit(solution)/shard_map/ppermute | solution.py:433
  45.5 9.9 %collective-permute-start.15 = (bf16[512,256]{1,0:T(8,128)(2,1)S(1)}, bf16[512,256]{1,0:T(8,128)(2,1)S(1)}, u32[]{:S(2)}, u32[]{:S(2)}) collective-permute-start(bf16[512,256]{1,0:T(8,128)(2,1)S(1)} %get-tuple-element.501), channel_id=1, source_target_pairs={{8,0},{16,8},{24,16},{28,24},{20,28},{12,20},{4,12},{0,4},{9,1},{1... | collective-permute-start | bytes 786440 | tf_op jit(solution)/shard_map/ppermute | solution.py:433
  59.5 11.8 %collective-permute-start.21 = (bf16[512,256]{1,0:T(8,128)(2,1)S(1)}, bf16[512,256]{1,0:T(8,128)(2,1)S(1)}, u32[]{:S(2)}, u32[]{:S(2)}) collective-permute-start(bf16[512,256]{1,0:T(8,128)(2,1)S(1)} %get-tuple-element.513), channel_id=1, source_target_pairs={{0,8},{8,16},{16,24},{24,28},{28,20},{20,12},{12,4},{4,0},{1,9},{9... | collective-permute-start | bytes 786440 | tf_op jit(solution)/shard_map/ppermute | solution.py:433
  60.6 11.4 %collective-permute-start.22 = (bf16[512,256]{1,0:T(8,128)(2,1)S(1)}, bf16[512,256]{1,0:T(8,128)(2,1)S(1)}, u32[]{:S(2)}, u32[]{:S(2)}) collective-permute-start(bf16[512,256]{1,0:T(8,128)(2,1)S(1)} %get-tuple-element.514), channel_id=1, source_target_pairs={{8,0},{16,8},{24,16},{28,24},{20,28},{12,20},{4,12},{0,4},{9,1},{1... | collective-permute-start | bytes 786440 | tf_op jit(solution)/shard_map/ppermute | solution.py:433
  67.5 14.6 %collective-permute-start.24 = (bf16[512,256]{1,0:T(8,128)(2,1)S(1)}, bf16[512,256]{1,0:T(8,128)(2,1)S(1)}, u32[]{:S(2)}, u32[]{:S(2)}) collective-permute-start(bf16[512,256]{1,0:T(8,128)(2,1)S(1)} %get-tuple-element.518), channel_id=1, source_target_pairs={{0,8},{8,16},{16,24},{24,28},{28,20},{20,12},{12,4},{4,0},{1,9},{9... | collective-permute-start | bytes 786440 | tf_op jit(solution)/shard_map/ppermute | solution.py:433
  68.0 14.0 %collective-permute-start.25 = (bf16[512,256]{1,0:T(8,128)(2,1)S(1)}, bf16[512,256]{1,0:T(8,128)(2,1)S(1)}, u32[]{:S(2)}, u32[]{:S(2)}) collective-permute-start(bf16[512,256]{1,0:T(8,128)(2,1)S(1)} %get-tuple-element.519), channel_id=1, source_target_pairs={{8,0},{16,8},{24,16},{28,24},{20,28},{12,20},{4,12},{0,4},{9,1},{1... | collective-permute-start | bytes 786440 | tf_op jit(solution)/shard_map/ppermute | solution.py:433
  97.5 11.9 %collective-permute-start.33 = (f32[16,8,256]{2,0,1:T(8,128)S(1)}, f32[16,8,256]{2,0,1:T(8,128)S(1)}, u32[]{:S(2)}, u32[]{:S(2)}) collective-permute-start(f32[16,8,256]{2,0,1:T(8,128)S(1)} %slice_select_fusion), channel_id=1, source_target_pairs={{0,16},{4,20},{8,24},{12,28},{16,0},{20,4},{24,8},{28,12},{1,17},{... | collective-permute-start | bytes 393224 | tf_op jit(solution)/shard_map/ppermute | solution.py:135
  99.7 14.7 %collective-permute-start.37 = (bf16[512,256]{1,0:T(8,128)(2,1)S(1)}, bf16[512,256]{1,0:T(8,128)(2,1)S(1)}, u32[]{:S(2)}, u32[]{:S(2)}) collective-permute-start(bf16[512,256]{1,0:T(8,128)(2,1)S(1)} %get-tuple-element.539), channel_id=1, source_target_pairs={{0,8},{8,16},{16,24},{24,28},{28,20},{20,12},{12,4},{4,0},{1,9},{9... | collective-permute-start | bytes 786440 | tf_op jit(solution)/shard_map/ppermute | solution.py:433
  100.6 13.8 %collective-permute-start.38 = (bf16[512,256]{1,0:T(8,128)(2,1)S(1)}, bf16[512,256]{1,0:T(8,128)(2,1)S(1)}, u32[]{:S(2)}, u32[]{:S(2)}) collective-permute-start(bf16[512,256]{1,0:T(8,128)(2,1)S(1)} %get-tuple-element.540), channel_id=1, source_target_pairs={{8,0},{16,8},{24,16},{28,24},{20,28},{12,20},{4,12},{0,4},{9,1},{1... | collective-permute-start | bytes 786440 | tf_op jit(solution)/shard_map/ppermute | solution.py:433
  115.5 10.4 %collective-permute-start.45 = (bf16[512,256]{1,0:T(8,128)(2,1)S(1)}, bf16[512,256]{1,0:T(8,128)(2,1)S(1)}, u32[]{:S(2)}, u32[]{:S(2)}) collective-permute-start(bf16[512,256]{1,0:T(8,128)(2,1)S(1)} %get-tuple-element.551), channel_id=1, source_target_pairs={{0,8},{8,16},{16,24},{24,28},{28,20},{20,12},{12,4},{4,0},{1,9},{9... | collective-permute-start | bytes 786440 | tf_op jit(solution)/shard_map/ppermute | solution.py:433
  130.2 10.7 %collective-permute-start.50 = (bf16[512,256]{1,0:T(8,128)(2,1)S(1)}, bf16[512,256]{1,0:T(8,128)(2,1)S(1)}, u32[]{:S(2)}, u32[]{:S(2)}) collective-permute-start(bf16[512,256]{1,0:T(8,128)(2,1)S(1)} %get-tuple-element.568), channel_id=1, source_target_pairs={{0,8},{8,16},{16,24},{24,28},{28,20},{20,12},{12,4},{4,0},{1,9},{9... | collective-permute-start | bytes 786440 | tf_op jit(solution)/shard_map/ppermute | solution.py:433
  136.7 10.8 %collective-permute-start.48 = (bf16[512,256]{1,0:T(8,128)(2,1)S(1)}, bf16[512,256]{1,0:T(8,128)(2,1)S(1)}, u32[]{:S(2)}, u32[]{:S(2)}) collective-permute-start(bf16[512,256]{1,0:T(8,128)(2,1)S(1)} %get-tuple-element.566), channel_id=1, source_target_pairs={{0,8},{8,16},{16,24},{24,28},{28,20},{20,12},{12,4},{4,0},{1,9},{9... | collective-permute-start | bytes 786440 | tf_op jit(solution)/shard_map/ppermute | solution.py:433
  138.3 11.8 %collective-permute-start.49 = (bf16[512,256]{1,0:T(8,128)(2,1)S(1)}, bf16[512,256]{1,0:T(8,128)(2,1)S(1)}, u32[]{:S(2)}, u32[]{:S(2)}) collective-permute-start(bf16[512,256]{1,0:T(8,128)(2,1)S(1)} %get-tuple-element.567), channel_id=1, source_target_pairs={{8,0},{16,8},{24,16},{28,24},{20,28},{12,20},{4,12},{0,4},{9,1},{1... | collective-permute-start | bytes 786440 | tf_op jit(solution)/shard_map/ppermute | solution.py:433
  138.8 11.3 %collective-permute-start.54 = (bf16[128,1024]{1,0:T(8,128)(2,1)S(1)}, bf16[128,1024]{1,0:T(8,128)(2,1)S(1)}, u32[]{:S(2)}, u32[]{:S(2)}) collective-permute-start(bf16[128,1024]{1,0:T(8,128)(2,1)S(1)} %collective-permute-done.53.refs_5_), channel_id=1, source_target_pairs={{0,1},{1,0},{2,3},{3,2},{4,5},{5,4},{6,7},{7,6},{8,9},{9,8},{10,11... | collective-permute-start | bytes 786440 | tf_op jit(solution)/shard_map/ppermute | solution.py:135
  145.4 20.1 %collective-permute-start.55 = (bf16[512,256]{1,0:T(8,128)(2,1)S(1)}, bf16[512,256]{1,0:T(8,128)(2,1)S(1)}, u32[]{:S(2)}, u32[]{:S(2)}) collective-permute-start(bf16[512,256]{1,0:T(8,128)(2,1)S(1)} %get-tuple-element.578), channel_id=1, source_target_pairs={{0,8},{8,16},{16,24},{24,28},{28,20},{20,12},{12,4},{4,0},{1,9},{9... | collective-permute-start | bytes 786440 | tf_op jit(solution)/shard_map/ppermute | solution.py:433
  146.2 19.3 %collective-permute-start.56 = (bf16[512,256]{1,0:T(8,128)(2,1)S(1)}, bf16[512,256]{1,0:T(8,128)(2,1)S(1)}, u32[]{:S(2)}, u32[]{:S(2)}) collective-permute-start(bf16[512,256]{1,0:T(8,128)(2,1)S(1)} %get-tuple-element.579), channel_id=1, source_target_pairs={{8,0},{16,8},{24,16},{28,24},{20,28},{12,20},{4,12},{0,4},{9,1},{1... | collective-permute-start | bytes 786440 | tf_op jit(solution)/shard_map/ppermute | solution.py:433
  169.3 11.1 %collective-permute-start.63 = (bf16[512,256]{1,0:T(8,128)(2,1)S(1)}, bf16[512,256]{1,0:T(8,128)(2,1)S(1)}, u32[]{:S(2)}, u32[]{:S(2)}) collective-permute-start(bf16[512,256]{1,0:T(8,128)(2,1)S(1)} %get-tuple-element.584), channel_id=1, source_target_pairs={{0,8},{8,16},{16,24},{24,28},{28,20},{20,12},{12,4},{4,0},{1,9},{9... | collective-permute-start | bytes 786440 | tf_op jit(solution)/shard_map/ppermute | solution.py:433
  170.2 11.1 %collective-permute-start.64 = (bf16[512,256]{1,0:T(8,128)(2,1)S(1)}, bf16[512,256]{1,0:T(8,128)(2,1)S(1)}, u32[]{:S(2)}, u32[]{:S(2)}) collective-permute-start(bf16[512,256]{1,0:T(8,128)(2,1)S(1)} %get-tuple-element.585), channel_id=1, source_target_pairs={{8,0},{16,8},{24,16},{28,24},{20,28},{12,20},{4,12},{0,4},{9,1},{1... | collective-permute-start | bytes 786440 | tf_op jit(solution)/shard_map/ppermute | solution.py:433
  184.2 10.4 %collective-permute-start.74 = (bf16[128,1024]{1,0:T(8,128)(2,1)S(1)}, bf16[128,1024]{1,0:T(8,128)(2,1)S(1)}, u32[]{:S(2)}, u32[]{:S(2)}) collective-permute-start(bf16[128,1024]{1,0:T(8,128)(2,1)S(1)} %get-tuple-element.590.refs_3_), channel_id=1, source_target_pairs={{0,2},{1,3},{2,0},{3,1},{4,6},{5,7},{6,4},{7,5},{8,10},{9,11},{10,... | collective-permute-start | bytes 786440 | tf_op jit(solution)/shard_map/ppermute | solution.py:135
  192.7 11.2 %collective-permute-start.71 = (bf16[512,256]{1,0:T(8,128)(2,1)S(1)}, bf16[512,256]{1,0:T(8,128)(2,1)S(1)}, u32[]{:S(2)}, u32[]{:S(2)}) collective-permute-start(bf16[512,256]{1,0:T(8,128)(2,1)S(1)} %get-tuple-element.605), channel_id=1, source_target_pairs={{0,8},{8,16},{16,24},{24,28},{28,20},{20,12},{12,4},{4,0},{1,9},{9... | collective-permute-start | bytes 786440 | tf_op jit(solution)/shard_map/ppermute | solution.py:433
  194.7 11.8 %collective-permute-start.72 = (bf16[512,256]{1,0:T(8,128)(2,1)S(1)}, bf16[512,256]{1,0:T(8,128)(2,1)S(1)}, u32[]{:S(2)}, u32[]{:S(2)}) collective-permute-start(bf16[512,256]{1,0:T(8,128)(2,1)S(1)} %get-tuple-element.606), channel_id=1, source_target_pairs={{8,0},{16,8},{24,16},{28,24},{20,28},{12,20},{4,12},{0,4},{9,1},{1... | collective-permute-start | bytes 786440 | tf_op jit(solution)/shard_map/ppermute | solution.py:433
  194.8 14.8 %collective-permute-start.75 = (bf16[128,1024]{1,0:T(8,128)(2,1)S(1)}, bf16[128,1024]{1,0:T(8,128)(2,1)S(1)}, u32[]{:S(2)}, u32[]{:S(2)}) collective-permute-start(bf16[128,1024]{1,0:T(8,128)(2,1)S(1)} %collective-permute-done.74.refs_5_), channel_id=1, source_target_pairs={{0,1},{1,0},{2,3},{3,2},{4,5},{5,4},{6,7},{7,6},{8,9},{9,8},{10,11... | collective-permute-start | bytes 786440 | tf_op jit(solution)/shard_map/ppermute | solution.py:135
  219.8 10.7 %collective-permute-start.84 = (bf16[512,256]{1,0:T(8,128)(2,1)S(1)}, bf16[512,256]{1,0:T(8,128)(2,1)S(1)}, u32[]{:S(2)}, u32[]{:S(2)}) collective-permute-start(bf16[512,256]{1,0:T(8,128)(2,1)S(1)} %get-tuple-element.621), channel_id=1, source_target_pairs={{0,8},{8,16},{16,24},{24,28},{28,20},{20,12},{12,4},{4,0},{1,9},{9... | collective-permute-start | bytes 786440 | tf_op jit(solution)/shard_map/ppermute | solution.py:433
  220.7 10.5 %collective-permute-start.85 = (bf16[512,256]{1,0:T(8,128)(2,1)S(1)}, bf16[512,256]{1,0:T(8,128)(2,1)S(1)}, u32[]{:S(2)}, u32[]{:S(2)}) collective-permute-start(bf16[512,256]{1,0:T(8,128)(2,1)S(1)} %get-tuple-element.622), channel_id=1, source_target_pairs={{8,0},{16,8},{24,16},{28,24},{20,28},{12,20},{4,12},{0,4},{9,1},{1... | collective-permute-start | bytes 786440 | tf_op jit(solution)/shard_map/ppermute | solution.py:433
  248.1 11.1 %collective-permute-start.92 = (bf16[512,256]{1,0:T(8,128)(2,1)S(1)}, bf16[512,256]{1,0:T(8,128)(2,1)S(1)}, u32[]{:S(2)}, u32[]{:S(2)}) collective-permute-start(bf16[512,256]{1,0:T(8,128)(2,1)S(1)} %get-tuple-element.646), channel_id=1, source_target_pairs={{0,8},{8,16},{16,24},{24,28},{28,20},{20,12},{12,4},{4,0},{1,9},{9... | collective-permute-start | bytes 786440 | tf_op jit(solution)/shard_map/ppermute | solution.py:433
  248.4 11.1 %collective-permute-start.93 = (bf16[512,256]{1,0:T(8,128)(2,1)S(1)}, bf16[512,256]{1,0:T(8,128)(2,1)S(1)}, u32[]{:S(2)}, u32[]{:S(2)}) collective-permute-start(bf16[512,256]{1,0:T(8,128)(2,1)S(1)} %get-tuple-element.647), channel_id=1, source_target_pairs={{8,0},{16,8},{24,16},{28,24},{20,28},{12,20},{4,12},{0,4},{9,1},{1... | collective-permute-start | bytes 786440 | tf_op jit(solution)/shard_map/ppermute | solution.py:433
  256.5 10.2 %collective-permute-start.100 = (bf16[512,256]{1,0:T(8,128)(2,1)S(1)}, bf16[512,256]{1,0:T(8,128)(2,1)S(1)}, u32[]{:S(2)}, u32[]{:S(2)}) collective-permute-start(bf16[512,256]{1,0:T(8,128)(2,1)S(1)} %get-tuple-element.659), channel_id=1, source_target_pairs={{8,0},{16,8},{24,16},{28,24},{20,28},{12,20},{4,12},{0,4},{9,1},{1... | collective-permute-start | bytes 786440 | tf_op jit(solution)/shard_map/ppermute | solution.py:433
  258.1 10.3 %collective-permute-start.108 = (bf16[128,1024]{1,0:T(8,128)(2,1)S(1)}, bf16[128,1024]{1,0:T(8,128)(2,1)S(1)}, u32[]{:S(2)}, u32[]{:S(2)}) collective-permute-start(bf16[128,1024]{1,0:T(8,128)(2,1)S(1)} %get-tuple-element.652.refs_5_.refs_1_), channel_id=1, source_target_pairs={{0,2},{1,3},{2,0},{3,1},{4,6},{5,7},{6,4},{7,5},{8,10},{9,11},{10,... | collective-permute-start | bytes 786440 | tf_op jit(solution)/shard_map/ppermute | solution.py:135
  259.1 10.5 %collective-permute-start.107 = (bf16[128,1024]{1,0:T(8,128)(2,1)S(1)}, bf16[128,1024]{1,0:T(8,128)(2,1)S(1)}, u32[]{:S(2)}, u32[]{:S(2)}) collective-permute-start(bf16[128,1024]{1,0:T(8,128)(2,1)S(1)} %get-tuple-element.652.refs_5_.refs_1_), channel_id=1, source_target_pairs={{0,1},{1,0},{2,3},{3,2},{4,5},{5,4},{6,7},{7,6},{8,9},{9,8},{10,11... | collective-permute-start | bytes 786440 | tf_op jit(solution)/shard_map/ppermute | solution.py:135
  260.5 10.5 %collective-permute-start.97 = (bf16[512,256]{1,0:T(8,128)(2,1)S(1)}, bf16[512,256]{1,0:T(8,128)(2,1)S(1)}, u32[]{:S(2)}, u32[]{:S(2)}) collective-permute-start(bf16[512,256]{1,0:T(8,128)(2,1)S(1)} %get-tuple-element.656), channel_id=1, source_target_pairs={{0,8},{8,16},{16,24},{24,28},{28,20},{20,12},{12,4},{4,0},{1,9},{9... | collective-permute-start | bytes 786440 | tf_op jit(solution)/shard_map/ppermute | solution.py:433
  267.6 10.0 %collective-permute-start.103 = (bf16[512,256]{1,0:T(8,128)(2,1)S(1)}, bf16[512,256]{1,0:T(8,128)(2,1)S(1)}, u32[]{:S(2)}, u32[]{:S(2)}) collective-permute-start(bf16[512,256]{1,0:T(8,128)(2,1)S(1)} %get-tuple-element.664), channel_id=1, source_target_pairs={{0,8},{8,16},{16,24},{24,28},{28,20},{20,12},{12,4},{4,0},{1,9},{9... | collective-permute-start | bytes 786440 | tf_op jit(solution)/shard_map/ppermute | solution.py:433
  268.4 11.8 %collective-permute-start.104 = (bf16[512,256]{1,0:T(8,128)(2,1)S(1)}, bf16[512,256]{1,0:T(8,128)(2,1)S(1)}, u32[]{:S(2)}, u32[]{:S(2)}) collective-permute-start(bf16[512,256]{1,0:T(8,128)(2,1)S(1)} %get-tuple-element.665), channel_id=1, source_target_pairs={{8,0},{16,8},{24,16},{28,24},{20,28},{12,20},{4,12},{0,4},{9,1},{1... | collective-permute-start | bytes 786440 | tf_op jit(solution)/shard_map/ppermute | solution.py:433
  269.7 13.6 %collective-permute-start.109 = (bf16[128,1024]{1,0:T(8,128)(2,1)S(1)}, bf16[128,1024]{1,0:T(8,128)(2,1)S(1)}, u32[]{:S(2)}, u32[]{:S(2)}) collective-permute-start(bf16[128,1024]{1,0:T(8,128)(2,1)S(1)} %collective-permute-done.108.refs_7_.refs_3_), channel_id=1, source_target_pairs={{0,1},{1,0},{2,3},{3,2},{4,5},{5,4},{6,7},{7,6},{8,9},{9,8},{10,11... | collective-permute-start | bytes 786440 | tf_op jit(solution)/shard_map/ppermute | solution.py:135
  422.1 18.4 %collective-permute-start.152 = (bf16[608,256]{1,0:T(8,128)(2,1)S(1)}, bf16[608,256]{1,0:T(8,128)(2,1)S(1)}, u32[]{:S(2)}, u32[]{:S(2)}) collective-permute-start(bf16[608,256]{1,0:T(8,128)(2,1)S(1)} %get-tuple-element.795), channel_id=1, source_target_pairs={{8,0},{16,8},{24,16},{28,24},{20,28},{12,20},{4,12},{0,4},{9,1},{1... | collective-permute-start | bytes 933896 | tf_op jit(solution)/shard_map/ppermute | solution.py:507
  423.5 17.0 %collective-permute-start.153 = (bf16[608,256]{1,0:T(8,128)(2,1)S(1)}, bf16[608,256]{1,0:T(8,128)(2,1)S(1)}, u32[]{:S(2)}, u32[]{:S(2)}) collective-permute-start(bf16[608,256]{1,0:T(8,128)(2,1)S(1)} %get-tuple-element.796), channel_id=1, source_target_pairs={{0,8},{8,16},{16,24},{24,28},{28,20},{20,12},{12,4},{4,0},{1,9},{9... | collective-permute-start | bytes 933896 | tf_op jit(solution)/shard_map/ppermute | solution.py:507
  424.2 12.2 %collective-permute-start.154 = (bf16[512,256]{1,0:T(8,128)(2,1)S(1)}, bf16[512,256]{1,0:T(8,128)(2,1)S(1)}, u32[]{:S(2)}, u32[]{:S(2)}) collective-permute-start(bf16[512,256]{1,0:T(8,128)(2,1)S(1)} %get-tuple-element.788), channel_id=1, source_target_pairs={{8,0},{16,8},{24,16},{28,24},{20,28},{12,20},{4,12},{0,4},{9,1},{1... | collective-permute-start | bytes 786440 | tf_op jit(solution)/shard_map/ppermute | solution.py:507
  425.5 12.0 %collective-permute-start.155 = (bf16[512,256]{1,0:T(8,128)(2,1)S(1)}, bf16[512,256]{1,0:T(8,128)(2,1)S(1)}, u32[]{:S(2)}, u32[]{:S(2)}) collective-permute-start(bf16[512,256]{1,0:T(8,128)(2,1)S(1)} %get-tuple-element.789), channel_id=1, source_target_pairs={{0,8},{8,16},{16,24},{24,28},{28,20},{20,12},{12,4},{4,0},{1,9},{9... | collective-permute-start | bytes 786440 | tf_op jit(solution)/shard_map/ppermute | solution.py:507
  438.4 10.3 %collective-permute-start.158 = (bf16[608,256]{1,0:T(8,128)(2,1)S(1)}, bf16[608,256]{1,0:T(8,128)(2,1)S(1)}, u32[]{:S(2)}, u32[]{:S(2)}) collective-permute-start(bf16[608,256]{1,0:T(8,128)(2,1)S(1)} %get-tuple-element.801), channel_id=1, source_target_pairs={{8,0},{16,8},{24,16},{28,24},{20,28},{12,20},{4,12},{0,4},{9,1},{1... | collective-permute-start | bytes 933896 | tf_op jit(solution)/shard_map/ppermute | solution.py:507
  440.2 10.3 %collective-permute-start.159 = (bf16[608,256]{1,0:T(8,128)(2,1)S(1)}, bf16[608,256]{1,0:T(8,128)(2,1)S(1)}, u32[]{:S(2)}, u32[]{:S(2)}) collective-permute-start(bf16[608,256]{1,0:T(8,128)(2,1)S(1)} %get-tuple-element.802), channel_id=1, source_target_pairs={{0,8},{8,16},{16,24},{24,28},{28,20},{20,12},{12,4},{4,0},{1,9},{9... | collective-permute-start | bytes 933896 | tf_op jit(solution)/shard_map/ppermute | solution.py:507
  441.5 13.9 %collective-permute-start.156 = (bf16[608,256]{1,0:T(8,128)(2,1)S(1)}, bf16[608,256]{1,0:T(8,128)(2,1)S(1)}, u32[]{:S(2)}, u32[]{:S(2)}) collective-permute-start(bf16[608,256]{1,0:T(8,128)(2,1)S(1)} %get-tuple-element.799), channel_id=1, source_target_pairs={{8,0},{16,8},{24,16},{28,24},{20,28},{12,20},{4,12},{0,4},{9,1},{1... | collective-permute-start | bytes 933896 | tf_op jit(solution)/shard_map/ppermute | solution.py:507
  443.2 13.9 %collective-permute-start.157 = (bf16[608,256]{1,0:T(8,128)(2,1)S(1)}, bf16[608,256]{1,0:T(8,128)(2,1)S(1)}, u32[]{:S(2)}, u32[]{:S(2)}) collective-permute-start(bf16[608,256]{1,0:T(8,128)(2,1)S(1)} %get-tuple-element.800), channel_id=1, source_target_pairs={{0,8},{8,16},{16,24},{24,28},{28,20},{20,12},{12,4},{4,0},{1,9},{9... | collective-permute-start | bytes 933896 | tf_op jit(solution)/shard_map/ppermute | solution.py:507
  451.5 10.6 %collective-permute-start.162 = (bf16[608,256]{1,0:T(8,128)(2,1)S(1)}, bf16[608,256]{1,0:T(8,128)(2,1)S(1)}, u32[]{:S(2)}, u32[]{:S(2)}) collective-permute-start(bf16[608,256]{1,0:T(8,128)(2,1)S(1)} %get-tuple-element.807), channel_id=1, source_target_pairs={{8,0},{16,8},{24,16},{28,24},{20,28},{12,20},{4,12},{0,4},{9,1},{1... | collective-permute-start | bytes 933896 | tf_op jit(solution)/shard_map/ppermute | solution.py:507
  452.7 11.1 %collective-permute-start.163 = (bf16[608,256]{1,0:T(8,128)(2,1)S(1)}, bf16[608,256]{1,0:T(8,128)(2,1)S(1)}, u32[]{:S(2)}, u32[]{:S(2)}) collective-permute-start(bf16[608,256]{1,0:T(8,128)(2,1)S(1)} %get-tuple-element.808), channel_id=1, source_target_pairs={{0,8},{8,16},{16,24},{24,28},{28,20},{20,12},{12,4},{4,0},{1,9},{9... | collective-permute-start | bytes 933896 | tf_op jit(solution)/shard_map/ppermute | solution.py:507
  458.1 10.7 %collective-permute-start.160 = (bf16[608,256]{1,0:T(8,128)(2,1)S(1)}, bf16[608,256]{1,0:T(8,128)(2,1)S(1)}, u32[]{:S(2)}, u32[]{:S(2)}) collective-permute-start(bf16[608,256]{1,0:T(8,128)(2,1)S(1)} %get-tuple-element.805), channel_id=1, source_target_pairs={{8,0},{16,8},{24,16},{28,24},{20,28},{12,20},{4,12},{0,4},{9,1},{1... | collective-permute-start | bytes 933896 | tf_op jit(solution)/shard_map/ppermute | solution.py:507
  459.5 11.0 %collective-permute-start.161 = (bf16[608,256]{1,0:T(8,128)(2,1)S(1)}, bf16[608,256]{1,0:T(8,128)(2,1)S(1)}, u32[]{:S(2)}, u32[]{:S(2)}) collective-permute-start(bf16[608,256]{1,0:T(8,128)(2,1)S(1)} %get-tuple-element.806), channel_id=1, source_target_pairs={{0,8},{8,16},{16,24},{24,28},{28,20},{20,12},{12,4},{4,0},{1,9},{9... | collective-permute-start | bytes 933896 | tf_op jit(solution)/shard_map/ppermute | solution.py:507
  464.8 10.7 %collective-permute-start.166 = (bf16[608,256]{1,0:T(8,128)(2,1)S(1)}, bf16[608,256]{1,0:T(8,128)(2,1)S(1)}, u32[]{:S(2)}, u32[]{:S(2)}) collective-permute-start(bf16[608,256]{1,0:T(8,128)(2,1)S(1)} %get-tuple-element.813), channel_id=1, source_target_pairs={{8,0},{16,8},{24,16},{28,24},{20,28},{12,20},{4,12},{0,4},{9,1},{1... | collective-permute-start | bytes 933896 | tf_op jit(solution)/shard_map/ppermute | solution.py:507
  466.2 11.0 %collective-permute-start.167 = (bf16[608,256]{1,0:T(8,128)(2,1)S(1)}, bf16[608,256]{1,0:T(8,128)(2,1)S(1)}, u32[]{:S(2)}, u32[]{:S(2)}) collective-permute-start(bf16[608,256]{1,0:T(8,128)(2,1)S(1)} %get-tuple-element.814), channel_id=1, source_target_pairs={{0,8},{8,16},{16,24},{24,28},{28,20},{20,12},{12,4},{4,0},{1,9},{9... | collective-permute-start | bytes 933896 | tf_op jit(solution)/shard_map/ppermute | solution.py:507
  471.4 10.7 %collective-permute-start.164 = (bf16[608,256]{1,0:T(8,128)(2,1)S(1)}, bf16[608,256]{1,0:T(8,128)(2,1)S(1)}, u32[]{:S(2)}, u32[]{:S(2)}) collective-permute-start(bf16[608,256]{1,0:T(8,128)(2,1)S(1)} %get-tuple-element.811), channel_id=1, source_target_pairs={{8,0},{16,8},{24,16},{28,24},{20,28},{12,20},{4,12},{0,4},{9,1},{1... | collective-permute-start | bytes 933896 | tf_op jit(solution)/shard_map/ppermute | solution.py:507
  472.8 11.0 %collective-permute-start.165 = (bf16[608,256]{1,0:T(8,128)(2,1)S(1)}, bf16[608,256]{1,0:T(8,128)(2,1)S(1)}, u32[]{:S(2)}, u32[]{:S(2)}) collective-permute-start(bf16[608,256]{1,0:T(8,128)(2,1)S(1)} %get-tuple-element.812), channel_id=1, source_target_pairs={{0,8},{8,16},{16,24},{24,28},{28,20},{20,12},{12,4},{4,0},{1,9},{9... | collective-permute-start | bytes 933896 | tf_op jit(solution)/shard_map/ppermute | solution.py:507
  478.1 10.7 %collective-permute-start.170 = (bf16[608,256]{1,0:T(8,128)(2,1)S(1)}, bf16[608,256]{1,0:T(8,128)(2,1)S(1)}, u32[]{:S(2)}, u32[]{:S(2)}) collective-permute-start(bf16[608,256]{1,0:T(8,128)(2,1)S(1)} %get-tuple-element.819), channel_id=1, source_target_pairs={{8,0},{16,8},{24,16},{28,24},{20,28},{12,20},{4,12},{0,4},{9,1},{1... | collective-permute-start | bytes 933896 | tf_op jit(solution)/shard_map/ppermute | solution.py:507
  479.5 11.0 %collective-permute-start.171 = (bf16[608,256]{1,0:T(8,128)(2,1)S(1)}, bf16[608,256]{1,0:T(8,128)(2,1)S(1)}, u32[]{:S(2)}, u32[]{:S(2)}) collective-permute-start(bf16[608,256]{1,0:T(8,128)(2,1)S(1)} %get-tuple-element.820), channel_id=1, source_target_pairs={{0,8},{8,16},{16,24},{24,28},{28,20},{20,12},{12,4},{4,0},{1,9},{9... | collective-permute-start | bytes 933896 | tf_op jit(solution)/shard_map/ppermute | solution.py:507
  499.0 11.2 %collective-permute-start.178 = (bf16[512,256]{1,0:T(8,128)(2,1)S(1)}, bf16[512,256]{1,0:T(8,128)(2,1)S(1)}, u32[]{:S(2)}, u32[]{:S(2)}) collective-permute-start(bf16[512,256]{1,0:T(8,128)(2,1)S(1)} %get-tuple-element.848), channel_id=1, source_target_pairs={{8,0},{16,8},{24,16},{28,24},{20,28},{12,20},{4,12},{0,4},{9,1},{1... | collective-permute-start | bytes 786440 | tf_op jit(solution)/shard_map/ppermute | solution.py:507
  499.9 10.3 %collective-permute-start.179 = (bf16[512,256]{1,0:T(8,128)(2,1)S(1)}, bf16[512,256]{1,0:T(8,128)(2,1)S(1)}, u32[]{:S(2)}, u32[]{:S(2)}) collective-permute-start(bf16[512,256]{1,0:T(8,128)(2,1)S(1)} %get-tuple-element.849), channel_id=1, source_target_pairs={{0,8},{8,16},{16,24},{24,28},{28,20},{20,12},{12,4},{4,0},{1,9},{9... | collective-permute-start | bytes 786440 | tf_op jit(solution)/shard_map/ppermute | solution.py:507
  511.3 12.1 %collective-permute-start.182 = (bf16[544,256]{1,0:T(8,128)(2,1)S(1)}, bf16[544,256]{1,0:T(8,128)(2,1)S(1)}, u32[]{:S(2)}, u32[]{:S(2)}) collective-permute-start(bf16[544,256]{1,0:T(8,128)(2,1)S(1)} %get-tuple-element.855), channel_id=1, source_target_pairs={{8,0},{16,8},{24,16},{28,24},{20,28},{12,20},{4,12},{0,4},{9,1},{1... | collective-permute-start | bytes 835592 | tf_op jit(solution)/shard_map/ppermute | solution.py:507
  512.0 12.1 %collective-permute-start.183 = (bf16[544,256]{1,0:T(8,128)(2,1)S(1)}, bf16[544,256]{1,0:T(8,128)(2,1)S(1)}, u32[]{:S(2)}, u32[]{:S(2)}) collective-permute-start(bf16[544,256]{1,0:T(8,128)(2,1)S(1)} %get-tuple-element.856), channel_id=1, source_target_pairs={{0,8},{8,16},{16,24},{24,28},{28,20},{20,12},{12,4},{4,0},{1,9},{9... | collective-permute-start | bytes 835592 | tf_op jit(solution)/shard_map/ppermute | solution.py:507
  525.1 9.9 %collective-permute-start.186 = (bf16[544,256]{1,0:T(8,128)(2,1)S(1)}, bf16[544,256]{1,0:T(8,128)(2,1)S(1)}, u32[]{:S(2)}, u32[]{:S(2)}) collective-permute-start(bf16[544,256]{1,0:T(8,128)(2,1)S(1)} %get-tuple-element.861), channel_id=1, source_target_pairs={{8,0},{16,8},{24,16},{28,24},{20,28},{12,20},{4,12},{0,4},{9,1},{1... | collective-permute-start | bytes 835592 | tf_op jit(solution)/shard_map/ppermute | solution.py:507
  579.3 11.6 %collective-permute-start.202 = (bf16[512,256]{1,0:T(8,128)(2,1)S(1)}, bf16[512,256]{1,0:T(8,128)(2,1)S(1)}, u32[]{:S(2)}, u32[]{:S(2)}) collective-permute-start(bf16[512,256]{1,0:T(8,128)(2,1)S(1)} %get-tuple-element.906), channel_id=1, source_target_pairs={{8,0},{16,8},{24,16},{28,24},{20,28},{12,20},{4,12},{0,4},{9,1},{1... | collective-permute-start | bytes 786440 | tf_op jit(solution)/shard_map/ppermute | solution.py:507
  580.4 11.7 %collective-permute-start.203 = (bf16[512,256]{1,0:T(8,128)(2,1)S(1)}, bf16[512,256]{1,0:T(8,128)(2,1)S(1)}, u32[]{:S(2)}, u32[]{:S(2)}) collective-permute-start(bf16[512,256]{1,0:T(8,128)(2,1)S(1)} %get-tuple-element.907), channel_id=1, source_target_pairs={{0,8},{8,16},{16,24},{24,28},{28,20},{20,12},{12,4},{4,0},{1,9},{9... | collective-permute-start | bytes 786440 | tf_op jit(solution)/shard_map/ppermute | solution.py:507
  587.6 10.1 %collective-permute-start.209 = (bf16[512,256]{1,0:T(8,128)(2,1)S(1)}, bf16[512,256]{1,0:T(8,128)(2,1)S(1)}, u32[]{:S(2)}, u32[]{:S(2)}) collective-permute-start(bf16[512,256]{1,0:T(8,128)(2,1)S(1)} %get-tuple-element.913), channel_id=1, source_target_pairs={{0,8},{8,16},{16,24},{24,28},{28,20},{20,12},{12,4},{4,0},{1,9},{9... | collective-permute-start | bytes 786440 | tf_op jit(solution)/shard_map/ppermute | solution.py:507
  609.7 61.7 %collective-permute-start.212 = (f32[56,256]{1,0:T(8,128)S(1)}, f32[56,256]{1,0:T(8,128)S(1)}, u32[]{:S(2)}, u32[]{:S(2)}) collective-permute-start(f32[56,256]{1,0:T(8,128)S(1)} %add.213), channel_id=1, source_target_pairs={{0,16},{4,20},{8,24},{12,28},{16,0},{20,4},{24,8},{28,12},{1,17},{... | collective-permute-start | bytes 172040 | tf_op jit(solution)/shard_map/ppermute | solution.py:135
  (185 other events, 1863.7 us)

commit v2 on v1

--- a/solution.py
+++ b/solution.py
@@ -181,8 +181,11 @@
     return flip(values, "tensor", 2, 4)
 
 
-def gather_tokens(own):
-    beside, across = yield (core_flip(own), x_flip(own))
+def gather_tokens(own, waits=1):
+    flying = core_flip(own), x_flip(own)
+    for _ in range(waits):
+        flying = yield flying
+    beside, across = flying
     return own, beside, across, core_flip(across)
 
 
@@ -515,6 +518,7 @@
         for start, payload in zip(starts, payloads):
             for j in range(far):
                 self.mail[start + j * self.depth] = (payload, j)
+        ISSUED.extend(payloads[1:])
         last = starts[-1] + far * self.depth
         assert len(payloads) <= self.depth and last < self.steps
         while self.at <= last:
@@ -791,10 +795,11 @@
     return NS_COEF[0] * x + (dot(xh, ph) + (dot(xl, ph) + dot(xh, pl_)))
 
 
-def newton_kernel(n_last, big_ref, left_ref, right_ref, tab_ref, a_ref, b_ref, bank_ref, mom_ref, *refs):
+def newton_kernel(n_last, base, big_ref, left_ref, right_ref, tab_ref, a_ref, b_ref, bank_ref, mom_ref, *refs):
     held, got = refs[0], refs[1 : 1 + n_last]
-    new_ref, mom_new_ref, grad, sem = refs[1 + n_last :]
-    s = pl.program_id(0)
+    new_ref, mom_new_ref, mark_ref, grad, sem = refs[-5:]
+    s = base + pl.program_id(0)
+    mark_ref[...] = jnp.zeros_like(mark_ref)
     unit, left, right = big_ref[s], left_ref[s], right_ref[s]
     half = got[0].shape[0]
 
@@ -831,29 +836,52 @@
         new_ref[0] = bank_ref[0] - LR_MUON * x
 
 
-def optimizer(big_slots, left_slots, right_slots, tab, a_all, b_all, master, momentum, held, got):
-    n_slots, rows, columns = master.shape
-    block = pl.BlockSpec((1, rows, columns), lambda s, *t: (s, 0, 0))
-    return pl.pallas_call(
-        functools.partial(newton_kernel, len(got)),
-        grid_spec=pltpu.PrefetchScalarGridSpec(
-            num_scalar_prefetch=4,
-            grid=(n_slots,),
-            in_specs=[
-                pl.BlockSpec(a_all.shape, lambda s, *t: (0, 0, 0)),
-                pl.BlockSpec(b_all.shape, lambda s, *t: (0, 0, 0)),
-                block,
-                block,
-            ]
-            + [pl.BlockSpec(memory_space=pl.ANY)]
-            + [pl.BlockSpec(g.shape, lambda s, *t: (0, 0)) for g in got],
-            out_specs=[block, block],
-            scratch_shapes=[pltpu.VMEM((rows, columns), BF16), pltpu.SemaphoreType.DMA((1,))],
-        ),
-        out_shape=[shape(master.shape, F32), shape(momentum.shape, F32)],
-        compiler_params=params(SCOPE, dimension_semantics=("arbitrary",)),
-        name="optimizer",
-    )(big_slots, left_slots, right_slots, tab, a_all, b_all, in_hbm(master), in_hbm(momentum), held, *got)
+class Optimizer:
+    def __init__(self, slots, tab, a_all, b_all, master, momentum, held, got):
+        self.scalars = [*slots, tab]
+        self.arrays = [a_all, b_all, in_hbm(master), in_hbm(momentum), held, *got]
+        self.news = []
+        self.at = 0
+
+    def step(self, after=(), count=3):
+        a_all, b_all, master, momentum, held, *got = self.arrays
+        n_slots, rows, columns = master.shape
+        base, count = self.at, min(count, n_slots - self.at)
+        if count == 0:
+            return ()
+        self.at += count
+        block = pl.BlockSpec((1, rows, columns), lambda s, *t: (base + s, 0, 0))
+        any_spec = pl.BlockSpec(memory_space=pl.ANY)
+        scalars = [order(self.scalars[0], after)] + self.scalars[1:]
+        first = len(scalars) + len(self.arrays)
+        *self.news, mark = pl.pallas_call(
+            functools.partial(newton_kernel, len(got), base),
+            grid_spec=pltpu.PrefetchScalarGridSpec(
+                num_scalar_prefetch=len(scalars),
+                grid=(count,),
+                in_specs=[
+                    pl.BlockSpec(a_all.shape, lambda s, *t: (0, 0, 0)),
+                    pl.BlockSpec(b_all.shape, lambda s, *t: (0, 0, 0)),
+                    block,
+                    block,
+                    any_spec,
+                ]
+                + [pl.BlockSpec(g.shape, lambda s, *t: (0, 0)) for g in got]
+                + [any_spec] * len(self.news),
+                out_specs=[block, block, pl.BlockSpec((8, 128), lambda s, *t: (0, 0))],
+                scratch_shapes=[pltpu.VMEM((rows, columns), BF16), pltpu.SemaphoreType.DMA((1,))],
+            ),
+            out_shape=[shape(master.shape, F32), shape(momentum.shape, F32), shape((8, 128), F32)],
+            input_output_aliases={first + i: i for i in range(len(self.news))},
+            compiler_params=params(SCOPE, dimension_semantics=("arbitrary",)),
+            name="optimizer",
+        )(*scalars, *self.arrays, *self.news)
+        return (mark,)
+
+    def all(self):
+        while self.at < self.arrays[2].shape[0]:
+            self.step()
+        return self.news
 
 
 def layer_norm(values):
@@ -1210,7 +1238,7 @@
         lefts, rights = {}, {}
         for layer in reversed(range(LAYERS)):
             inner, normed, inv, qkv, mixed, attended, inner_mid, normed_mid, inv_mid, hidden, active = kept[layer][:11]
-            d_branch = yield from gather_tokens(d_branch)
+            d_branch = yield from gather_tokens(d_branch, 1 if layer == LAYERS - 1 else 2)
             d_hidden, keep, send = ring.work(mlp_back(d_branch, hidden, BIG * layer + 4))
             work = scatter_tokens(keep, send)
             flying = next(work)
@@ -1218,6 +1246,8 @@
                 weight_grads(BIG * layer + 4, [(inner_mid, d_hidden), (d_branch, active)], n_lat), ISSUED
             )
             ring.ready = BIG * layer + 4
+            if layer == LAYERS - 1:
+                ring.step((lefts[2 * layer + 1],))
             parts = finish(work, order(flying, (lefts[2 * layer + 1],) + ring.sent))
             grad, d_attended, rows = back(
                 parts,
@@ -1232,7 +1262,7 @@
                 small_at(layer, 3),
                 [ring.held],
             )
-            d_attended = yield from gather_tokens(d_attended)
+            d_attended = yield from gather_tokens(d_attended, 2)
             d_qkv, keep, send = ring.work(attention_back(d_attended, qkv, BIG * layer, n_lat))
             work = scatter_tokens(keep, send)
             flying = next(work)
@@ -1259,7 +1289,7 @@
 
     def cond_backward(rows, d_stream, edge_head, lefts, rights):
         mine = core_columns_sum(rows, core)
-        near, far = pick(*mine, chip), (yield x_flip(pick(*mine, chip, True)))
+        near, far = pick(*mine, chip), x_flip(pick(*mine, chip, True))
         own = [pick(near, far, chip).astype(BF16), pick(far, near, chip).astype(BF16)]
         if n_data == 8:
             first, *others = factor_rows(lefts, rights)
@@ -1290,19 +1320,12 @@
         grad_patch = lax.dot_general(noisy_own, d_stream, (((0,), (0,)), ((), ())), preferred_element_type=F32)
         sums = yield from own_columns_sum(jnp.concatenate([d_time_act, grad_patch, edge_head], 0), chip, core)
         ring.drain()
-        sums = yield from dp_sum(order(sums, ring.last()), n_data)
         if n_data != 8:
             factors = yield from dp_rows(jnp.stack(factor_rows(lefts, rights)), n_data)
         n_left = sum(v.shape[0] for v in lefts.values())
         a_rows = jnp.concatenate([factors[:, j * n_left : (j + 1) * n_left] for j in range(4)], 2).transpose(1, 0, 2)
         b_rows = factors[:, 4 * n_left : 4 * n_left + N_BIG].transpose(1, 0, 2)
-        d_time_act, edges = sums[:n_all], sums[n_all:]
-        unused, time_pull = jax.vjp(jax.nn.silu, time_one)
-        d_time_one = time_pull(d_time_act)[0].astype(BF16)
-        grad_time_one = lax.dot_general(
-            features, d_time_one, (((0,), (0,)), ((), ())), preferred_element_type=F32
-        )
-        return d_small, d_second, grad_class, grad_time_one, edges, (a_rows, b_rows)
+        return d_small, d_second, grad_class, sums, a_rows, b_rows
 
     def factor_rows(lefts, rights):
         a_rows = jnp.concatenate([lefts[g] for g in range(len(GROUPS))], 0)
@@ -1314,14 +1337,31 @@
             parts.append(jnp.pad(part, ((0, -len(part) % 32), (0, 0))))
         return parts
 
-    d_small, d_second, grad_class, grad_time_one, edges, (a_rows, b_rows) = drive(backward(), ring.step)
+    d_small, d_second, grad_class, sums, a_rows, b_rows = drive(backward(), ring.step)
+    a_all = jnp.concatenate([cond_in[None], time_act[None], a_rows], 0)
+    small_rows = jnp.where(
+        jnp.arange(SMALL_ROWS)[:, None, None] == TIME_AT, d_second[None], d_small.transpose(1, 0, 2)
+    )
+    b_all = jnp.concatenate([small_rows, b_rows], 0)
+    optimizer = Optimizer(
+        (big_slots, left_slots, right_slots), tab, a_all, b_all, master_bank, momentum_bank, ring.held, ring.last()
+    )
+    adding = dp_sum(order(sums, ring.last()), n_data)
+    flying = next(adding)
+    try:
+        while True:
+            (mark,) = optimizer.step(ISSUED[-2:-1]) or (jnp.zeros((8, 128), F32),)
+            flying = adding.send(flying + mark[:1, :1])
+    except StopIteration as end:
+        sums = end.value
+    master_new, momentum_new = optimizer.all()
+    d_time_act, edges = sums[:n_all], sums[n_all:]
+    unused, time_pull = jax.vjp(jax.nn.silu, time_one)
+    d_time_one = time_pull(d_time_act)[0].astype(BF16)
+    grad_time_one = lax.dot_general(
+        features, d_time_one, (((0,), (0,)), ((), ())), preferred_element_type=F32
+    )
     loss = edges[2 * n_patch, 0]
-    a_all = jnp.concatenate([cond_in[None], time_act[None], a_rows], 0)
-    small_rows = jnp.where(jnp.arange(SMALL_ROWS)[:, None, None] == TIME_AT, d_second[None], d_small.transpose(1, 0, 2))
-    b_all = jnp.concatenate([small_rows, b_rows], 0)
-    master_new, momentum_new = optimizer(
-        big_slots, left_slots, right_slots, tab, a_all, b_all, master_bank, momentum_bank, ring.held, ring.last()
-    )
     embed_new, first_new, second_new = update_tables(
         n_patch, early["bias_fix"], edges, grad_time_one, grad_class, embed_tables, embed_first, embed_second
     )

time: 678 us -> 660 us (0.973)
  the two profiles are of different devices: /device:TPU:0 before, /device:TPU:20 now
where the time goes in v2:
time: 660 us; the launch traced here: 652 us
  waiting for transfers between devices  230 us (35%)
  Pallas kernels  208 us (32%)
  starting transfers between devices  190 us (29%)
  other arithmetic  7.8 us (1%)
  local copies, waits for them, and re-layouts  7.35 us (1%)
    ppermute x144, waiting for transfers between devices, work(): lax.ppermute(sends[way], 'dp', self.perms[way])  177 us
    ppermute x144, starting transfers between devices, work(): lax.ppermute(sends[way], 'dp', self.perms[way])  152 us
    pallas_call x75, Pallas kernels, ring_step(): pl.pallas_call(kernel, out_shape=[pltpu.VMEM(held.shape, held.dtype)] + [...  123 us
    pallas_call x3, Pallas kernels, step(): pl.pallas_call(functools.partial(newton_kernel, len(got), base), grid_spe...  67.7 us
    ppermute x69, waiting for transfers between devices, flip(): got = lax.ppermute(values, axis, [(i, i ^ bit) for i in range(size)])  53.3 us
    ppermute x69, starting transfers between devices, flip(): got = lax.ppermute(values, axis, [(i, i ^ bit) for i in range(size)])  37.5 us
  transfers between devices with their start and end apart: 213, of which 133 were waited for; matrix products, arithmetic and copies ran while one was open for 1% of the time, Pallas kernels for 29%

profile of v2, /device:TPU:20, one launch (start us, length us, event | category | flops | bytes accessed | tf_op | source)
XLA Modules:
  0.0 652.1 jit_solution(14398927187143536719)
XLA Ops:
  2.1 6.4 plan.1
  19.6 3.5 own_weights.1.refs_0_
  30.0 3.2 collective-permute-done.3.refs_0_
  39.5 3.3 collective-permute-start.14
  42.8 2.4 collective-permute-done.9
  47.0 3.1 collective-permute-done.13
  58.4 2.7 collective-permute-done.18.refs_0_
  68.1 4.4 collective-permute-done.20
  78.6 3.1 collective-permute-done.27
  86.4 2.8 spread_step_modulations.1
  93.5 2.5 collective-permute-start.33
  100.0 2.8 collective-permute-done.35.refs_1_
  103.4 4.1 collective-permute-start.36
  112.6 2.1 collective-permute-start.45
  116.8 3.2 collective-permute-done.42
  126.7 4.0 collective-permute-done.43.refs_0_
  136.2 3.6 collective-permute-done.51.refs_1_
  142.9 2.6 collective-permute-done.49.refs_1_
  145.5 4.8 spread_step_attention.2
  156.2 3.4 collective-permute-done.59.refs_0_
  182.8 2.8 collective-permute-done.66.refs_1_
  188.6 2.6 collective-permute-done.72.refs_1_
  196.9 3.9 spread_step_mlp.2
  206.7 3.4 collective-permute-done.80.refs_0_
  216.6 2.4 collective-permute-done.83.refs_5_
  223.8 4.3 spread_step_attention.3
  236.1 3.1 collective-permute-done.95.refs_0_
  248.8 2.3 collective-permute-done.99.refs_0_
  254.4 2.2 collective-permute-done.97.refs_0_
  256.7 3.3 collective-permute-done.98.refs_1_
  263.1 2.6 collective-permute-done.104.refs_1_
  275.0 4.1 spread_step_mlp.3
  281.2 8.3 %collective-permute-done.111.far_ref = bf16[128,1024]{1,0:T(8,128)(2,1)S(1)} collective-permute-done((bf16[128,1024]{1,0:T(8,128)(2,1)S(1)}, bf16[128,1024]{1,0:T(8,128)(2,1)S(1)}, u32[]{:S(2)}, u32[]{:S(2)}) %collective-permute-start.111) | collective-permute-done | bytes 262176 | tf_op jit(solution)/shard_map/ppermute | solution.py:135
  290.8 7.2 %collective-permute-done.113.refs_3_.refs_7_ = bf16[128,1024]{1,0:T(8,128)(2,1)S(1)} collective-permute-done((bf16[128,1024]{1,0:T(8,128)(2,1)S(1)}, bf16[128,1024]{1,0:T(8,128)(2,1)S(1)}, u32[]{:S(2)}, u32[]{:S(2)}) %collective-permute-start.113) | collective-permute-done | bytes 262176 | tf_op jit(solution)/shard_map/ppermute | solution.py:135
  299.6 4.5 layer__mlp_back.1
  306.8 4.5 layer__weight_grads.1
  317.3 3.0 collective-permute-done.119.refs_0_
  322.6 3.3 collective-permute-done.121.refs_0_
  329.5 7.1 %reduce_step_attention_back.2 = (bf16[36,1024,256]{2,1,0:T(8,128)(2,1)S(1)}, bf16[512,256]{1,0:T(8,128)(2,1)S(1)}, bf16[512,256]{1,0:T(8,128)(2,1)S(1)}, bf16[3,...) custom-call(s32[36,4]{1,0:T(8,128)S(1)} %bitcast.173, ...), custom_call_target="tpu_custom_call", output_to_operand_aliasing={{0}: (3, {})} | custom-call | tf_op jit(solution)/shard_map/reduce_step_attention_back/pallas_call | solution.py:383
  340.4 2.9 reduce_step_weight_grads.3
  354.9 3.9 collective-permute-done.130.refs_0_
  361.3 5.0 reduce_step_mlp_back.1
  371.7 4.5 reduce_step_weight_grads.4
  386.7 3.6 collective-permute-done.147.refs_0_
  393.5 7.1 %reduce_step_attention_back.3 = (bf16[36,1024,256]{2,1,0:T(8,128)(2,1)S(1)}, bf16[512,256]{1,0:T(8,128)(2,1)S(1)}, bf16[512,256]{1,0:T(8,128)(2,1)S(1)}, bf16[3,...) custom-call(s32[36,4]{1,0:T(8,128)S(1)} %bitcast.181, ...), custom_call_target="tpu_custom_call", output_to_operand_aliasing={{0}: (3, {})} | custom-call | tf_op jit(solution)/shard_map/reduce_step_attention_back/pallas_call | solution.py:383
  405.2 2.9 reduce_step_weight_grads.5
  417.2 2.5 collective-permute-done.157
  425.8 5.3 collective-permute-done.158.refs_0_
  435.3 2.4 collective-permute-done.164.refs_0_
  442.0 2.4 collective-permute-done.162.refs_0_
  448.7 2.4 collective-permute-done.168.refs_0_
  455.2 2.5 collective-permute-done.166.refs_0_
  462.0 2.4 collective-permute-done.172.refs_0_
  468.7 2.3 collective-permute-done.170.refs_0_
  484.5 2.9 reduce_step_cond_back.1
  491.9 2.8 collective-permute-done.181
  501.0 4.0 collective-permute-done.182.refs_0_
  559.9 3.3 collective-permute-done.205
  566.9 4.7 collective-permute-done.208.refs_1_
  573.6 25.0 %optimizer.3 = (f32[8,1024,256]{2,1,0:T(8,128)}, f32[8,1024,256]{2,1,0:T(8,128)}, f32[8,128]{1,0:T(8,128)S(1)}) custom-call(s32[8]{0:T(128)S(1)} %get-tuple-element.958.big_ref, s32[8]{0:T(128)S(1)} %get-tuple-element.1034.left_ref, s32[8]{0:T(128)S(1)} %get-tuple-element.1033.right_ref, s32[36,4]{1,0:T(8,128)S(1)} %bitcast.206, ...), custom_call_target="tpu_custom_call" | custom-call | tf_op jit(solution)/shard_map/optimizer/pallas_call | solution.py:857
  600.1 24.9 %optimizer.4 = (f32[8,1024,256]{2,1,0:T(8,128)}, f32[8,1024,256]{2,1,0:T(8,128)}, f32[8,128]{1,0:T(8,128)S(1)}) custom-call(s32[8]{0:T(128)S(1)} %get-tuple-element.958.big_ref, s32[8]{0:T(128)S(1)} %get-tuple-element.1034.left_ref, s32[8]{0:T(128)S(1)} %get-tuple-element.1033.right_ref, ...), custom_call_target="tpu_custom_call", output_to_operand_aliasing={{0}: (13, {}), {1}: (14, {})} | custom-call | tf_op jit(solution)/shard_map/optimizer/pallas_call | solution.py:857
  626.2 2.5 collective-permute-start.212
  629.4 17.8 %optimizer.5 = (f32[8,1024,256]{2,1,0:T(8,128)}, f32[8,1024,256]{2,1,0:T(8,128)}, f32[8,128]{1,0:T(8,128)S(1)}) custom-call(s32[8]{0:T(128)S(1)} %get-tuple-element.958.big_ref, s32[8]{0:T(128)S(1)} %get-tuple-element.1034.left_ref, s32[8]{0:T(128)S(1)} %get-tuple-element.1033.right_ref, ...), custom_call_target="tpu_custom_call", output_to_operand_aliasing={{0}: (13, {}), {1}: (14, {})} | custom-call | tf_op jit(solution)/shard_map/optimizer/pallas_call | solution.py:857
  649.2 2.7 update_tables.1
  (651 shorter events, 360.3 us)
Async XLA Ops:
  27.8 10.7 %collective-permute-start.7 = (bf16[512,256]{1,0:T(8,128)(2,1)S(1)}, bf16[512,256]{1,0:T(8,128)(2,1)S(1)}, u32[]{:S(2)}, u32[]{:S(2)}) collective-permute-start(bf16[512,256]{1,0:T(8,128)(2,1)S(1)} %get-tuple-element.502), channel_id=1, source_target_pairs={{0,8},{8,16},{16,24},{24,28},{28,20},{20,12},{12,4},{4,0},{1,9},{9... | collective-permute-start | bytes 786440 | tf_op jit(solution)/shard_map/ppermute | solution.py:436
  27.9 10.6 %collective-permute-start.8 = (bf16[512,256]{1,0:T(8,128)(2,1)S(1)}, bf16[512,256]{1,0:T(8,128)(2,1)S(1)}, u32[]{:S(2)}, u32[]{:S(2)}) collective-permute-start(bf16[512,256]{1,0:T(8,128)(2,1)S(1)} %get-tuple-element.503), channel_id=1, source_target_pairs={{8,0},{16,8},{24,16},{28,24},{20,28},{12,20},{4,12},{0,4},{9,1},{1... | collective-permute-start | bytes 786440 | tf_op jit(solution)/shard_map/ppermute | solution.py:436
  39.5 11.5 %collective-permute-start.14 = (bf16[512,256]{1,0:T(8,128)(2,1)S(1)}, bf16[512,256]{1,0:T(8,128)(2,1)S(1)}, u32[]{:S(2)}, u32[]{:S(2)}) collective-permute-start(bf16[512,256]{1,0:T(8,128)(2,1)S(1)} %get-tuple-element.515), channel_id=1, source_target_pairs={{0,8},{8,16},{16,24},{24,28},{28,20},{20,12},{12,4},{4,0},{1,9},{9... | collective-permute-start | bytes 786440 | tf_op jit(solution)/shard_map/ppermute | solution.py:436
  56.3 10.4 %collective-permute-start.21 = (bf16[512,256]{1,0:T(8,128)(2,1)S(1)}, bf16[512,256]{1,0:T(8,128)(2,1)S(1)}, u32[]{:S(2)}, u32[]{:S(2)}) collective-permute-start(bf16[512,256]{1,0:T(8,128)(2,1)S(1)} %get-tuple-element.528), channel_id=1, source_target_pairs={{0,8},{8,16},{16,24},{24,28},{28,20},{20,12},{12,4},{4,0},{1,9},{9... | collective-permute-start | bytes 786440 | tf_op jit(solution)/shard_map/ppermute | solution.py:436
  57.8 10.3 %collective-permute-start.22 = (bf16[512,256]{1,0:T(8,128)(2,1)S(1)}, bf16[512,256]{1,0:T(8,128)(2,1)S(1)}, u32[]{:S(2)}, u32[]{:S(2)}) collective-permute-start(bf16[512,256]{1,0:T(8,128)(2,1)S(1)} %get-tuple-element.529), channel_id=1, source_target_pairs={{8,0},{16,8},{24,16},{28,24},{20,28},{12,20},{4,12},{0,4},{9,1},{1... | collective-permute-start | bytes 786440 | tf_op jit(solution)/shard_map/ppermute | solution.py:436
  63.5 13.7 %collective-permute-start.24 = (bf16[512,256]{1,0:T(8,128)(2,1)S(1)}, bf16[512,256]{1,0:T(8,128)(2,1)S(1)}, u32[]{:S(2)}, u32[]{:S(2)}) collective-permute-start(bf16[512,256]{1,0:T(8,128)(2,1)S(1)} %get-tuple-element.533), channel_id=1, source_target_pairs={{0,8},{8,16},{16,24},{24,28},{28,20},{20,12},{12,4},{4,0},{1,9},{9... | collective-permute-start | bytes 786440 | tf_op jit(solution)/shard_map/ppermute | solution.py:436
  64.6 12.6 %collective-permute-start.25 = (bf16[512,256]{1,0:T(8,128)(2,1)S(1)}, bf16[512,256]{1,0:T(8,128)(2,1)S(1)}, u32[]{:S(2)}, u32[]{:S(2)}) collective-permute-start(bf16[512,256]{1,0:T(8,128)(2,1)S(1)} %get-tuple-element.534), channel_id=1, source_target_pairs={{8,0},{16,8},{24,16},{28,24},{20,28},{12,20},{4,12},{0,4},{9,1},{1... | collective-permute-start | bytes 786440 | tf_op jit(solution)/shard_map/ppermute | solution.py:436
  89.1 10.9 %collective-permute-start.34 = (bf16[512,256]{1,0:T(8,128)(2,1)S(1)}, bf16[512,256]{1,0:T(8,128)(2,1)S(1)}, u32[]{:S(2)}, u32[]{:S(2)}) collective-permute-start(bf16[512,256]{1,0:T(8,128)(2,1)S(1)} %get-tuple-element.556), channel_id=1, source_target_pairs={{0,8},{8,16},{16,24},{24,28},{28,20},{20,12},{12,4},{4,0},{1,9},{9... | collective-permute-start | bytes 786440 | tf_op jit(solution)/shard_map/ppermute | solution.py:436
  91.0 11.8 %collective-permute-start.35 = (bf16[512,256]{1,0:T(8,128)(2,1)S(1)}, bf16[512,256]{1,0:T(8,128)(2,1)S(1)}, u32[]{:S(2)}, u32[]{:S(2)}) collective-permute-start(bf16[512,256]{1,0:T(8,128)(2,1)S(1)} %get-tuple-element.557), channel_id=1, source_target_pairs={{8,0},{16,8},{24,16},{28,24},{20,28},{12,20},{4,12},{0,4},{9,1},{1... | collective-permute-start | bytes 786440 | tf_op jit(solution)/shard_map/ppermute | solution.py:436
  93.5 9.9 %collective-permute-start.33 = (f32[16,8,256]{2,0,1:T(8,128)S(1)}, f32[16,8,256]{2,0,1:T(8,128)S(1)}, u32[]{:S(2)}, u32[]{:S(2)}) collective-permute-start(f32[16,8,256]{2,0,1:T(8,128)S(1)} %slice_select_fusion), channel_id=1, source_target_pairs={{0,16},{4,20},{8,24},{12,28},{16,0},{20,4},{24,8},{28,12},{1,17},{... | collective-permute-start | bytes 393224 | tf_op jit(solution)/shard_map/ppermute | solution.py:135
  96.9 13.6 %collective-permute-start.37 = (bf16[512,256]{1,0:T(8,128)(2,1)S(1)}, bf16[512,256]{1,0:T(8,128)(2,1)S(1)}, u32[]{:S(2)}, u32[]{:S(2)}) collective-permute-start(bf16[512,256]{1,0:T(8,128)(2,1)S(1)} %get-tuple-element.554), channel_id=1, source_target_pairs={{0,8},{8,16},{16,24},{24,28},{28,20},{20,12},{12,4},{4,0},{1,9},{9... | collective-permute-start | bytes 786440 | tf_op jit(solution)/shard_map/ppermute | solution.py:436
  97.4 14.1 %collective-permute-start.38 = (bf16[512,256]{1,0:T(8,128)(2,1)S(1)}, bf16[512,256]{1,0:T(8,128)(2,1)S(1)}, u32[]{:S(2)}, u32[]{:S(2)}) collective-permute-start(bf16[512,256]{1,0:T(8,128)(2,1)S(1)} %get-tuple-element.555), channel_id=1, source_target_pairs={{8,0},{16,8},{24,16},{28,24},{20,28},{12,20},{4,12},{0,4},{9,1},{1... | collective-permute-start | bytes 786440 | tf_op jit(solution)/shard_map/ppermute | solution.py:436
  122.1 9.8 %collective-permute-start.44 = (bf16[512,256]{1,0:T(8,128)(2,1)S(1)}, bf16[512,256]{1,0:T(8,128)(2,1)S(1)}, u32[]{:S(2)}, u32[]{:S(2)}) collective-permute-start(bf16[512,256]{1,0:T(8,128)(2,1)S(1)} %get-tuple-element.572), channel_id=1, source_target_pairs={{8,0},{16,8},{24,16},{28,24},{20,28},{12,20},{4,12},{0,4},{9,1},{1... | collective-permute-start | bytes 786440 | tf_op jit(solution)/shard_map/ppermute | solution.py:436
  124.0 10.0 %collective-permute-start.53 = (bf16[128,1024]{1,0:T(8,128)(2,1)S(1)}, bf16[128,1024]{1,0:T(8,128)(2,1)S(1)}, u32[]{:S(2)}, u32[]{:S(2)}) collective-permute-start(bf16[128,1024]{1,0:T(8,128)(2,1)S(1)} %get-tuple-element.577.refs_3_), channel_id=1, source_target_pairs={{0,2},{1,3},{2,0},{3,1},{4,6},{5,7},{6,4},{7,5},{8,10},{9,11},{10,... | collective-permute-start | bytes 786440 | tf_op jit(solution)/shard_map/ppermute | solution.py:135
  124.6 10.3 %collective-permute-start.52 = (bf16[128,1024]{1,0:T(8,128)(2,1)S(1)}, bf16[128,1024]{1,0:T(8,128)(2,1)S(1)}, u32[]{:S(2)}, u32[]{:S(2)}) collective-permute-start(bf16[128,1024]{1,0:T(8,128)(2,1)S(1)} %get-tuple-element.577.refs_3_), channel_id=1, source_target_pairs={{0,1},{1,0},{2,3},{3,2},{4,5},{5,4},{6,7},{7,6},{8,9},{9,8},{10,11... | collective-permute-start | bytes 786440 | tf_op jit(solution)/shard_map/ppermute | solution.py:135
  125.6 10.7 %collective-permute-start.50 = (bf16[512,256]{1,0:T(8,128)(2,1)S(1)}, bf16[512,256]{1,0:T(8,128)(2,1)S(1)}, u32[]{:S(2)}, u32[]{:S(2)}) collective-permute-start(bf16[512,256]{1,0:T(8,128)(2,1)S(1)} %get-tuple-element.583), channel_id=1, source_target_pairs={{0,8},{8,16},{16,24},{24,28},{28,20},{20,12},{12,4},{4,0},{1,9},{9... | collective-permute-start | bytes 786440 | tf_op jit(solution)/shard_map/ppermute | solution.py:436
  132.8 10.1 %collective-permute-start.48 = (bf16[512,256]{1,0:T(8,128)(2,1)S(1)}, bf16[512,256]{1,0:T(8,128)(2,1)S(1)}, u32[]{:S(2)}, u32[]{:S(2)}) collective-permute-start(bf16[512,256]{1,0:T(8,128)(2,1)S(1)} %get-tuple-element.581), channel_id=1, source_target_pairs={{0,8},{8,16},{16,24},{24,28},{28,20},{20,12},{12,4},{4,0},{1,9},{9... | collective-permute-start | bytes 786440 | tf_op jit(solution)/shard_map/ppermute | solution.py:436
  134.0 11.5 %collective-permute-start.49 = (bf16[512,256]{1,0:T(8,128)(2,1)S(1)}, bf16[512,256]{1,0:T(8,128)(2,1)S(1)}, u32[]{:S(2)}, u32[]{:S(2)}) collective-permute-start(bf16[512,256]{1,0:T(8,128)(2,1)S(1)} %get-tuple-element.582), channel_id=1, source_target_pairs={{8,0},{16,8},{24,16},{28,24},{20,28},{12,20},{4,12},{0,4},{9,1},{1... | collective-permute-start | bytes 786440 | tf_op jit(solution)/shard_map/ppermute | solution.py:436
  134.9 10.6 %collective-permute-start.54 = (bf16[128,1024]{1,0:T(8,128)(2,1)S(1)}, bf16[128,1024]{1,0:T(8,128)(2,1)S(1)}, u32[]{:S(2)}, u32[]{:S(2)}) collective-permute-start(bf16[128,1024]{1,0:T(8,128)(2,1)S(1)} %collective-permute-done.53.refs_5_), channel_id=1, source_target_pairs={{0,1},{1,0},{2,3},{3,2},{4,5},{5,4},{6,7},{7,6},{8,9},{9,8},{10,11... | collective-permute-start | bytes 786440 | tf_op jit(solution)/shard_map/ppermute | solution.py:135
  154.1 11.1 %collective-permute-start.63 = (bf16[512,256]{1,0:T(8,128)(2,1)S(1)}, bf16[512,256]{1,0:T(8,128)(2,1)S(1)}, u32[]{:S(2)}, u32[]{:S(2)}) collective-permute-start(bf16[512,256]{1,0:T(8,128)(2,1)S(1)} %get-tuple-element.599), channel_id=1, source_target_pairs={{0,8},{8,16},{16,24},{24,28},{28,20},{20,12},{12,4},{4,0},{1,9},{9... | collective-permute-start | bytes 786440 | tf_op jit(solution)/shard_map/ppermute | solution.py:436
  155.3 11.0 %collective-permute-start.64 = (bf16[512,256]{1,0:T(8,128)(2,1)S(1)}, bf16[512,256]{1,0:T(8,128)(2,1)S(1)}, u32[]{:S(2)}, u32[]{:S(2)}) collective-permute-start(bf16[512,256]{1,0:T(8,128)(2,1)S(1)} %get-tuple-element.600), channel_id=1, source_target_pairs={{8,0},{16,8},{24,16},{28,24},{20,28},{12,20},{4,12},{0,4},{9,1},{1... | collective-permute-start | bytes 786440 | tf_op jit(solution)/shard_map/ppermute | solution.py:436
  169.3 10.4 %collective-permute-start.74 = (bf16[128,1024]{1,0:T(8,128)(2,1)S(1)}, bf16[128,1024]{1,0:T(8,128)(2,1)S(1)}, u32[]{:S(2)}, u32[]{:S(2)}) collective-permute-start(bf16[128,1024]{1,0:T(8,128)(2,1)S(1)} %get-tuple-element.605.refs_3_), channel_id=1, source_target_pairs={{0,2},{1,3},{2,0},{3,1},{4,6},{5,7},{6,4},{7,5},{8,10},{9,11},{10,... | collective-permute-start | bytes 786440 | tf_op jit(solution)/shard_map/ppermute | solution.py:135
  178.6 10.0 %collective-permute-start.71 = (bf16[512,256]{1,0:T(8,128)(2,1)S(1)}, bf16[512,256]{1,0:T(8,128)(2,1)S(1)}, u32[]{:S(2)}, u32[]{:S(2)}) collective-permute-start(bf16[512,256]{1,0:T(8,128)(2,1)S(1)} %get-tuple-element.620), channel_id=1, source_target_pairs={{0,8},{8,16},{16,24},{24,28},{28,20},{20,12},{12,4},{4,0},{1,9},{9... | collective-permute-start | bytes 786440 | tf_op jit(solution)/shard_map/ppermute | solution.py:436
  179.8 11.5 %collective-permute-start.72 = (bf16[512,256]{1,0:T(8,128)(2,1)S(1)}, bf16[512,256]{1,0:T(8,128)(2,1)S(1)}, u32[]{:S(2)}, u32[]{:S(2)}) collective-permute-start(bf16[512,256]{1,0:T(8,128)(2,1)S(1)} %get-tuple-element.621), channel_id=1, source_target_pairs={{8,0},{16,8},{24,16},{28,24},{20,28},{12,20},{4,12},{0,4},{9,1},{1... | collective-permute-start | bytes 786440 | tf_op jit(solution)/shard_map/ppermute | solution.py:436
  180.7 13.6 %collective-permute-start.75 = (bf16[128,1024]{1,0:T(8,128)(2,1)S(1)}, bf16[128,1024]{1,0:T(8,128)(2,1)S(1)}, u32[]{:S(2)}, u32[]{:S(2)}) collective-permute-start(bf16[128,1024]{1,0:T(8,128)(2,1)S(1)} %collective-permute-done.74.refs_5_), channel_id=1, source_target_pairs={{0,1},{1,0},{2,3},{3,2},{4,5},{5,4},{6,7},{7,6},{8,9},{9,8},{10,11... | collective-permute-start | bytes 786440 | tf_op jit(solution)/shard_map/ppermute | solution.py:135
  204.6 10.7 %collective-permute-start.84 = (bf16[512,256]{1,0:T(8,128)(2,1)S(1)}, bf16[512,256]{1,0:T(8,128)(2,1)S(1)}, u32[]{:S(2)}, u32[]{:S(2)}) collective-permute-start(bf16[512,256]{1,0:T(8,128)(2,1)S(1)} %get-tuple-element.636), channel_id=1, source_target_pairs={{0,8},{8,16},{16,24},{24,28},{28,20},{20,12},{12,4},{4,0},{1,9},{9... | collective-permute-start | bytes 786440 | tf_op jit(solution)/shard_map/ppermute | solution.py:436
  206.3 10.3 %collective-permute-start.85 = (bf16[512,256]{1,0:T(8,128)(2,1)S(1)}, bf16[512,256]{1,0:T(8,128)(2,1)S(1)}, u32[]{:S(2)}, u32[]{:S(2)}) collective-permute-start(bf16[512,256]{1,0:T(8,128)(2,1)S(1)} %get-tuple-element.637), channel_id=1, source_target_pairs={{8,0},{16,8},{24,16},{28,24},{20,28},{12,20},{4,12},{0,4},{9,1},{1... | collective-permute-start | bytes 786440 | tf_op jit(solution)/shard_map/ppermute | solution.py:436
  234.0 10.8 %collective-permute-start.92 = (bf16[512,256]{1,0:T(8,128)(2,1)S(1)}, bf16[512,256]{1,0:T(8,128)(2,1)S(1)}, u32[]{:S(2)}, u32[]{:S(2)}) collective-permute-start(bf16[512,256]{1,0:T(8,128)(2,1)S(1)} %get-tuple-element.661), channel_id=1, source_target_pairs={{0,8},{8,16},{16,24},{24,28},{28,20},{20,12},{12,4},{4,0},{1,9},{9... | collective-permute-start | bytes 786440 | tf_op jit(solution)/shard_map/ppermute | solution.py:436
  235.5 11.0 %collective-permute-start.93 = (bf16[512,256]{1,0:T(8,128)(2,1)S(1)}, bf16[512,256]{1,0:T(8,128)(2,1)S(1)}, u32[]{:S(2)}, u32[]{:S(2)}) collective-permute-start(bf16[512,256]{1,0:T(8,128)(2,1)S(1)} %get-tuple-element.662), channel_id=1, source_target_pairs={{8,0},{16,8},{24,16},{28,24},{20,28},{12,20},{4,12},{0,4},{9,1},{1... | collective-permute-start | bytes 786440 | tf_op jit(solution)/shard_map/ppermute | solution.py:436
  244.2 9.9 %collective-permute-start.108 = (bf16[128,1024]{1,0:T(8,128)(2,1)S(1)}, bf16[128,1024]{1,0:T(8,128)(2,1)S(1)}, u32[]{:S(2)}, u32[]{:S(2)}) collective-permute-start(bf16[128,1024]{1,0:T(8,128)(2,1)S(1)} %get-tuple-element.667.refs_5_.refs_1_), channel_id=1, source_target_pairs={{0,2},{1,3},{2,0},{3,1},{4,6},{5,7},{6,4},{7,5},{8,10},{9,11},{10,... | collective-permute-start | bytes 786440 | tf_op jit(solution)/shard_map/ppermute | solution.py:135
  244.8 9.7 %collective-permute-start.107 = (bf16[128,1024]{1,0:T(8,128)(2,1)S(1)}, bf16[128,1024]{1,0:T(8,128)(2,1)S(1)}, u32[]{:S(2)}, u32[]{:S(2)}) collective-permute-start(bf16[128,1024]{1,0:T(8,128)(2,1)S(1)} %get-tuple-element.667.refs_5_.refs_1_), channel_id=1, source_target_pairs={{0,1},{1,0},{2,3},{3,2},{4,5},{5,4},{6,7},{7,6},{8,9},{9,8},{10,11... | collective-permute-start | bytes 786440 | tf_op jit(solution)/shard_map/ppermute | solution.py:135
  252.3 10.7 %collective-permute-start.103 = (bf16[512,256]{1,0:T(8,128)(2,1)S(1)}, bf16[512,256]{1,0:T(8,128)(2,1)S(1)}, u32[]{:S(2)}, u32[]{:S(2)}) collective-permute-start(bf16[512,256]{1,0:T(8,128)(2,1)S(1)} %get-tuple-element.679), channel_id=1, source_target_pairs={{0,8},{8,16},{16,24},{24,28},{28,20},{20,12},{12,4},{4,0},{1,9},{9... | collective-permute-start | bytes 786440 | tf_op jit(solution)/shard_map/ppermute | solution.py:436
  254.1 11.6 %collective-permute-start.104 = (bf16[512,256]{1,0:T(8,128)(2,1)S(1)}, bf16[512,256]{1,0:T(8,128)(2,1)S(1)}, u32[]{:S(2)}, u32[]{:S(2)}) collective-permute-start(bf16[512,256]{1,0:T(8,128)(2,1)S(1)} %get-tuple-element.680), channel_id=1, source_target_pairs={{8,0},{16,8},{24,16},{28,24},{20,28},{12,20},{4,12},{0,4},{9,1},{1... | collective-permute-start | bytes 786440 | tf_op jit(solution)/shard_map/ppermute | solution.py:436
  254.4 14.2 %collective-permute-start.109 = (bf16[128,1024]{1,0:T(8,128)(2,1)S(1)}, bf16[128,1024]{1,0:T(8,128)(2,1)S(1)}, u32[]{:S(2)}, u32[]{:S(2)}) collective-permute-start(bf16[128,1024]{1,0:T(8,128)(2,1)S(1)} %collective-permute-done.108.refs_7_.refs_3_), channel_id=1, source_target_pairs={{0,1},{1,0},{2,3},{3,2},{4,5},{5,4},{6,7},{7,6},{8,9},{9,8},{10,11... | collective-permute-start | bytes 786440 | tf_op jit(solution)/shard_map/ppermute | solution.py:135
  403.8 9.7 %collective-permute-start.153 = (bf16[128,1024]{1,0:T(8,128)(2,1)S(1)}, bf16[128,1024]{1,0:T(8,128)(2,1)S(1)}, u32[]{:S(2)}, u32[]{:S(2)}) collective-permute-start(bf16[128,1024]{1,0:T(8,128)(2,1)S(1)} %fusion.8), channel_id=1, source_target_pairs={{0,2},{1,3},{2,0},{3,1},{4,6},{5,7},{6,4},{7,5},{8,10},{9,11},{10,... | collective-permute-start | bytes 786440 | tf_op jit(solution)/shard_map/ppermute | solution.py:135
  411.3 11.4 %collective-permute-start.160 = (bf16[512,256]{1,0:T(8,128)(2,1)S(1)}, bf16[512,256]{1,0:T(8,128)(2,1)S(1)}, u32[]{:S(2)}, u32[]{:S(2)}) collective-permute-start(bf16[512,256]{1,0:T(8,128)(2,1)S(1)} %get-tuple-element.811), channel_id=1, source_target_pairs={{8,0},{16,8},{24,16},{28,24},{20,28},{12,20},{4,12},{0,4},{9,1},{1... | collective-permute-start | bytes 786440 | tf_op jit(solution)/shard_map/ppermute | solution.py:510
  412.6 10.2 %collective-permute-start.161 = (bf16[512,256]{1,0:T(8,128)(2,1)S(1)}, bf16[512,256]{1,0:T(8,128)(2,1)S(1)}, u32[]{:S(2)}, u32[]{:S(2)}) collective-permute-start(bf16[512,256]{1,0:T(8,128)(2,1)S(1)} %get-tuple-element.812), channel_id=1, source_target_pairs={{0,8},{8,16},{16,24},{24,28},{28,20},{20,12},{12,4},{4,0},{1,9},{9... | collective-permute-start | bytes 786440 | tf_op jit(solution)/shard_map/ppermute | solution.py:510
  420.7 10.4 %collective-permute-start.158 = (bf16[608,256]{1,0:T(8,128)(2,1)S(1)}, bf16[608,256]{1,0:T(8,128)(2,1)S(1)}, u32[]{:S(2)}, u32[]{:S(2)}) collective-permute-start(bf16[608,256]{1,0:T(8,128)(2,1)S(1)} %get-tuple-element.825), channel_id=1, source_target_pairs={{8,0},{16,8},{24,16},{28,24},{20,28},{12,20},{4,12},{0,4},{9,1},{1... | collective-permute-start | bytes 933896 | tf_op jit(solution)/shard_map/ppermute | solution.py:510
  421.9 10.3 %collective-permute-start.159 = (bf16[608,256]{1,0:T(8,128)(2,1)S(1)}, bf16[608,256]{1,0:T(8,128)(2,1)S(1)}, u32[]{:S(2)}, u32[]{:S(2)}) collective-permute-start(bf16[608,256]{1,0:T(8,128)(2,1)S(1)} %get-tuple-element.826), channel_id=1, source_target_pairs={{0,8},{8,16},{16,24},{24,28},{28,20},{20,12},{12,4},{4,0},{1,9},{9... | collective-permute-start | bytes 933896 | tf_op jit(solution)/shard_map/ppermute | solution.py:510
  423.7 14.0 %collective-permute-start.164 = (bf16[608,256]{1,0:T(8,128)(2,1)S(1)}, bf16[608,256]{1,0:T(8,128)(2,1)S(1)}, u32[]{:S(2)}, u32[]{:S(2)}) collective-permute-start(bf16[608,256]{1,0:T(8,128)(2,1)S(1)} %get-tuple-element.831), channel_id=1, source_target_pairs={{8,0},{16,8},{24,16},{28,24},{20,28},{12,20},{4,12},{0,4},{9,1},{1... | collective-permute-start | bytes 933896 | tf_op jit(solution)/shard_map/ppermute | solution.py:510
  425.0 13.9 %collective-permute-start.165 = (bf16[608,256]{1,0:T(8,128)(2,1)S(1)}, bf16[608,256]{1,0:T(8,128)(2,1)S(1)}, u32[]{:S(2)}, u32[]{:S(2)}) collective-permute-start(bf16[608,256]{1,0:T(8,128)(2,1)S(1)} %get-tuple-element.832), channel_id=1, source_target_pairs={{0,8},{8,16},{16,24},{24,28},{28,20},{20,12},{12,4},{4,0},{1,9},{9... | collective-permute-start | bytes 933896 | tf_op jit(solution)/shard_map/ppermute | solution.py:510
  433.2 11.2 %collective-permute-start.162 = (bf16[608,256]{1,0:T(8,128)(2,1)S(1)}, bf16[608,256]{1,0:T(8,128)(2,1)S(1)}, u32[]{:S(2)}, u32[]{:S(2)}) collective-permute-start(bf16[608,256]{1,0:T(8,128)(2,1)S(1)} %get-tuple-element.829), channel_id=1, source_target_pairs={{8,0},{16,8},{24,16},{28,24},{20,28},{12,20},{4,12},{0,4},{9,1},{1... | collective-permute-start | bytes 933896 | tf_op jit(solution)/shard_map/ppermute | solution.py:510
  434.4 11.2 %collective-permute-start.163 = (bf16[608,256]{1,0:T(8,128)(2,1)S(1)}, bf16[608,256]{1,0:T(8,128)(2,1)S(1)}, u32[]{:S(2)}, u32[]{:S(2)}) collective-permute-start(bf16[608,256]{1,0:T(8,128)(2,1)S(1)} %get-tuple-element.830), channel_id=1, source_target_pairs={{0,8},{8,16},{16,24},{24,28},{28,20},{20,12},{12,4},{4,0},{1,9},{9... | collective-permute-start | bytes 933896 | tf_op jit(solution)/shard_map/ppermute | solution.py:510
  439.9 11.1 %collective-permute-start.168 = (bf16[608,256]{1,0:T(8,128)(2,1)S(1)}, bf16[608,256]{1,0:T(8,128)(2,1)S(1)}, u32[]{:S(2)}, u32[]{:S(2)}) collective-permute-start(bf16[608,256]{1,0:T(8,128)(2,1)S(1)} %get-tuple-element.837), channel_id=1, source_target_pairs={{8,0},{16,8},{24,16},{28,24},{20,28},{12,20},{4,12},{0,4},{9,1},{1... | collective-permute-start | bytes 933896 | tf_op jit(solution)/shard_map/ppermute | solution.py:510
  441.0 11.2 %collective-permute-start.169 = (bf16[608,256]{1,0:T(8,128)(2,1)S(1)}, bf16[608,256]{1,0:T(8,128)(2,1)S(1)}, u32[]{:S(2)}, u32[]{:S(2)}) collective-permute-start(bf16[608,256]{1,0:T(8,128)(2,1)S(1)} %get-tuple-element.838), channel_id=1, source_target_pairs={{0,8},{8,16},{16,24},{24,28},{28,20},{20,12},{12,4},{4,0},{1,9},{9... | collective-permute-start | bytes 933896 | tf_op jit(solution)/shard_map/ppermute | solution.py:510
  446.6 11.1 %collective-permute-start.166 = (bf16[608,256]{1,0:T(8,128)(2,1)S(1)}, bf16[608,256]{1,0:T(8,128)(2,1)S(1)}, u32[]{:S(2)}, u32[]{:S(2)}) collective-permute-start(bf16[608,256]{1,0:T(8,128)(2,1)S(1)} %get-tuple-element.835), channel_id=1, source_target_pairs={{8,0},{16,8},{24,16},{28,24},{20,28},{12,20},{4,12},{0,4},{9,1},{1... | collective-permute-start | bytes 933896 | tf_op jit(solution)/shard_map/ppermute | solution.py:510
  447.8 11.1 %collective-permute-start.167 = (bf16[608,256]{1,0:T(8,128)(2,1)S(1)}, bf16[608,256]{1,0:T(8,128)(2,1)S(1)}, u32[]{:S(2)}, u32[]{:S(2)}) collective-permute-start(bf16[608,256]{1,0:T(8,128)(2,1)S(1)} %get-tuple-element.836), channel_id=1, source_target_pairs={{0,8},{8,16},{16,24},{24,28},{28,20},{20,12},{12,4},{4,0},{1,9},{9... | collective-permute-start | bytes 933896 | tf_op jit(solution)/shard_map/ppermute | solution.py:510
  453.1 11.2 %collective-permute-start.172 = (bf16[608,256]{1,0:T(8,128)(2,1)S(1)}, bf16[608,256]{1,0:T(8,128)(2,1)S(1)}, u32[]{:S(2)}, u32[]{:S(2)}) collective-permute-start(bf16[608,256]{1,0:T(8,128)(2,1)S(1)} %get-tuple-element.843), channel_id=1, source_target_pairs={{8,0},{16,8},{24,16},{28,24},{20,28},{12,20},{4,12},{0,4},{9,1},{1... | collective-permute-start | bytes 933896 | tf_op jit(solution)/shard_map/ppermute | solution.py:510
  454.4 11.1 %collective-permute-start.173 = (bf16[608,256]{1,0:T(8,128)(2,1)S(1)}, bf16[608,256]{1,0:T(8,128)(2,1)S(1)}, u32[]{:S(2)}, u32[]{:S(2)}) collective-permute-start(bf16[608,256]{1,0:T(8,128)(2,1)S(1)} %get-tuple-element.844), channel_id=1, source_target_pairs={{0,8},{8,16},{16,24},{24,28},{28,20},{20,12},{12,4},{4,0},{1,9},{9... | collective-permute-start | bytes 933896 | tf_op jit(solution)/shard_map/ppermute | solution.py:510
  459.9 11.1 %collective-permute-start.170 = (bf16[608,256]{1,0:T(8,128)(2,1)S(1)}, bf16[608,256]{1,0:T(8,128)(2,1)S(1)}, u32[]{:S(2)}, u32[]{:S(2)}) collective-permute-start(bf16[608,256]{1,0:T(8,128)(2,1)S(1)} %get-tuple-element.841), channel_id=1, source_target_pairs={{8,0},{16,8},{24,16},{28,24},{20,28},{12,20},{4,12},{0,4},{9,1},{1... | collective-permute-start | bytes 933896 | tf_op jit(solution)/shard_map/ppermute | solution.py:510
  461.1 11.1 %collective-permute-start.171 = (bf16[608,256]{1,0:T(8,128)(2,1)S(1)}, bf16[608,256]{1,0:T(8,128)(2,1)S(1)}, u32[]{:S(2)}, u32[]{:S(2)}) collective-permute-start(bf16[608,256]{1,0:T(8,128)(2,1)S(1)} %get-tuple-element.842), channel_id=1, source_target_pairs={{0,8},{8,16},{16,24},{24,28},{28,20},{20,12},{12,4},{4,0},{1,9},{9... | collective-permute-start | bytes 933896 | tf_op jit(solution)/shard_map/ppermute | solution.py:510
  466.6 11.1 %collective-permute-start.176 = (bf16[608,256]{1,0:T(8,128)(2,1)S(1)}, bf16[608,256]{1,0:T(8,128)(2,1)S(1)}, u32[]{:S(2)}, u32[]{:S(2)}) collective-permute-start(bf16[608,256]{1,0:T(8,128)(2,1)S(1)} %get-tuple-element.849), channel_id=1, source_target_pairs={{8,0},{16,8},{24,16},{28,24},{20,28},{12,20},{4,12},{0,4},{9,1},{1... | collective-permute-start | bytes 933896 | tf_op jit(solution)/shard_map/ppermute | solution.py:510
  467.7 11.2 %collective-permute-start.177 = (bf16[608,256]{1,0:T(8,128)(2,1)S(1)}, bf16[608,256]{1,0:T(8,128)(2,1)S(1)}, u32[]{:S(2)}, u32[]{:S(2)}) collective-permute-start(bf16[608,256]{1,0:T(8,128)(2,1)S(1)} %get-tuple-element.850), channel_id=1, source_target_pairs={{0,8},{8,16},{16,24},{24,28},{28,20},{20,12},{12,4},{4,0},{1,9},{9... | collective-permute-start | bytes 933896 | tf_op jit(solution)/shard_map/ppermute | solution.py:510
  487.5 10.3 %collective-permute-start.184 = (bf16[512,256]{1,0:T(8,128)(2,1)S(1)}, bf16[512,256]{1,0:T(8,128)(2,1)S(1)}, u32[]{:S(2)}, u32[]{:S(2)}) collective-permute-start(bf16[512,256]{1,0:T(8,128)(2,1)S(1)} %get-tuple-element.878), channel_id=1, source_target_pairs={{8,0},{16,8},{24,16},{28,24},{20,28},{12,20},{4,12},{0,4},{9,1},{1... | collective-permute-start | bytes 786440 | tf_op jit(solution)/shard_map/ppermute | solution.py:510
  498.9 12.1 %collective-permute-start.188 = (bf16[544,256]{1,0:T(8,128)(2,1)S(1)}, bf16[544,256]{1,0:T(8,128)(2,1)S(1)}, u32[]{:S(2)}, u32[]{:S(2)}) collective-permute-start(bf16[544,256]{1,0:T(8,128)(2,1)S(1)} %get-tuple-element.885), channel_id=1, source_target_pairs={{8,0},{16,8},{24,16},{28,24},{20,28},{12,20},{4,12},{0,4},{9,1},{1... | collective-permute-start | bytes 835592 | tf_op jit(solution)/shard_map/ppermute | solution.py:510
  500.5 12.1 %collective-permute-start.189 = (bf16[544,256]{1,0:T(8,128)(2,1)S(1)}, bf16[544,256]{1,0:T(8,128)(2,1)S(1)}, u32[]{:S(2)}, u32[]{:S(2)}) collective-permute-start(bf16[544,256]{1,0:T(8,128)(2,1)S(1)} %get-tuple-element.886), channel_id=1, source_target_pairs={{0,8},{8,16},{16,24},{24,28},{28,20},{20,12},{12,4},{4,0},{1,9},{9... | collective-permute-start | bytes 835592 | tf_op jit(solution)/shard_map/ppermute | solution.py:510
  513.6 9.7 %collective-permute-start.192 = (bf16[544,256]{1,0:T(8,128)(2,1)S(1)}, bf16[544,256]{1,0:T(8,128)(2,1)S(1)}, u32[]{:S(2)}, u32[]{:S(2)}) collective-permute-start(bf16[544,256]{1,0:T(8,128)(2,1)S(1)} %get-tuple-element.891), channel_id=1, source_target_pairs={{8,0},{16,8},{24,16},{28,24},{20,28},{12,20},{4,12},{0,4},{9,1},{1... | collective-permute-start | bytes 835592 | tf_op jit(solution)/shard_map/ppermute | solution.py:510
  519.3 9.7 %collective-permute-start.190 = (bf16[512,256]{1,0:T(8,128)(2,1)S(1)}, bf16[512,256]{1,0:T(8,128)(2,1)S(1)}, u32[]{:S(2)}, u32[]{:S(2)}) collective-permute-start(bf16[512,256]{1,0:T(8,128)(2,1)S(1)} %get-tuple-element.889), channel_id=1, source_target_pairs={{8,0},{16,8},{24,16},{28,24},{20,28},{12,20},{4,12},{0,4},{9,1},{1... | collective-permute-start | bytes 786440 | tf_op jit(solution)/shard_map/ppermute | solution.py:510
  531.0 9.7 %collective-permute-start.194 = (bf16[512,256]{1,0:T(8,128)(2,1)S(1)}, bf16[512,256]{1,0:T(8,128)(2,1)S(1)}, u32[]{:S(2)}, u32[]{:S(2)}) collective-permute-start(bf16[512,256]{1,0:T(8,128)(2,1)S(1)} %get-tuple-element.895), channel_id=1, source_target_pairs={{8,0},{16,8},{24,16},{28,24},{20,28},{12,20},{4,12},{0,4},{9,1},{1... | collective-permute-start | bytes 786440 | tf_op jit(solution)/shard_map/ppermute | solution.py:510
  537.0 9.7 %collective-permute-start.200 = (bf16[544,256]{1,0:T(8,128)(2,1)S(1)}, bf16[544,256]{1,0:T(8,128)(2,1)S(1)}, u32[]{:S(2)}, u32[]{:S(2)}) collective-permute-start(bf16[544,256]{1,0:T(8,128)(2,1)S(1)} %get-tuple-element.903), channel_id=1, source_target_pairs={{8,0},{16,8},{24,16},{28,24},{20,28},{12,20},{4,12},{0,4},{9,1},{1... | collective-permute-start | bytes 835592 | tf_op jit(solution)/shard_map/ppermute | solution.py:510
  556.9 10.0 %collective-permute-start.206 = (bf16[512,256]{1,0:T(8,128)(2,1)S(1)}, bf16[512,256]{1,0:T(8,128)(2,1)S(1)}, u32[]{:S(2)}, u32[]{:S(2)}) collective-permute-start(bf16[512,256]{1,0:T(8,128)(2,1)S(1)} %get-tuple-element.932), channel_id=1, source_target_pairs={{8,0},{16,8},{24,16},{28,24},{20,28},{12,20},{4,12},{0,4},{9,1},{1... | collective-permute-start | bytes 786440 | tf_op jit(solution)/shard_map/ppermute | solution.py:510
  572.7 26.5 %collective-permute-start.210 = (f32[56,256]{1,0:T(8,128)S(1)}, f32[56,256]{1,0:T(8,128)S(1)}, u32[]{:S(2)}, u32[]{:S(2)}) collective-permute-start(f32[56,256]{1,0:T(8,128)S(1)} %select_add_fusion.2), channel_id=1, source_target_pairs={{0,4},{4,0},{8,12},{12,8},{16,20},{20,16},{24,28},{28,24},{1,5},{5... | collective-permute-start | bytes 172040 | tf_op jit(solution)/shard_map/ppermute | solution.py:135
  599.8 25.7 %collective-permute-start.211 = (f32[56,256]{1,0:T(8,128)S(1)}, f32[56,256]{1,0:T(8,128)S(1)}, u32[]{:S(2)}, u32[]{:S(2)}) collective-permute-start(f32[56,256]{1,0:T(8,128)S(1)} %add_add_fusion.2), channel_id=1, source_target_pairs={{0,8},{4,12},{8,0},{12,4},{16,24},{20,28},{24,16},{28,20},{1,9},{5... | collective-permute-start | bytes 172040 | tf_op jit(solution)/shard_map/ppermute | solution.py:135
  626.2 21.6 %collective-permute-start.212 = (f32[56,256]{1,0:T(8,128)S(1)}, f32[56,256]{1,0:T(8,128)S(1)}, u32[]{:S(2)}, u32[]{:S(2)}) collective-permute-start(f32[56,256]{1,0:T(8,128)S(1)} %add_add_fusion.1), channel_id=1, source_target_pairs={{0,16},{4,20},{8,24},{12,28},{16,0},{20,4},{24,8},{28,12},{1,17},{... | collective-permute-start | bytes 172040 | tf_op jit(solution)/shard_map/ppermute | solution.py:135
  (183 other events, 1559.5 us)

commit v3 on v2

--- a/solution.py
+++ b/solution.py
@@ -832,7 +832,7 @@
         norm = jnp.sqrt(jnp.sum(block * block)) + 1e-07
         x = block / norm
         for sweep in range(5):
-            x = newton_sweep_coarse(x) if sweep < 3 else newton_sweep(x)
+            x = newton_sweep_coarse(x) if sweep < 4 else newton_sweep(x)
         new_ref[0] = bank_ref[0] - LR_MUON * x
 
 

time: 660 us -> 660 us (level)
  the two profiles are of different devices: /device:TPU:20 before, /device:TPU:0 now
where the time goes in v3:
time: 660 us; the launch traced here: 650 us
  waiting for transfers between devices  242 us (37%)
  Pallas kernels  202 us (31%)
  starting transfers between devices  181 us (27%)
  other arithmetic  7.8 us (1%)
  local copies, waits for them, and re-layouts  7.35 us (1%)
    ppermute x144, waiting for transfers between devices, work(): lax.ppermute(sends[way], 'dp', self.perms[way])  169 us
    ppermute x144, starting transfers between devices, work(): lax.ppermute(sends[way], 'dp', self.perms[way])  149 us
    pallas_call x75, Pallas kernels, ring_step(): pl.pallas_call(kernel, out_shape=[pltpu.VMEM(held.shape, held.dtype)] + [...  131 us
    ppermute x69, waiting for transfers between devices, flip(): got = lax.ppermute(values, axis, [(i, i ^ bit) for i in range(size)])  72.7 us
    pallas_call x3, Pallas kernels, step(): pl.pallas_call(functools.partial(newton_kernel, len(got), base), grid_spe...  54.7 us
    ppermute x69, starting transfers between devices, flip(): got = lax.ppermute(values, axis, [(i, i ^ bit) for i in range(size)])  32.1 us
  transfers between devices with their start and end apart: 213, of which 131 were waited for; matrix products, arithmetic and copies ran while one was open for 1% of the time, Pallas kernels for 27%

profile of v3, /device:TPU:0, one launch (start us, length us, event | category | flops | bytes accessed | tf_op | source)
XLA Modules:
  0.0 649.9 jit_solution(5575645536725114733)
XLA Ops:
  2.1 6.4 plan.1
  18.0 3.0 collective-permute-start.2
  21.0 2.9 own_weights.1.refs_0_
  30.7 3.3 collective-permute-done
  46.3 3.5 collective-permute-done.9
  51.3 3.1 collective-permute-done.13
  62.1 3.5 collective-permute-done.17
  72.1 5.2 collective-permute-done.20
  83.4 3.1 collective-permute-done.27
  90.4 2.8 spread_step_modulations.1
  104.1 5.0 collective-permute-done.33
  117.3 3.0 collective-permute-done.39
  121.1 3.2 collective-permute-done.42
  130.7 3.9 collective-permute-done.43.refs_0_
  140.2 3.6 collective-permute-done.51.refs_1_
  146.9 2.6 collective-permute-done.49.refs_1_
  149.5 4.6 spread_step_attention.2
  160.0 3.3 collective-permute-done.59.refs_0_
  177.5 2.7 collective-permute-done.67.refs_0_
  186.5 2.9 collective-permute-done.66.refs_1_
  192.5 2.6 collective-permute-done.72.refs_1_
  200.8 4.0 spread_step_mlp.2
  210.7 3.4 collective-permute-done.80.refs_0_
  220.4 2.6 collective-permute-done.83.refs_5_
  227.1 4.3 spread_step_attention.3
  239.1 3.4 collective-permute-done.95.refs_0_
  250.8 3.5 collective-permute-done.99.refs_0_
  259.9 3.6 collective-permute-done.98.refs_1_
  266.6 2.6 collective-permute-done.104.refs_1_
  277.5 12.5 %spread_step_mlp.3 = (bf16[36,1024,256]{2,1,0:T(8,128)(2,1)S(1)}, f32[4,512,256]{2,1,0:T(8,128)S(1)}, bf16[4,512,256]{2,1,0:T(8,128)(2,1)S(1)}, f32[2,128,1024]{2,1,0:T(8,128)S(1)}, bf16[2,128,1024]{2,1,0:T(8,128)(2,1)S(1)}) custom-call(s32[36,4]{1,0:T(8,128)S(1)} %bitcast.167, ...), custom_call_target="tpu_custom_call", output_to_operand_aliasing={{0}: (5, {})} | custom-call | tf_op jit(solution)/shard_map/spread_step_mlp/pallas_call | solution.py:383
  292.6 7.8 %collective-permute-done.111.far_ref = bf16[128,1024]{1,0:T(8,128)(2,1)S(1)} collective-permute-done((bf16[128,1024]{1,0:T(8,128)(2,1)S(1)}, bf16[128,1024]{1,0:T(8,128)(2,1)S(1)}, u32[]{:S(2)}, u32[]{:S(2)}) %collective-permute-start.111) | collective-permute-done | bytes 262176 | tf_op jit(solution)/shard_map/ppermute | solution.py:135
  302.0 7.0 %collective-permute-done.113.refs_3_.refs_7_ = bf16[128,1024]{1,0:T(8,128)(2,1)S(1)} collective-permute-done((bf16[128,1024]{1,0:T(8,128)(2,1)S(1)}, bf16[128,1024]{1,0:T(8,128)(2,1)S(1)}, u32[]{:S(2)}, u32[]{:S(2)}) %collective-permute-start.113) | collective-permute-done | bytes 262176 | tf_op jit(solution)/shard_map/ppermute | solution.py:135
  310.5 4.5 layer__mlp_back.1
  317.7 4.5 layer__weight_grads.1
  333.6 3.3 collective-permute-done.121.refs_0_
  340.5 7.1 %reduce_step_attention_back.2 = (bf16[36,1024,256]{2,1,0:T(8,128)(2,1)S(1)}, bf16[512,256]{1,0:T(8,128)(2,1)S(1)}, bf16[512,256]{1,0:T(8,128)(2,1)S(1)}, bf16[3,...) custom-call(s32[36,4]{1,0:T(8,128)S(1)} %bitcast.173, ...), custom_call_target="tpu_custom_call", output_to_operand_aliasing={{0}: (3, {})} | custom-call | tf_op jit(solution)/shard_map/reduce_step_attention_back/pallas_call | solution.py:383
  351.6 2.9 reduce_step_weight_grads.3
  366.2 3.9 collective-permute-done.130.refs_0_
  373.0 5.0 reduce_step_mlp_back.1
  383.9 4.6 reduce_step_weight_grads.4
  398.8 3.6 collective-permute-done.147.refs_0_
  405.5 7.1 %reduce_step_attention_back.3 = (bf16[36,1024,256]{2,1,0:T(8,128)(2,1)S(1)}, bf16[512,256]{1,0:T(8,128)(2,1)S(1)}, bf16[512,256]{1,0:T(8,128)(2,1)S(1)}, bf16[3,...) custom-call(s32[36,4]{1,0:T(8,128)S(1)} %bitcast.181, ...), custom_call_target="tpu_custom_call", output_to_operand_aliasing={{0}: (3, {})} | custom-call | tf_op jit(solution)/shard_map/reduce_step_attention_back/pallas_call | solution.py:383
  416.0 3.0 reduce_step_weight_grads.5
  419.0 2.5 collective-permute-done.154.refs_0_
  427.7 2.6 collective-permute-done.157
  436.5 5.1 collective-permute-done.158.refs_0_
  445.9 2.4 collective-permute-done.164.refs_0_
  452.6 2.4 collective-permute-done.162.refs_0_
  459.3 2.4 collective-permute-done.168.refs_0_
  465.8 2.5 collective-permute-done.166.refs_0_
  472.6 2.4 collective-permute-done.172.refs_0_
  479.2 2.5 collective-permute-done.170.refs_0_
  495.1 2.9 reduce_step_cond_back.1
  502.4 3.3 collective-permute-done.181
  512.0 4.0 collective-permute-done.182.refs_0_
  519.5 2.5 collective-permute-done.188.refs_0_
  525.5 2.1 collective-permute-done.186.refs_0_
  531.3 2.3 collective-permute-done.192.refs_0_
  571.3 3.1 collective-permute-done.205
  577.9 4.9 collective-permute-done.208.refs_1_
  584.8 22.2 %optimizer.3 = (f32[8,1024,256]{2,1,0:T(8,128)}, f32[8,1024,256]{2,1,0:T(8,128)}, f32[8,128]{1,0:T(8,128)S(1)}) custom-call(s32[8]{0:T(128)S(1)} %get-tuple-element.958.big_ref, s32[8]{0:T(128)S(1)} %get-tuple-element.1034.left_ref, s32[8]{0:T(128)S(1)} %get-tuple-element.1033.right_ref, s32[36,4]{1,0:T(8,128)S(1)} %bitcast.206, ...), custom_call_target="tpu_custom_call" | custom-call | tf_op jit(solution)/shard_map/optimizer/pallas_call | solution.py:857
  608.9 21.8 %optimizer.4 = (f32[8,1024,256]{2,1,0:T(8,128)}, f32[8,1024,256]{2,1,0:T(8,128)}, f32[8,128]{1,0:T(8,128)S(1)}) custom-call(s32[8]{0:T(128)S(1)} %get-tuple-element.958.big_ref, s32[8]{0:T(128)S(1)} %get-tuple-element.1034.left_ref, s32[8]{0:T(128)S(1)} %get-tuple-element.1033.right_ref, ...), custom_call_target="tpu_custom_call", output_to_operand_aliasing={{0}: (13, {}), {1}: (14, {})} | custom-call | tf_op jit(solution)/shard_map/optimizer/pallas_call | solution.py:857
  634.0 10.7 %optimizer.5 = (f32[8,1024,256]{2,1,0:T(8,128)}, f32[8,1024,256]{2,1,0:T(8,128)}, f32[8,128]{1,0:T(8,128)S(1)}) custom-call(s32[8]{0:T(128)S(1)} %get-tuple-element.958.big_ref, s32[8]{0:T(128)S(1)} %get-tuple-element.1034.left_ref, s32[8]{0:T(128)S(1)} %get-tuple-element.1033.right_ref, ...), custom_call_target="tpu_custom_call", output_to_operand_aliasing={{0}: (13, {}), {1}: (14, {})} | custom-call | tf_op jit(solution)/shard_map/optimizer/pallas_call | solution.py:857
  646.7 2.7 update_tables.1
  (651 shorter events, 357.7 us)
Async XLA Ops:
  25.5 10.5 %collective-permute-start.4 = (bf16[512,256]{1,0:T(8,128)(2,1)S(1)}, bf16[512,256]{1,0:T(8,128)(2,1)S(1)}, u32[]{:S(2)}, u32[]{:S(2)}) collective-permute-start(bf16[512,256]{1,0:T(8,128)(2,1)S(1)} %get-tuple-element.505), channel_id=1, source_target_pairs={{8,0},{16,8},{24,16},{28,24},{20,28},{12,20},{4,12},{0,4},{9,1},{1... | collective-permute-start | bytes 786440 | tf_op jit(solution)/shard_map/ppermute | solution.py:436
  28.6 12.7 %collective-permute-start.7 = (bf16[512,256]{1,0:T(8,128)(2,1)S(1)}, bf16[512,256]{1,0:T(8,128)(2,1)S(1)}, u32[]{:S(2)}, u32[]{:S(2)}) collective-permute-start(bf16[512,256]{1,0:T(8,128)(2,1)S(1)} %get-tuple-element.502), channel_id=1, source_target_pairs={{0,8},{8,16},{16,24},{24,28},{28,20},{20,12},{12,4},{4,0},{1,9},{9... | collective-permute-start | bytes 786440 | tf_op jit(solution)/shard_map/ppermute | solution.py:436
  30.7 10.7 %collective-permute-start.8 = (bf16[512,256]{1,0:T(8,128)(2,1)S(1)}, bf16[512,256]{1,0:T(8,128)(2,1)S(1)}, u32[]{:S(2)}, u32[]{:S(2)}) collective-permute-start(bf16[512,256]{1,0:T(8,128)(2,1)S(1)} %get-tuple-element.503), channel_id=1, source_target_pairs={{8,0},{16,8},{24,16},{28,24},{20,28},{12,20},{4,12},{0,4},{9,1},{1... | collective-permute-start | bytes 786440 | tf_op jit(solution)/shard_map/ppermute | solution.py:436
  39.2 10.7 %collective-permute-start.10 = (bf16[512,256]{1,0:T(8,128)(2,1)S(1)}, bf16[512,256]{1,0:T(8,128)(2,1)S(1)}, u32[]{:S(2)}, u32[]{:S(2)}) collective-permute-start(bf16[512,256]{1,0:T(8,128)(2,1)S(1)} %get-tuple-element.510), channel_id=1, source_target_pairs={{0,8},{8,16},{16,24},{24,28},{28,20},{20,12},{12,4},{4,0},{1,9},{9... | collective-permute-start | bytes 786440 | tf_op jit(solution)/shard_map/ppermute | solution.py:436
  44.2 11.2 %collective-permute-start.14 = (bf16[512,256]{1,0:T(8,128)(2,1)S(1)}, bf16[512,256]{1,0:T(8,128)(2,1)S(1)}, u32[]{:S(2)}, u32[]{:S(2)}) collective-permute-start(bf16[512,256]{1,0:T(8,128)(2,1)S(1)} %get-tuple-element.515), channel_id=1, source_target_pairs={{0,8},{8,16},{16,24},{24,28},{28,20},{20,12},{12,4},{4,0},{1,9},{9... | collective-permute-start | bytes 786440 | tf_op jit(solution)/shard_map/ppermute | solution.py:436
  60.0 11.2 %collective-permute-start.21 = (bf16[512,256]{1,0:T(8,128)(2,1)S(1)}, bf16[512,256]{1,0:T(8,128)(2,1)S(1)}, u32[]{:S(2)}, u32[]{:S(2)}) collective-permute-start(bf16[512,256]{1,0:T(8,128)(2,1)S(1)} %get-tuple-element.528), channel_id=1, source_target_pairs={{0,8},{8,16},{16,24},{24,28},{28,20},{20,12},{12,4},{4,0},{1,9},{9... | collective-permute-start | bytes 786440 | tf_op jit(solution)/shard_map/ppermute | solution.py:436
  60.6 11.4 %collective-permute-start.22 = (bf16[512,256]{1,0:T(8,128)(2,1)S(1)}, bf16[512,256]{1,0:T(8,128)(2,1)S(1)}, u32[]{:S(2)}, u32[]{:S(2)}) collective-permute-start(bf16[512,256]{1,0:T(8,128)(2,1)S(1)} %get-tuple-element.529), channel_id=1, source_target_pairs={{8,0},{16,8},{24,16},{28,24},{20,28},{12,20},{4,12},{0,4},{9,1},{1... | collective-permute-start | bytes 786440 | tf_op jit(solution)/shard_map/ppermute | solution.py:436
  67.5 14.6 %collective-permute-start.24 = (bf16[512,256]{1,0:T(8,128)(2,1)S(1)}, bf16[512,256]{1,0:T(8,128)(2,1)S(1)}, u32[]{:S(2)}, u32[]{:S(2)}) collective-permute-start(bf16[512,256]{1,0:T(8,128)(2,1)S(1)} %get-tuple-element.533), channel_id=1, source_target_pairs={{0,8},{8,16},{16,24},{24,28},{28,20},{20,12},{12,4},{4,0},{1,9},{9... | collective-permute-start | bytes 786440 | tf_op jit(solution)/shard_map/ppermute | solution.py:436
  68.0 14.0 %collective-permute-start.25 = (bf16[512,256]{1,0:T(8,128)(2,1)S(1)}, bf16[512,256]{1,0:T(8,128)(2,1)S(1)}, u32[]{:S(2)}, u32[]{:S(2)}) collective-permute-start(bf16[512,256]{1,0:T(8,128)(2,1)S(1)} %get-tuple-element.534), channel_id=1, source_target_pairs={{8,0},{16,8},{24,16},{28,24},{20,28},{12,20},{4,12},{0,4},{9,1},{1... | collective-permute-start | bytes 786440 | tf_op jit(solution)/shard_map/ppermute | solution.py:436
  97.8 11.4 %collective-permute-start.33 = (f32[16,8,256]{2,0,1:T(8,128)S(1)}, f32[16,8,256]{2,0,1:T(8,128)S(1)}, u32[]{:S(2)}, u32[]{:S(2)}) collective-permute-start(f32[16,8,256]{2,0,1:T(8,128)S(1)} %slice_select_fusion), channel_id=1, source_target_pairs={{0,16},{4,20},{8,24},{12,28},{16,0},{20,4},{24,8},{28,12},{1,17},{... | collective-permute-start | bytes 393224 | tf_op jit(solution)/shard_map/ppermute | solution.py:135
  99.7 14.2 %collective-permute-start.37 = (bf16[512,256]{1,0:T(8,128)(2,1)S(1)}, bf16[512,256]{1,0:T(8,128)(2,1)S(1)}, u32[]{:S(2)}, u32[]{:S(2)}) collective-permute-start(bf16[512,256]{1,0:T(8,128)(2,1)S(1)} %get-tuple-element.554), channel_id=1, source_target_pairs={{0,8},{8,16},{16,24},{24,28},{28,20},{20,12},{12,4},{4,0},{1,9},{9... | collective-permute-start | bytes 786440 | tf_op jit(solution)/shard_map/ppermute | solution.py:436
  100.7 13.2 %collective-permute-start.38 = (bf16[512,256]{1,0:T(8,128)(2,1)S(1)}, bf16[512,256]{1,0:T(8,128)(2,1)S(1)}, u32[]{:S(2)}, u32[]{:S(2)}) collective-permute-start(bf16[512,256]{1,0:T(8,128)(2,1)S(1)} %get-tuple-element.555), channel_id=1, source_target_pairs={{8,0},{16,8},{24,16},{28,24},{20,28},{12,20},{4,12},{0,4},{9,1},{1... | collective-permute-start | bytes 786440 | tf_op jit(solution)/shard_map/ppermute | solution.py:436
  110.3 10.0 %collective-permute-start.40 = (bf16[512,256]{1,0:T(8,128)(2,1)S(1)}, bf16[512,256]{1,0:T(8,128)(2,1)S(1)}, u32[]{:S(2)}, u32[]{:S(2)}) collective-permute-start(bf16[512,256]{1,0:T(8,128)(2,1)S(1)} %get-tuple-element.561), channel_id=1, source_target_pairs={{0,8},{8,16},{16,24},{24,28},{28,20},{20,12},{12,4},{4,0},{1,9},{9... | collective-permute-start | bytes 786440 | tf_op jit(solution)/shard_map/ppermute | solution.py:436
  115.3 10.0 %collective-permute-start.45 = (bf16[512,256]{1,0:T(8,128)(2,1)S(1)}, bf16[512,256]{1,0:T(8,128)(2,1)S(1)}, u32[]{:S(2)}, u32[]{:S(2)}) collective-permute-start(bf16[512,256]{1,0:T(8,128)(2,1)S(1)} %get-tuple-element.566), channel_id=1, source_target_pairs={{0,8},{8,16},{16,24},{24,28},{28,20},{20,12},{12,4},{4,0},{1,9},{9... | collective-permute-start | bytes 786440 | tf_op jit(solution)/shard_map/ppermute | solution.py:436
  128.6 10.4 %collective-permute-start.52 = (bf16[128,1024]{1,0:T(8,128)(2,1)S(1)}, bf16[128,1024]{1,0:T(8,128)(2,1)S(1)}, u32[]{:S(2)}, u32[]{:S(2)}) collective-permute-start(bf16[128,1024]{1,0:T(8,128)(2,1)S(1)} %get-tuple-element.577.refs_3_), channel_id=1, source_target_pairs={{0,1},{1,0},{2,3},{3,2},{4,5},{5,4},{6,7},{7,6},{8,9},{9,8},{10,11... | collective-permute-start | bytes 786440 | tf_op jit(solution)/shard_map/ppermute | solution.py:135
  129.6 10.7 %collective-permute-start.50 = (bf16[512,256]{1,0:T(8,128)(2,1)S(1)}, bf16[512,256]{1,0:T(8,128)(2,1)S(1)}, u32[]{:S(2)}, u32[]{:S(2)}) collective-permute-start(bf16[512,256]{1,0:T(8,128)(2,1)S(1)} %get-tuple-element.583), channel_id=1, source_target_pairs={{0,8},{8,16},{16,24},{24,28},{28,20},{20,12},{12,4},{4,0},{1,9},{9... | collective-permute-start | bytes 786440 | tf_op jit(solution)/shard_map/ppermute | solution.py:436
  136.9 10.0 %collective-permute-start.48 = (bf16[512,256]{1,0:T(8,128)(2,1)S(1)}, bf16[512,256]{1,0:T(8,128)(2,1)S(1)}, u32[]{:S(2)}, u32[]{:S(2)}) collective-permute-start(bf16[512,256]{1,0:T(8,128)(2,1)S(1)} %get-tuple-element.581), channel_id=1, source_target_pairs={{0,8},{8,16},{16,24},{24,28},{28,20},{20,12},{12,4},{4,0},{1,9},{9... | collective-permute-start | bytes 786440 | tf_op jit(solution)/shard_map/ppermute | solution.py:436
  137.7 11.8 %collective-permute-start.49 = (bf16[512,256]{1,0:T(8,128)(2,1)S(1)}, bf16[512,256]{1,0:T(8,128)(2,1)S(1)}, u32[]{:S(2)}, u32[]{:S(2)}) collective-permute-start(bf16[512,256]{1,0:T(8,128)(2,1)S(1)} %get-tuple-element.582), channel_id=1, source_target_pairs={{8,0},{16,8},{24,16},{28,24},{20,28},{12,20},{4,12},{0,4},{9,1},{1... | collective-permute-start | bytes 786440 | tf_op jit(solution)/shard_map/ppermute | solution.py:436
  139.0 10.5 %collective-permute-start.54 = (bf16[128,1024]{1,0:T(8,128)(2,1)S(1)}, bf16[128,1024]{1,0:T(8,128)(2,1)S(1)}, u32[]{:S(2)}, u32[]{:S(2)}) collective-permute-start(bf16[128,1024]{1,0:T(8,128)(2,1)S(1)} %collective-permute-done.53.refs_5_), channel_id=1, source_target_pairs={{0,1},{1,0},{2,3},{3,2},{4,5},{5,4},{6,7},{7,6},{8,9},{9,8},{10,11... | collective-permute-start | bytes 786440 | tf_op jit(solution)/shard_map/ppermute | solution.py:135
  157.9 11.0 %collective-permute-start.63 = (bf16[512,256]{1,0:T(8,128)(2,1)S(1)}, bf16[512,256]{1,0:T(8,128)(2,1)S(1)}, u32[]{:S(2)}, u32[]{:S(2)}) collective-permute-start(bf16[512,256]{1,0:T(8,128)(2,1)S(1)} %get-tuple-element.599), channel_id=1, source_target_pairs={{0,8},{8,16},{16,24},{24,28},{28,20},{20,12},{12,4},{4,0},{1,9},{9... | collective-permute-start | bytes 786440 | tf_op jit(solution)/shard_map/ppermute | solution.py:436
  159.1 11.1 %collective-permute-start.64 = (bf16[512,256]{1,0:T(8,128)(2,1)S(1)}, bf16[512,256]{1,0:T(8,128)(2,1)S(1)}, u32[]{:S(2)}, u32[]{:S(2)}) collective-permute-start(bf16[512,256]{1,0:T(8,128)(2,1)S(1)} %get-tuple-element.600), channel_id=1, source_target_pairs={{8,0},{16,8},{24,16},{28,24},{20,28},{12,20},{4,12},{0,4},{9,1},{1... | collective-permute-start | bytes 786440 | tf_op jit(solution)/shard_map/ppermute | solution.py:436
  171.3 10.2 %collective-permute-start.68 = (bf16[512,256]{1,0:T(8,128)(2,1)S(1)}, bf16[512,256]{1,0:T(8,128)(2,1)S(1)}, u32[]{:S(2)}, u32[]{:S(2)}) collective-permute-start(bf16[512,256]{1,0:T(8,128)(2,1)S(1)} %get-tuple-element.615), channel_id=1, source_target_pairs={{8,0},{16,8},{24,16},{28,24},{20,28},{12,20},{4,12},{0,4},{9,1},{1... | collective-permute-start | bytes 786440 | tf_op jit(solution)/shard_map/ppermute | solution.py:436
  173.2 10.0 %collective-permute-start.74 = (bf16[128,1024]{1,0:T(8,128)(2,1)S(1)}, bf16[128,1024]{1,0:T(8,128)(2,1)S(1)}, u32[]{:S(2)}, u32[]{:S(2)}) collective-permute-start(bf16[128,1024]{1,0:T(8,128)(2,1)S(1)} %get-tuple-element.605.refs_3_), channel_id=1, source_target_pairs={{0,2},{1,3},{2,0},{3,1},{4,6},{5,7},{6,4},{7,5},{8,10},{9,11},{10,... | collective-permute-start | bytes 786440 | tf_op jit(solution)/shard_map/ppermute | solution.py:135
  182.5 10.0 %collective-permute-start.71 = (bf16[512,256]{1,0:T(8,128)(2,1)S(1)}, bf16[512,256]{1,0:T(8,128)(2,1)S(1)}, u32[]{:S(2)}, u32[]{:S(2)}) collective-permute-start(bf16[512,256]{1,0:T(8,128)(2,1)S(1)} %get-tuple-element.620), channel_id=1, source_target_pairs={{0,8},{8,16},{16,24},{24,28},{28,20},{20,12},{12,4},{4,0},{1,9},{9... | collective-permute-start | bytes 786440 | tf_op jit(solution)/shard_map/ppermute | solution.py:436
  183.2 11.8 %collective-permute-start.72 = (bf16[512,256]{1,0:T(8,128)(2,1)S(1)}, bf16[512,256]{1,0:T(8,128)(2,1)S(1)}, u32[]{:S(2)}, u32[]{:S(2)}) collective-permute-start(bf16[512,256]{1,0:T(8,128)(2,1)S(1)} %get-tuple-element.621), channel_id=1, source_target_pairs={{8,0},{16,8},{24,16},{28,24},{20,28},{12,20},{4,12},{0,4},{9,1},{1... | collective-permute-start | bytes 786440 | tf_op jit(solution)/shard_map/ppermute | solution.py:436
  184.6 13.5 %collective-permute-start.75 = (bf16[128,1024]{1,0:T(8,128)(2,1)S(1)}, bf16[128,1024]{1,0:T(8,128)(2,1)S(1)}, u32[]{:S(2)}, u32[]{:S(2)}) collective-permute-start(bf16[128,1024]{1,0:T(8,128)(2,1)S(1)} %collective-permute-done.74.refs_5_), channel_id=1, source_target_pairs={{0,1},{1,0},{2,3},{3,2},{4,5},{5,4},{6,7},{7,6},{8,9},{9,8},{10,11... | collective-permute-start | bytes 786440 | tf_op jit(solution)/shard_map/ppermute | solution.py:135
  208.6 10.6 %collective-permute-start.84 = (bf16[512,256]{1,0:T(8,128)(2,1)S(1)}, bf16[512,256]{1,0:T(8,128)(2,1)S(1)}, u32[]{:S(2)}, u32[]{:S(2)}) collective-permute-start(bf16[512,256]{1,0:T(8,128)(2,1)S(1)} %get-tuple-element.636), channel_id=1, source_target_pairs={{0,8},{8,16},{16,24},{24,28},{28,20},{20,12},{12,4},{4,0},{1,9},{9... | collective-permute-start | bytes 786440 | tf_op jit(solution)/shard_map/ppermute | solution.py:436
  209.6 10.8 %collective-permute-start.85 = (bf16[512,256]{1,0:T(8,128)(2,1)S(1)}, bf16[512,256]{1,0:T(8,128)(2,1)S(1)}, u32[]{:S(2)}, u32[]{:S(2)}) collective-permute-start(bf16[512,256]{1,0:T(8,128)(2,1)S(1)} %get-tuple-element.637), channel_id=1, source_target_pairs={{8,0},{16,8},{24,16},{28,24},{20,28},{12,20},{4,12},{0,4},{9,1},{1... | collective-permute-start | bytes 786440 | tf_op jit(solution)/shard_map/ppermute | solution.py:436
  237.0 11.1 %collective-permute-start.92 = (bf16[512,256]{1,0:T(8,128)(2,1)S(1)}, bf16[512,256]{1,0:T(8,128)(2,1)S(1)}, u32[]{:S(2)}, u32[]{:S(2)}) collective-permute-start(bf16[512,256]{1,0:T(8,128)(2,1)S(1)} %get-tuple-element.661), channel_id=1, source_target_pairs={{0,8},{8,16},{16,24},{24,28},{28,20},{20,12},{12,4},{4,0},{1,9},{9... | collective-permute-start | bytes 786440 | tf_op jit(solution)/shard_map/ppermute | solution.py:436
  237.4 11.1 %collective-permute-start.93 = (bf16[512,256]{1,0:T(8,128)(2,1)S(1)}, bf16[512,256]{1,0:T(8,128)(2,1)S(1)}, u32[]{:S(2)}, u32[]{:S(2)}) collective-permute-start(bf16[512,256]{1,0:T(8,128)(2,1)S(1)} %get-tuple-element.662), channel_id=1, source_target_pairs={{8,0},{16,8},{24,16},{28,24},{20,28},{12,20},{4,12},{0,4},{9,1},{1... | collective-permute-start | bytes 786440 | tf_op jit(solution)/shard_map/ppermute | solution.py:436
  247.1 10.2 %collective-permute-start.108 = (bf16[128,1024]{1,0:T(8,128)(2,1)S(1)}, bf16[128,1024]{1,0:T(8,128)(2,1)S(1)}, u32[]{:S(2)}, u32[]{:S(2)}) collective-permute-start(bf16[128,1024]{1,0:T(8,128)(2,1)S(1)} %get-tuple-element.667.refs_5_.refs_1_), channel_id=1, source_target_pairs={{0,2},{1,3},{2,0},{3,1},{4,6},{5,7},{6,4},{7,5},{8,10},{9,11},{10,... | collective-permute-start | bytes 786440 | tf_op jit(solution)/shard_map/ppermute | solution.py:135
  248.1 10.3 %collective-permute-start.107 = (bf16[128,1024]{1,0:T(8,128)(2,1)S(1)}, bf16[128,1024]{1,0:T(8,128)(2,1)S(1)}, u32[]{:S(2)}, u32[]{:S(2)}) collective-permute-start(bf16[128,1024]{1,0:T(8,128)(2,1)S(1)} %get-tuple-element.667.refs_5_.refs_1_), channel_id=1, source_target_pairs={{0,1},{1,0},{2,3},{3,2},{4,5},{5,4},{6,7},{7,6},{8,9},{9,8},{10,11... | collective-permute-start | bytes 786440 | tf_op jit(solution)/shard_map/ppermute | solution.py:135
  249.4 10.5 %collective-permute-start.97 = (bf16[512,256]{1,0:T(8,128)(2,1)S(1)}, bf16[512,256]{1,0:T(8,128)(2,1)S(1)}, u32[]{:S(2)}, u32[]{:S(2)}) collective-permute-start(bf16[512,256]{1,0:T(8,128)(2,1)S(1)} %get-tuple-element.671), channel_id=1, source_target_pairs={{0,8},{8,16},{16,24},{24,28},{28,20},{20,12},{12,4},{4,0},{1,9},{9... | collective-permute-start | bytes 786440 | tf_op jit(solution)/shard_map/ppermute | solution.py:436
  256.3 10.3 %collective-permute-start.103 = (bf16[512,256]{1,0:T(8,128)(2,1)S(1)}, bf16[512,256]{1,0:T(8,128)(2,1)S(1)}, u32[]{:S(2)}, u32[]{:S(2)}) collective-permute-start(bf16[512,256]{1,0:T(8,128)(2,1)S(1)} %get-tuple-element.679), channel_id=1, source_target_pairs={{0,8},{8,16},{16,24},{24,28},{28,20},{20,12},{12,4},{4,0},{1,9},{9... | collective-permute-start | bytes 786440 | tf_op jit(solution)/shard_map/ppermute | solution.py:436
  257.3 11.8 %collective-permute-start.104 = (bf16[512,256]{1,0:T(8,128)(2,1)S(1)}, bf16[512,256]{1,0:T(8,128)(2,1)S(1)}, u32[]{:S(2)}, u32[]{:S(2)}) collective-permute-start(bf16[512,256]{1,0:T(8,128)(2,1)S(1)} %get-tuple-element.680), channel_id=1, source_target_pairs={{8,0},{16,8},{24,16},{28,24},{20,28},{12,20},{4,12},{0,4},{9,1},{1... | collective-permute-start | bytes 786440 | tf_op jit(solution)/shard_map/ppermute | solution.py:436
  258.4 13.8 %collective-permute-start.109 = (bf16[128,1024]{1,0:T(8,128)(2,1)S(1)}, bf16[128,1024]{1,0:T(8,128)(2,1)S(1)}, u32[]{:S(2)}, u32[]{:S(2)}) collective-permute-start(bf16[128,1024]{1,0:T(8,128)(2,1)S(1)} %collective-permute-done.108.refs_7_.refs_3_), channel_id=1, source_target_pairs={{0,1},{1,0},{2,3},{3,2},{4,5},{5,4},{6,7},{7,6},{8,9},{9,8},{10,11... | collective-permute-start | bytes 786440 | tf_op jit(solution)/shard_map/ppermute | solution.py:135
  264.7 10.0 %collective-permute-start.102 = (bf16[512,256]{1,0:T(8,128)(2,1)S(1)}, bf16[512,256]{1,0:T(8,128)(2,1)S(1)}, u32[]{:S(2)}, u32[]{:S(2)}) collective-permute-start(bf16[512,256]{1,0:T(8,128)(2,1)S(1)} %get-tuple-element.678), channel_id=1, source_target_pairs={{8,0},{16,8},{24,16},{28,24},{20,28},{12,20},{4,12},{0,4},{9,1},{1... | collective-permute-start | bytes 786440 | tf_op jit(solution)/shard_map/ppermute | solution.py:436
  421.9 11.5 %collective-permute-start.160 = (bf16[512,256]{1,0:T(8,128)(2,1)S(1)}, bf16[512,256]{1,0:T(8,128)(2,1)S(1)}, u32[]{:S(2)}, u32[]{:S(2)}) collective-permute-start(bf16[512,256]{1,0:T(8,128)(2,1)S(1)} %get-tuple-element.811), channel_id=1, source_target_pairs={{8,0},{16,8},{24,16},{28,24},{20,28},{12,20},{4,12},{0,4},{9,1},{1... | collective-permute-start | bytes 786440 | tf_op jit(solution)/shard_map/ppermute | solution.py:510
  423.0 10.4 %collective-permute-start.161 = (bf16[512,256]{1,0:T(8,128)(2,1)S(1)}, bf16[512,256]{1,0:T(8,128)(2,1)S(1)}, u32[]{:S(2)}, u32[]{:S(2)}) collective-permute-start(bf16[512,256]{1,0:T(8,128)(2,1)S(1)} %get-tuple-element.812), channel_id=1, source_target_pairs={{0,8},{8,16},{16,24},{24,28},{28,20},{20,12},{12,4},{4,0},{1,9},{9... | collective-permute-start | bytes 786440 | tf_op jit(solution)/shard_map/ppermute | solution.py:510
  431.3 10.4 %collective-permute-start.158 = (bf16[608,256]{1,0:T(8,128)(2,1)S(1)}, bf16[608,256]{1,0:T(8,128)(2,1)S(1)}, u32[]{:S(2)}, u32[]{:S(2)}) collective-permute-start(bf16[608,256]{1,0:T(8,128)(2,1)S(1)} %get-tuple-element.825), channel_id=1, source_target_pairs={{8,0},{16,8},{24,16},{28,24},{20,28},{12,20},{4,12},{0,4},{9,1},{1... | collective-permute-start | bytes 933896 | tf_op jit(solution)/shard_map/ppermute | solution.py:510
  432.5 10.3 %collective-permute-start.159 = (bf16[608,256]{1,0:T(8,128)(2,1)S(1)}, bf16[608,256]{1,0:T(8,128)(2,1)S(1)}, u32[]{:S(2)}, u32[]{:S(2)}) collective-permute-start(bf16[608,256]{1,0:T(8,128)(2,1)S(1)} %get-tuple-element.826), channel_id=1, source_target_pairs={{0,8},{8,16},{16,24},{24,28},{28,20},{20,12},{12,4},{4,0},{1,9},{9... | collective-permute-start | bytes 933896 | tf_op jit(solution)/shard_map/ppermute | solution.py:510
  434.5 13.9 %collective-permute-start.164 = (bf16[608,256]{1,0:T(8,128)(2,1)S(1)}, bf16[608,256]{1,0:T(8,128)(2,1)S(1)}, u32[]{:S(2)}, u32[]{:S(2)}) collective-permute-start(bf16[608,256]{1,0:T(8,128)(2,1)S(1)} %get-tuple-element.831), channel_id=1, source_target_pairs={{8,0},{16,8},{24,16},{28,24},{20,28},{12,20},{4,12},{0,4},{9,1},{1... | collective-permute-start | bytes 933896 | tf_op jit(solution)/shard_map/ppermute | solution.py:510
  435.6 13.8 %collective-permute-start.165 = (bf16[608,256]{1,0:T(8,128)(2,1)S(1)}, bf16[608,256]{1,0:T(8,128)(2,1)S(1)}, u32[]{:S(2)}, u32[]{:S(2)}) collective-permute-start(bf16[608,256]{1,0:T(8,128)(2,1)S(1)} %get-tuple-element.832), channel_id=1, source_target_pairs={{0,8},{8,16},{16,24},{24,28},{28,20},{20,12},{12,4},{4,0},{1,9},{9... | collective-permute-start | bytes 933896 | tf_op jit(solution)/shard_map/ppermute | solution.py:510
  443.8 11.2 %collective-permute-start.162 = (bf16[608,256]{1,0:T(8,128)(2,1)S(1)}, bf16[608,256]{1,0:T(8,128)(2,1)S(1)}, u32[]{:S(2)}, u32[]{:S(2)}) collective-permute-start(bf16[608,256]{1,0:T(8,128)(2,1)S(1)} %get-tuple-element.829), channel_id=1, source_target_pairs={{8,0},{16,8},{24,16},{28,24},{20,28},{12,20},{4,12},{0,4},{9,1},{1... | collective-permute-start | bytes 933896 | tf_op jit(solution)/shard_map/ppermute | solution.py:510
  444.7 11.4 %collective-permute-start.163 = (bf16[608,256]{1,0:T(8,128)(2,1)S(1)}, bf16[608,256]{1,0:T(8,128)(2,1)S(1)}, u32[]{:S(2)}, u32[]{:S(2)}) collective-permute-start(bf16[608,256]{1,0:T(8,128)(2,1)S(1)} %get-tuple-element.830), channel_id=1, source_target_pairs={{0,8},{8,16},{16,24},{24,28},{28,20},{20,12},{12,4},{4,0},{1,9},{9... | collective-permute-start | bytes 933896 | tf_op jit(solution)/shard_map/ppermute | solution.py:510
  450.5 11.2 %collective-permute-start.168 = (bf16[608,256]{1,0:T(8,128)(2,1)S(1)}, bf16[608,256]{1,0:T(8,128)(2,1)S(1)}, u32[]{:S(2)}, u32[]{:S(2)}) collective-permute-start(bf16[608,256]{1,0:T(8,128)(2,1)S(1)} %get-tuple-element.837), channel_id=1, source_target_pairs={{8,0},{16,8},{24,16},{28,24},{20,28},{12,20},{4,12},{0,4},{9,1},{1... | collective-permute-start | bytes 933896 | tf_op jit(solution)/shard_map/ppermute | solution.py:510
  451.4 11.4 %collective-permute-start.169 = (bf16[608,256]{1,0:T(8,128)(2,1)S(1)}, bf16[608,256]{1,0:T(8,128)(2,1)S(1)}, u32[]{:S(2)}, u32[]{:S(2)}) collective-permute-start(bf16[608,256]{1,0:T(8,128)(2,1)S(1)} %get-tuple-element.838), channel_id=1, source_target_pairs={{0,8},{8,16},{16,24},{24,28},{28,20},{20,12},{12,4},{4,0},{1,9},{9... | collective-permute-start | bytes 933896 | tf_op jit(solution)/shard_map/ppermute | solution.py:510
  457.2 11.2 %collective-permute-start.166 = (bf16[608,256]{1,0:T(8,128)(2,1)S(1)}, bf16[608,256]{1,0:T(8,128)(2,1)S(1)}, u32[]{:S(2)}, u32[]{:S(2)}) collective-permute-start(bf16[608,256]{1,0:T(8,128)(2,1)S(1)} %get-tuple-element.835), channel_id=1, source_target_pairs={{8,0},{16,8},{24,16},{28,24},{20,28},{12,20},{4,12},{0,4},{9,1},{1... | collective-permute-start | bytes 933896 | tf_op jit(solution)/shard_map/ppermute | solution.py:510
  458.1 11.4 %collective-permute-start.167 = (bf16[608,256]{1,0:T(8,128)(2,1)S(1)}, bf16[608,256]{1,0:T(8,128)(2,1)S(1)}, u32[]{:S(2)}, u32[]{:S(2)}) collective-permute-start(bf16[608,256]{1,0:T(8,128)(2,1)S(1)} %get-tuple-element.836), channel_id=1, source_target_pairs={{0,8},{8,16},{16,24},{24,28},{28,20},{20,12},{12,4},{4,0},{1,9},{9... | collective-permute-start | bytes 933896 | tf_op jit(solution)/shard_map/ppermute | solution.py:510
  463.7 11.3 %collective-permute-start.172 = (bf16[608,256]{1,0:T(8,128)(2,1)S(1)}, bf16[608,256]{1,0:T(8,128)(2,1)S(1)}, u32[]{:S(2)}, u32[]{:S(2)}) collective-permute-start(bf16[608,256]{1,0:T(8,128)(2,1)S(1)} %get-tuple-element.843), channel_id=1, source_target_pairs={{8,0},{16,8},{24,16},{28,24},{20,28},{12,20},{4,12},{0,4},{9,1},{1... | collective-permute-start | bytes 933896 | tf_op jit(solution)/shard_map/ppermute | solution.py:510
  464.7 11.4 %collective-permute-start.173 = (bf16[608,256]{1,0:T(8,128)(2,1)S(1)}, bf16[608,256]{1,0:T(8,128)(2,1)S(1)}, u32[]{:S(2)}, u32[]{:S(2)}) collective-permute-start(bf16[608,256]{1,0:T(8,128)(2,1)S(1)} %get-tuple-element.844), channel_id=1, source_target_pairs={{0,8},{8,16},{16,24},{24,28},{28,20},{20,12},{12,4},{4,0},{1,9},{9... | collective-permute-start | bytes 933896 | tf_op jit(solution)/shard_map/ppermute | solution.py:510
  470.5 11.2 %collective-permute-start.170 = (bf16[608,256]{1,0:T(8,128)(2,1)S(1)}, bf16[608,256]{1,0:T(8,128)(2,1)S(1)}, u32[]{:S(2)}, u32[]{:S(2)}) collective-permute-start(bf16[608,256]{1,0:T(8,128)(2,1)S(1)} %get-tuple-element.841), channel_id=1, source_target_pairs={{8,0},{16,8},{24,16},{28,24},{20,28},{12,20},{4,12},{0,4},{9,1},{1... | collective-permute-start | bytes 933896 | tf_op jit(solution)/shard_map/ppermute | solution.py:510
  471.4 11.4 %collective-permute-start.171 = (bf16[608,256]{1,0:T(8,128)(2,1)S(1)}, bf16[608,256]{1,0:T(8,128)(2,1)S(1)}, u32[]{:S(2)}, u32[]{:S(2)}) collective-permute-start(bf16[608,256]{1,0:T(8,128)(2,1)S(1)} %get-tuple-element.842), channel_id=1, source_target_pairs={{0,8},{8,16},{16,24},{24,28},{28,20},{20,12},{12,4},{4,0},{1,9},{9... | collective-permute-start | bytes 933896 | tf_op jit(solution)/shard_map/ppermute | solution.py:510
  477.1 11.3 %collective-permute-start.176 = (bf16[608,256]{1,0:T(8,128)(2,1)S(1)}, bf16[608,256]{1,0:T(8,128)(2,1)S(1)}, u32[]{:S(2)}, u32[]{:S(2)}) collective-permute-start(bf16[608,256]{1,0:T(8,128)(2,1)S(1)} %get-tuple-element.849), channel_id=1, source_target_pairs={{8,0},{16,8},{24,16},{28,24},{20,28},{12,20},{4,12},{0,4},{9,1},{1... | collective-permute-start | bytes 933896 | tf_op jit(solution)/shard_map/ppermute | solution.py:510
  478.1 11.4 %collective-permute-start.177 = (bf16[608,256]{1,0:T(8,128)(2,1)S(1)}, bf16[608,256]{1,0:T(8,128)(2,1)S(1)}, u32[]{:S(2)}, u32[]{:S(2)}) collective-permute-start(bf16[608,256]{1,0:T(8,128)(2,1)S(1)} %get-tuple-element.850), channel_id=1, source_target_pairs={{0,8},{8,16},{16,24},{24,28},{28,20},{20,12},{12,4},{4,0},{1,9},{9... | collective-permute-start | bytes 933896 | tf_op jit(solution)/shard_map/ppermute | solution.py:510
  498.0 10.8 %collective-permute-start.184 = (bf16[512,256]{1,0:T(8,128)(2,1)S(1)}, bf16[512,256]{1,0:T(8,128)(2,1)S(1)}, u32[]{:S(2)}, u32[]{:S(2)}) collective-permute-start(bf16[512,256]{1,0:T(8,128)(2,1)S(1)} %get-tuple-element.878), channel_id=1, source_target_pairs={{8,0},{16,8},{24,16},{28,24},{20,28},{12,20},{4,12},{0,4},{9,1},{1... | collective-permute-start | bytes 786440 | tf_op jit(solution)/shard_map/ppermute | solution.py:510
  498.6 10.2 %collective-permute-start.185 = (bf16[512,256]{1,0:T(8,128)(2,1)S(1)}, bf16[512,256]{1,0:T(8,128)(2,1)S(1)}, u32[]{:S(2)}, u32[]{:S(2)}) collective-permute-start(bf16[512,256]{1,0:T(8,128)(2,1)S(1)} %get-tuple-element.879), channel_id=1, source_target_pairs={{0,8},{8,16},{16,24},{24,28},{28,20},{20,12},{12,4},{4,0},{1,9},{9... | collective-permute-start | bytes 786440 | tf_op jit(solution)/shard_map/ppermute | solution.py:510
  509.9 12.1 %collective-permute-start.188 = (bf16[544,256]{1,0:T(8,128)(2,1)S(1)}, bf16[544,256]{1,0:T(8,128)(2,1)S(1)}, u32[]{:S(2)}, u32[]{:S(2)}) collective-permute-start(bf16[544,256]{1,0:T(8,128)(2,1)S(1)} %get-tuple-element.885), channel_id=1, source_target_pairs={{8,0},{16,8},{24,16},{28,24},{20,28},{12,20},{4,12},{0,4},{9,1},{1... | collective-permute-start | bytes 835592 | tf_op jit(solution)/shard_map/ppermute | solution.py:510
  510.3 12.0 %collective-permute-start.189 = (bf16[544,256]{1,0:T(8,128)(2,1)S(1)}, bf16[544,256]{1,0:T(8,128)(2,1)S(1)}, u32[]{:S(2)}, u32[]{:S(2)}) collective-permute-start(bf16[544,256]{1,0:T(8,128)(2,1)S(1)} %get-tuple-element.886), channel_id=1, source_target_pairs={{0,8},{8,16},{16,24},{24,28},{28,20},{20,12},{12,4},{4,0},{1,9},{9... | collective-permute-start | bytes 835592 | tf_op jit(solution)/shard_map/ppermute | solution.py:510
  517.4 10.2 %collective-permute-start.186 = (bf16[512,256]{1,0:T(8,128)(2,1)S(1)}, bf16[512,256]{1,0:T(8,128)(2,1)S(1)}, u32[]{:S(2)}, u32[]{:S(2)}) collective-permute-start(bf16[512,256]{1,0:T(8,128)(2,1)S(1)} %get-tuple-element.883), channel_id=1, source_target_pairs={{8,0},{16,8},{24,16},{28,24},{20,28},{12,20},{4,12},{0,4},{9,1},{1... | collective-permute-start | bytes 786440 | tf_op jit(solution)/shard_map/ppermute | solution.py:510
  523.4 10.2 %collective-permute-start.192 = (bf16[544,256]{1,0:T(8,128)(2,1)S(1)}, bf16[544,256]{1,0:T(8,128)(2,1)S(1)}, u32[]{:S(2)}, u32[]{:S(2)}) collective-permute-start(bf16[544,256]{1,0:T(8,128)(2,1)S(1)} %get-tuple-element.891), channel_id=1, source_target_pairs={{8,0},{16,8},{24,16},{28,24},{20,28},{12,20},{4,12},{0,4},{9,1},{1... | collective-permute-start | bytes 835592 | tf_op jit(solution)/shard_map/ppermute | solution.py:510
  584.0 23.6 %collective-permute-start.210 = (f32[56,256]{1,0:T(8,128)S(1)}, f32[56,256]{1,0:T(8,128)S(1)}, u32[]{:S(2)}, u32[]{:S(2)}) collective-permute-start(f32[56,256]{1,0:T(8,128)S(1)} %select_add_fusion.2), channel_id=1, source_target_pairs={{0,4},{4,0},{8,12},{12,8},{16,20},{20,16},{24,28},{28,24},{1,5},{5... | collective-permute-start | bytes 172040 | tf_op jit(solution)/shard_map/ppermute | solution.py:135
  608.2 23.0 %collective-permute-start.211 = (f32[56,256]{1,0:T(8,128)S(1)}, f32[56,256]{1,0:T(8,128)S(1)}, u32[]{:S(2)}, u32[]{:S(2)}) collective-permute-start(f32[56,256]{1,0:T(8,128)S(1)} %add_add_fusion.2), channel_id=1, source_target_pairs={{0,8},{4,12},{8,0},{12,4},{16,24},{20,28},{24,16},{28,20},{1,9},{5... | collective-permute-start | bytes 172040 | tf_op jit(solution)/shard_map/ppermute | solution.py:135
  631.8 13.4 %collective-permute-start.212 = (f32[56,256]{1,0:T(8,128)S(1)}, f32[56,256]{1,0:T(8,128)S(1)}, u32[]{:S(2)}, u32[]{:S(2)}) collective-permute-start(f32[56,256]{1,0:T(8,128)S(1)} %add_add_fusion.1), channel_id=1, source_target_pairs={{0,16},{4,20},{8,24},{12,28},{16,0},{20,4},{24,8},{28,12},{1,17},{... | collective-permute-start | bytes 172040 | tf_op jit(solution)/shard_map/ppermute | solution.py:135
  (183 other events, 1540.8 us)

commit v4 on v2

--- a/solution.py
+++ b/solution.py
@@ -843,7 +843,7 @@
         self.news = []
         self.at = 0
 
-    def step(self, after=(), count=3):
+    def step(self, after=(), count=4):
         a_all, b_all, master, momentum, held, *got = self.arrays
         n_slots, rows, columns = master.shape
         base, count = self.at, min(count, n_slots - self.at)

time: 660 us -> 667 us (1.011)
  the two profiles are of different devices: /device:TPU:20 before, /device:TPU:0 now
where the time goes in v4:
time: 667 us; the launch traced here: 659 us
  waiting for transfers between devices  243 us (36%)
  starting transfers between devices  198 us (30%)
  Pallas kernels  194 us (29%)
  other arithmetic  7.16 us (1%)
  local copies, waits for them, and re-layouts  6.84 us (1%)
    ppermute x144, waiting for transfers between devices, work(): lax.ppermute(sends[way], 'dp', self.perms[way])  170 us
    ppermute x144, starting transfers between devices, work(): lax.ppermute(sends[way], 'dp', self.perms[way])  146 us
    pallas_call x75, Pallas kernels, ring_step(): pl.pallas_call(kernel, out_shape=[pltpu.VMEM(held.shape, held.dtype)] + [...  132 us
    ppermute x69, waiting for transfers between devices, flip(): got = lax.ppermute(values, axis, [(i, i ^ bit) for i in range(size)])  73.2 us
    ppermute x69, starting transfers between devices, flip(): got = lax.ppermute(values, axis, [(i, i ^ bit) for i in range(size)])  51.4 us
    pallas_call x2, Pallas kernels, step(): pl.pallas_call(functools.partial(newton_kernel, len(got), base), grid_spe...  46.4 us
  transfers between devices with their start and end apart: 213, of which 133 were waited for; matrix products, arithmetic and copies ran while one was open for 1% of the time, Pallas kernels for 25%

profile of v4, /device:TPU:0, one launch (start us, length us, event | category | flops | bytes accessed | tf_op | source)
XLA Modules:
  0.0 659.1 jit_solution(11836212299178739385)
XLA Ops:
  2.1 6.4 plan.1
  18.0 3.0 collective-permute-start.2
  23.9 2.3 collective-permute-start.3
  33.1 2.3 collective-permute-done.4.refs_1_
  40.8 2.4 collective-permute-start.9
  46.3 3.5 collective-permute-done.9
  51.3 3.1 collective-permute-done.13
  61.6 4.0 collective-permute-done.17
  72.1 5.2 collective-permute-done.20
  83.4 3.1 collective-permute-done.27
  90.4 3.4 spread_step_modulations.1
  104.2 5.1 collective-permute-done.33
  117.5 2.9 collective-permute-done.39
  121.6 3.2 collective-permute-done.42
  130.9 4.1 collective-permute-done.43.refs_0_
  140.7 3.6 collective-permute-done.51.refs_1_
  147.3 2.6 collective-permute-done.49.refs_1_
  149.9 4.6 spread_step_attention.2
  160.4 3.4 collective-permute-done.59.refs_0_
  177.6 3.0 collective-permute-done.67.refs_0_
  184.2 2.5 collective-permute-done.65.refs_0_
  186.7 3.2 collective-permute-done.66.refs_1_
  192.9 2.6 collective-permute-done.72.refs_1_
  201.1 3.9 spread_step_mlp.2
  210.9 3.4 collective-permute-done.80.refs_0_
  220.5 2.8 collective-permute-done.83.refs_5_
  227.4 4.3 spread_step_attention.3
  239.2 3.4 collective-permute-done.95.refs_0_
  250.1 4.3 collective-permute-done.99.refs_0_
  260.0 3.6 collective-permute-done.98.refs_1_
  266.7 2.6 collective-permute-done.104.refs_1_
  277.6 12.5 %spread_step_mlp.3 = (bf16[36,1024,256]{2,1,0:T(8,128)(2,1)S(1)}, f32[4,512,256]{2,1,0:T(8,128)S(1)}, bf16[4,512,256]{2,1,0:T(8,128)(2,1)S(1)}, f32[2,128,1024]{2,1,0:T(8,128)S(1)}, bf16[2,128,1024]{2,1,0:T(8,128)(2,1)S(1)}) custom-call(s32[36,4]{1,0:T(8,128)S(1)} %bitcast.166, ...), custom_call_target="tpu_custom_call", output_to_operand_aliasing={{0}: (5, {})} | custom-call | tf_op jit(solution)/shard_map/spread_step_mlp/pallas_call | solution.py:383
  292.7 7.8 %collective-permute-done.111.far_ref = bf16[128,1024]{1,0:T(8,128)(2,1)S(1)} collective-permute-done((bf16[128,1024]{1,0:T(8,128)(2,1)S(1)}, bf16[128,1024]{1,0:T(8,128)(2,1)S(1)}, u32[]{:S(2)}, u32[]{:S(2)}) %collective-permute-start.111) | collective-permute-done | bytes 262176 | tf_op jit(solution)/shard_map/ppermute | solution.py:135
  302.1 7.0 %collective-permute-done.113.refs_3_.refs_7_ = bf16[128,1024]{1,0:T(8,128)(2,1)S(1)} collective-permute-done((bf16[128,1024]{1,0:T(8,128)(2,1)S(1)}, bf16[128,1024]{1,0:T(8,128)(2,1)S(1)}, u32[]{:S(2)}, u32[]{:S(2)}) %collective-permute-start.113) | collective-permute-done | bytes 262176 | tf_op jit(solution)/shard_map/ppermute | solution.py:135
  310.6 4.5 layer__mlp_back.1
  317.8 4.5 layer__weight_grads.1
  333.6 3.3 collective-permute-done.121.refs_0_
  340.5 7.1 %reduce_step_attention_back.2 = (bf16[36,1024,256]{2,1,0:T(8,128)(2,1)S(1)}, bf16[512,256]{1,0:T(8,128)(2,1)S(1)}, bf16[512,256]{1,0:T(8,128)(2,1)S(1)}, bf16[3,...) custom-call(s32[36,4]{1,0:T(8,128)S(1)} %bitcast.172, ...), custom_call_target="tpu_custom_call", output_to_operand_aliasing={{0}: (3, {})} | custom-call | tf_op jit(solution)/shard_map/reduce_step_attention_back/pallas_call | solution.py:383
  351.9 2.9 reduce_step_weight_grads.3
  366.5 3.9 collective-permute-done.130.refs_0_
  373.1 5.0 reduce_step_mlp_back.1
  383.9 4.6 reduce_step_weight_grads.4
  398.9 3.6 collective-permute-done.147.refs_0_
  405.6 7.0 %reduce_step_attention_back.3 = (bf16[36,1024,256]{2,1,0:T(8,128)(2,1)S(1)}, bf16[512,256]{1,0:T(8,128)(2,1)S(1)}, bf16[512,256]{1,0:T(8,128)(2,1)S(1)}, bf16[3,...) custom-call(s32[36,4]{1,0:T(8,128)S(1)} %bitcast.180, ...), custom_call_target="tpu_custom_call", output_to_operand_aliasing={{0}: (3, {})} | custom-call | tf_op jit(solution)/shard_map/reduce_step_attention_back/pallas_call | solution.py:383
  416.0 2.9 reduce_step_weight_grads.5
  419.0 2.5 collective-permute-done.154.refs_0_
  427.5 2.8 collective-permute-done.157
  436.6 5.2 collective-permute-done.158.refs_0_
  445.5 3.0 collective-permute-done.164.refs_0_
  452.1 3.0 collective-permute-done.162.refs_0_
  458.8 3.0 collective-permute-done.168.refs_0_
  465.4 3.0 collective-permute-done.166.refs_0_
  472.1 3.0 collective-permute-done.172.refs_0_
  478.8 2.9 collective-permute-done.170.refs_0_
  486.2 2.2 collective-permute-done.176.refs_0_
  494.7 3.4 reduce_step_cond_back.1
  503.0 2.4 collective-permute-done.181
  511.7 4.0 collective-permute-done.182.refs_0_
  570.8 3.1 collective-permute-done.205
  577.4 4.9 collective-permute-done.208.refs_1_
  584.3 31.6 %optimizer.2 = (f32[8,1024,256]{2,1,0:T(8,128)}, f32[8,1024,256]{2,1,0:T(8,128)}, f32[8,128]{1,0:T(8,128)S(1)}) custom-call(s32[8]{0:T(128)S(1)} %get-tuple-element.950.big_ref, s32[8]{0:T(128)S(1)} %get-tuple-element.1026.left_ref, s32[8]{0:T(128)S(1)} %get-tuple-element.1025.right_ref, s32[36,4]{1,0:T(8,128)S(1)} %bitcast.205, ...), custom_call_target="tpu_custom_call" | custom-call | tf_op jit(solution)/shard_map/optimizer/pallas_call | solution.py:857
  618.5 14.8 %optimizer.3 = (f32[8,1024,256]{2,1,0:T(8,128)}, f32[8,1024,256]{2,1,0:T(8,128)}, f32[8,128]{1,0:T(8,128)S(1)}) custom-call(s32[8]{0:T(128)S(1)} %get-tuple-element.950.big_ref, s32[8]{0:T(128)S(1)} %get-tuple-element.1026.left_ref, s32[8]{0:T(128)S(1)} %get-tuple-element.1025.right_ref, ...), custom_call_target="tpu_custom_call", output_to_operand_aliasing={{0}: (13, {}), {1}: (14, {})} | custom-call | tf_op jit(solution)/shard_map/optimizer/pallas_call | solution.py:857
  634.5 18.5 %collective-permute-start.212 = (f32[56,256]{1,0:T(8,128)S(1)}, f32[56,256]{1,0:T(8,128)S(1)}, u32[]{:S(2)}, u32[]{:S(2)}) collective-permute-start(f32[56,256]{1,0:T(8,128)S(1)} %add_add_fusion), channel_id=1, source_target_pairs={{0,16},{4,20},{8,24},{12,28},{16,0},{20,4},{24,8},{28,12},{1,17},{... | collective-permute-start | bytes 172040 | tf_op jit(solution)/shard_map/ppermute | solution.py:135
  655.9 2.7 update_tables.1
  (653 shorter events, 352.0 us)
Async XLA Ops:
  18.0 10.1 %collective-permute-start.2 = (bf16[32,256]{1,0:T(8,128)(2,1)S(1)}, bf16[32,256]{1,0:T(8,128)(2,1)S(1)}, u32[]{:S(2)}, u32[]{:S(2)}) collective-permute-start(bf16[32,256]{1,0:T(8,128)(2,1)S(1)} %pad_maximum_fusion.15), channel_id=1, source_target_pairs={{0,2},{1,3},{2,0},{3,1},{4,6},{5,7},{6,4},{7,5},{8,10},{9,11},{10,... | collective-permute-start | bytes 49160 | tf_op jit(solution)/shard_map/ppermute | solution.py:135
  29.0 11.7 %collective-permute-start.7 = (bf16[512,256]{1,0:T(8,128)(2,1)S(1)}, bf16[512,256]{1,0:T(8,128)(2,1)S(1)}, u32[]{:S(2)}, u32[]{:S(2)}) collective-permute-start(bf16[512,256]{1,0:T(8,128)(2,1)S(1)} %get-tuple-element.498), channel_id=1, source_target_pairs={{0,8},{8,16},{16,24},{24,28},{28,20},{20,12},{12,4},{4,0},{1,9},{9... | collective-permute-start | bytes 786440 | tf_op jit(solution)/shard_map/ppermute | solution.py:436
  38.6 11.3 %collective-permute-start.10 = (bf16[512,256]{1,0:T(8,128)(2,1)S(1)}, bf16[512,256]{1,0:T(8,128)(2,1)S(1)}, u32[]{:S(2)}, u32[]{:S(2)}) collective-permute-start(bf16[512,256]{1,0:T(8,128)(2,1)S(1)} %get-tuple-element.506), channel_id=1, source_target_pairs={{0,8},{8,16},{16,24},{24,28},{28,20},{20,12},{12,4},{4,0},{1,9},{9... | collective-permute-start | bytes 786440 | tf_op jit(solution)/shard_map/ppermute | solution.py:436
  39.7 10.1 %collective-permute-start.11 = (bf16[512,256]{1,0:T(8,128)(2,1)S(1)}, bf16[512,256]{1,0:T(8,128)(2,1)S(1)}, u32[]{:S(2)}, u32[]{:S(2)}) collective-permute-start(bf16[512,256]{1,0:T(8,128)(2,1)S(1)} %get-tuple-element.507), channel_id=1, source_target_pairs={{8,0},{16,8},{24,16},{28,24},{20,28},{12,20},{4,12},{0,4},{9,1},{1... | collective-permute-start | bytes 786440 | tf_op jit(solution)/shard_map/ppermute | solution.py:436
  44.2 11.1 %collective-permute-start.14 = (bf16[512,256]{1,0:T(8,128)(2,1)S(1)}, bf16[512,256]{1,0:T(8,128)(2,1)S(1)}, u32[]{:S(2)}, u32[]{:S(2)}) collective-permute-start(bf16[512,256]{1,0:T(8,128)(2,1)S(1)} %get-tuple-element.511), channel_id=1, source_target_pairs={{0,8},{8,16},{16,24},{24,28},{28,20},{20,12},{12,4},{4,0},{1,9},{9... | collective-permute-start | bytes 786440 | tf_op jit(solution)/shard_map/ppermute | solution.py:436
  45.4 10.0 %collective-permute-start.15 = (bf16[512,256]{1,0:T(8,128)(2,1)S(1)}, bf16[512,256]{1,0:T(8,128)(2,1)S(1)}, u32[]{:S(2)}, u32[]{:S(2)}) collective-permute-start(bf16[512,256]{1,0:T(8,128)(2,1)S(1)} %get-tuple-element.512), channel_id=1, source_target_pairs={{8,0},{16,8},{24,16},{28,24},{20,28},{12,20},{4,12},{0,4},{9,1},{1... | collective-permute-start | bytes 786440 | tf_op jit(solution)/shard_map/ppermute | solution.py:436
  59.5 11.8 %collective-permute-start.21 = (bf16[512,256]{1,0:T(8,128)(2,1)S(1)}, bf16[512,256]{1,0:T(8,128)(2,1)S(1)}, u32[]{:S(2)}, u32[]{:S(2)}) collective-permute-start(bf16[512,256]{1,0:T(8,128)(2,1)S(1)} %get-tuple-element.524), channel_id=1, source_target_pairs={{0,8},{8,16},{16,24},{24,28},{28,20},{20,12},{12,4},{4,0},{1,9},{9... | collective-permute-start | bytes 786440 | tf_op jit(solution)/shard_map/ppermute | solution.py:436
  60.6 11.4 %collective-permute-start.22 = (bf16[512,256]{1,0:T(8,128)(2,1)S(1)}, bf16[512,256]{1,0:T(8,128)(2,1)S(1)}, u32[]{:S(2)}, u32[]{:S(2)}) collective-permute-start(bf16[512,256]{1,0:T(8,128)(2,1)S(1)} %get-tuple-element.525), channel_id=1, source_target_pairs={{8,0},{16,8},{24,16},{28,24},{20,28},{12,20},{4,12},{0,4},{9,1},{1... | collective-permute-start | bytes 786440 | tf_op jit(solution)/shard_map/ppermute | solution.py:436
  67.4 14.6 %collective-permute-start.24 = (bf16[512,256]{1,0:T(8,128)(2,1)S(1)}, bf16[512,256]{1,0:T(8,128)(2,1)S(1)}, u32[]{:S(2)}, u32[]{:S(2)}) collective-permute-start(bf16[512,256]{1,0:T(8,128)(2,1)S(1)} %get-tuple-element.529), channel_id=1, source_target_pairs={{0,8},{8,16},{16,24},{24,28},{28,20},{20,12},{12,4},{4,0},{1,9},{9... | collective-permute-start | bytes 786440 | tf_op jit(solution)/shard_map/ppermute | solution.py:436
  68.0 14.0 %collective-permute-start.25 = (bf16[512,256]{1,0:T(8,128)(2,1)S(1)}, bf16[512,256]{1,0:T(8,128)(2,1)S(1)}, u32[]{:S(2)}, u32[]{:S(2)}) collective-permute-start(bf16[512,256]{1,0:T(8,128)(2,1)S(1)} %get-tuple-element.530), channel_id=1, source_target_pairs={{8,0},{16,8},{24,16},{28,24},{20,28},{12,20},{4,12},{0,4},{9,1},{1... | collective-permute-start | bytes 786440 | tf_op jit(solution)/shard_map/ppermute | solution.py:436
  97.8 11.5 %collective-permute-start.33 = (f32[16,8,256]{2,0,1:T(8,128)S(1)}, f32[16,8,256]{2,0,1:T(8,128)S(1)}, u32[]{:S(2)}, u32[]{:S(2)}) collective-permute-start(f32[16,8,256]{2,0,1:T(8,128)S(1)} %slice_select_fusion), channel_id=1, source_target_pairs={{0,16},{4,20},{8,24},{12,28},{16,0},{20,4},{24,8},{28,12},{1,17},{... | collective-permute-start | bytes 393224 | tf_op jit(solution)/shard_map/ppermute | solution.py:135
  99.5 14.7 %collective-permute-start.37 = (bf16[512,256]{1,0:T(8,128)(2,1)S(1)}, bf16[512,256]{1,0:T(8,128)(2,1)S(1)}, u32[]{:S(2)}, u32[]{:S(2)}) collective-permute-start(bf16[512,256]{1,0:T(8,128)(2,1)S(1)} %get-tuple-element.550), channel_id=1, source_target_pairs={{0,8},{8,16},{16,24},{24,28},{28,20},{20,12},{12,4},{4,0},{1,9},{9... | collective-permute-start | bytes 786440 | tf_op jit(solution)/shard_map/ppermute | solution.py:436
  100.6 13.6 %collective-permute-start.38 = (bf16[512,256]{1,0:T(8,128)(2,1)S(1)}, bf16[512,256]{1,0:T(8,128)(2,1)S(1)}, u32[]{:S(2)}, u32[]{:S(2)}) collective-permute-start(bf16[512,256]{1,0:T(8,128)(2,1)S(1)} %get-tuple-element.551), channel_id=1, source_target_pairs={{8,0},{16,8},{24,16},{28,24},{20,28},{12,20},{4,12},{0,4},{9,1},{1... | collective-permute-start | bytes 786440 | tf_op jit(solution)/shard_map/ppermute | solution.py:436
  110.4 9.9 %collective-permute-start.40 = (bf16[512,256]{1,0:T(8,128)(2,1)S(1)}, bf16[512,256]{1,0:T(8,128)(2,1)S(1)}, u32[]{:S(2)}, u32[]{:S(2)}) collective-permute-start(bf16[512,256]{1,0:T(8,128)(2,1)S(1)} %get-tuple-element.557), channel_id=1, source_target_pairs={{0,8},{8,16},{16,24},{24,28},{28,20},{20,12},{12,4},{4,0},{1,9},{9... | collective-permute-start | bytes 786440 | tf_op jit(solution)/shard_map/ppermute | solution.py:436
  115.3 10.4 %collective-permute-start.45 = (bf16[512,256]{1,0:T(8,128)(2,1)S(1)}, bf16[512,256]{1,0:T(8,128)(2,1)S(1)}, u32[]{:S(2)}, u32[]{:S(2)}) collective-permute-start(bf16[512,256]{1,0:T(8,128)(2,1)S(1)} %get-tuple-element.562), channel_id=1, source_target_pairs={{0,8},{8,16},{16,24},{24,28},{28,20},{20,12},{12,4},{4,0},{1,9},{9... | collective-permute-start | bytes 786440 | tf_op jit(solution)/shard_map/ppermute | solution.py:436
  129.0 9.8 %collective-permute-start.52 = (bf16[128,1024]{1,0:T(8,128)(2,1)S(1)}, bf16[128,1024]{1,0:T(8,128)(2,1)S(1)}, u32[]{:S(2)}, u32[]{:S(2)}) collective-permute-start(bf16[128,1024]{1,0:T(8,128)(2,1)S(1)} %get-tuple-element.573.refs_3_), channel_id=1, source_target_pairs={{0,1},{1,0},{2,3},{3,2},{4,5},{5,4},{6,7},{7,6},{8,9},{9,8},{10,11... | collective-permute-start | bytes 786440 | tf_op jit(solution)/shard_map/ppermute | solution.py:135
  130.0 10.7 %collective-permute-start.50 = (bf16[512,256]{1,0:T(8,128)(2,1)S(1)}, bf16[512,256]{1,0:T(8,128)(2,1)S(1)}, u32[]{:S(2)}, u32[]{:S(2)}) collective-permute-start(bf16[512,256]{1,0:T(8,128)(2,1)S(1)} %get-tuple-element.579), channel_id=1, source_target_pairs={{0,8},{8,16},{16,24},{24,28},{28,20},{20,12},{12,4},{4,0},{1,9},{9... | collective-permute-start | bytes 786440 | tf_op jit(solution)/shard_map/ppermute | solution.py:436
  136.7 10.6 %collective-permute-start.48 = (bf16[512,256]{1,0:T(8,128)(2,1)S(1)}, bf16[512,256]{1,0:T(8,128)(2,1)S(1)}, u32[]{:S(2)}, u32[]{:S(2)}) collective-permute-start(bf16[512,256]{1,0:T(8,128)(2,1)S(1)} %get-tuple-element.577), channel_id=1, source_target_pairs={{0,8},{8,16},{16,24},{24,28},{28,20},{20,12},{12,4},{4,0},{1,9},{9... | collective-permute-start | bytes 786440 | tf_op jit(solution)/shard_map/ppermute | solution.py:436
  138.1 11.8 %collective-permute-start.49 = (bf16[512,256]{1,0:T(8,128)(2,1)S(1)}, bf16[512,256]{1,0:T(8,128)(2,1)S(1)}, u32[]{:S(2)}, u32[]{:S(2)}) collective-permute-start(bf16[512,256]{1,0:T(8,128)(2,1)S(1)} %get-tuple-element.578), channel_id=1, source_target_pairs={{8,0},{16,8},{24,16},{28,24},{20,28},{12,20},{4,12},{0,4},{9,1},{1... | collective-permute-start | bytes 786440 | tf_op jit(solution)/shard_map/ppermute | solution.py:436
  138.8 11.1 %collective-permute-start.54 = (bf16[128,1024]{1,0:T(8,128)(2,1)S(1)}, bf16[128,1024]{1,0:T(8,128)(2,1)S(1)}, u32[]{:S(2)}, u32[]{:S(2)}) collective-permute-start(bf16[128,1024]{1,0:T(8,128)(2,1)S(1)} %collective-permute-done.53.refs_5_), channel_id=1, source_target_pairs={{0,1},{1,0},{2,3},{3,2},{4,5},{5,4},{6,7},{7,6},{8,9},{9,8},{10,11... | collective-permute-start | bytes 786440 | tf_op jit(solution)/shard_map/ppermute | solution.py:135
  158.4 11.0 %collective-permute-start.63 = (bf16[512,256]{1,0:T(8,128)(2,1)S(1)}, bf16[512,256]{1,0:T(8,128)(2,1)S(1)}, u32[]{:S(2)}, u32[]{:S(2)}) collective-permute-start(bf16[512,256]{1,0:T(8,128)(2,1)S(1)} %get-tuple-element.595), channel_id=1, source_target_pairs={{0,8},{8,16},{16,24},{24,28},{28,20},{20,12},{12,4},{4,0},{1,9},{9... | collective-permute-start | bytes 786440 | tf_op jit(solution)/shard_map/ppermute | solution.py:436
  159.2 11.1 %collective-permute-start.64 = (bf16[512,256]{1,0:T(8,128)(2,1)S(1)}, bf16[512,256]{1,0:T(8,128)(2,1)S(1)}, u32[]{:S(2)}, u32[]{:S(2)}) collective-permute-start(bf16[512,256]{1,0:T(8,128)(2,1)S(1)} %get-tuple-element.596), channel_id=1, source_target_pairs={{8,0},{16,8},{24,16},{28,24},{20,28},{12,20},{4,12},{0,4},{9,1},{1... | collective-permute-start | bytes 786440 | tf_op jit(solution)/shard_map/ppermute | solution.py:436
  173.3 10.3 %collective-permute-start.74 = (bf16[128,1024]{1,0:T(8,128)(2,1)S(1)}, bf16[128,1024]{1,0:T(8,128)(2,1)S(1)}, u32[]{:S(2)}, u32[]{:S(2)}) collective-permute-start(bf16[128,1024]{1,0:T(8,128)(2,1)S(1)} %get-tuple-element.601.refs_3_), channel_id=1, source_target_pairs={{0,2},{1,3},{2,0},{3,1},{4,6},{5,7},{6,4},{7,5},{8,10},{9,11},{10,... | collective-permute-start | bytes 786440 | tf_op jit(solution)/shard_map/ppermute | solution.py:135
  182.1 10.8 %collective-permute-start.71 = (bf16[512,256]{1,0:T(8,128)(2,1)S(1)}, bf16[512,256]{1,0:T(8,128)(2,1)S(1)}, u32[]{:S(2)}, u32[]{:S(2)}) collective-permute-start(bf16[512,256]{1,0:T(8,128)(2,1)S(1)} %get-tuple-element.616), channel_id=1, source_target_pairs={{0,8},{8,16},{16,24},{24,28},{28,20},{20,12},{12,4},{4,0},{1,9},{9... | collective-permute-start | bytes 786440 | tf_op jit(solution)/shard_map/ppermute | solution.py:436
  183.7 11.8 %collective-permute-start.72 = (bf16[512,256]{1,0:T(8,128)(2,1)S(1)}, bf16[512,256]{1,0:T(8,128)(2,1)S(1)}, u32[]{:S(2)}, u32[]{:S(2)}) collective-permute-start(bf16[512,256]{1,0:T(8,128)(2,1)S(1)} %get-tuple-element.617), channel_id=1, source_target_pairs={{8,0},{16,8},{24,16},{28,24},{20,28},{12,20},{4,12},{0,4},{9,1},{1... | collective-permute-start | bytes 786440 | tf_op jit(solution)/shard_map/ppermute | solution.py:436
  184.2 14.3 %collective-permute-start.75 = (bf16[128,1024]{1,0:T(8,128)(2,1)S(1)}, bf16[128,1024]{1,0:T(8,128)(2,1)S(1)}, u32[]{:S(2)}, u32[]{:S(2)}) collective-permute-start(bf16[128,1024]{1,0:T(8,128)(2,1)S(1)} %collective-permute-done.74.refs_5_), channel_id=1, source_target_pairs={{0,1},{1,0},{2,3},{3,2},{4,5},{5,4},{6,7},{7,6},{8,9},{9,8},{10,11... | collective-permute-start | bytes 786440 | tf_op jit(solution)/shard_map/ppermute | solution.py:135
  208.8 10.7 %collective-permute-start.84 = (bf16[512,256]{1,0:T(8,128)(2,1)S(1)}, bf16[512,256]{1,0:T(8,128)(2,1)S(1)}, u32[]{:S(2)}, u32[]{:S(2)}) collective-permute-start(bf16[512,256]{1,0:T(8,128)(2,1)S(1)} %get-tuple-element.632), channel_id=1, source_target_pairs={{0,8},{8,16},{16,24},{24,28},{28,20},{20,12},{12,4},{4,0},{1,9},{9... | collective-permute-start | bytes 786440 | tf_op jit(solution)/shard_map/ppermute | solution.py:436
  209.7 10.8 %collective-permute-start.85 = (bf16[512,256]{1,0:T(8,128)(2,1)S(1)}, bf16[512,256]{1,0:T(8,128)(2,1)S(1)}, u32[]{:S(2)}, u32[]{:S(2)}) collective-permute-start(bf16[512,256]{1,0:T(8,128)(2,1)S(1)} %get-tuple-element.633), channel_id=1, source_target_pairs={{8,0},{16,8},{24,16},{28,24},{20,28},{12,20},{4,12},{0,4},{9,1},{1... | collective-permute-start | bytes 786440 | tf_op jit(solution)/shard_map/ppermute | solution.py:436
  237.1 11.1 %collective-permute-start.92 = (bf16[512,256]{1,0:T(8,128)(2,1)S(1)}, bf16[512,256]{1,0:T(8,128)(2,1)S(1)}, u32[]{:S(2)}, u32[]{:S(2)}) collective-permute-start(bf16[512,256]{1,0:T(8,128)(2,1)S(1)} %get-tuple-element.657), channel_id=1, source_target_pairs={{0,8},{8,16},{16,24},{24,28},{28,20},{20,12},{12,4},{4,0},{1,9},{9... | collective-permute-start | bytes 786440 | tf_op jit(solution)/shard_map/ppermute | solution.py:436
  237.5 11.1 %collective-permute-start.93 = (bf16[512,256]{1,0:T(8,128)(2,1)S(1)}, bf16[512,256]{1,0:T(8,128)(2,1)S(1)}, u32[]{:S(2)}, u32[]{:S(2)}) collective-permute-start(bf16[512,256]{1,0:T(8,128)(2,1)S(1)} %get-tuple-element.658), channel_id=1, source_target_pairs={{8,0},{16,8},{24,16},{28,24},{20,28},{12,20},{4,12},{0,4},{9,1},{1... | collective-permute-start | bytes 786440 | tf_op jit(solution)/shard_map/ppermute | solution.py:436
  245.5 10.1 %collective-permute-start.100 = (bf16[512,256]{1,0:T(8,128)(2,1)S(1)}, bf16[512,256]{1,0:T(8,128)(2,1)S(1)}, u32[]{:S(2)}, u32[]{:S(2)}) collective-permute-start(bf16[512,256]{1,0:T(8,128)(2,1)S(1)} %get-tuple-element.670), channel_id=1, source_target_pairs={{8,0},{16,8},{24,16},{28,24},{20,28},{12,20},{4,12},{0,4},{9,1},{1... | collective-permute-start | bytes 786440 | tf_op jit(solution)/shard_map/ppermute | solution.py:436
  247.2 10.2 %collective-permute-start.108 = (bf16[128,1024]{1,0:T(8,128)(2,1)S(1)}, bf16[128,1024]{1,0:T(8,128)(2,1)S(1)}, u32[]{:S(2)}, u32[]{:S(2)}) collective-permute-start(bf16[128,1024]{1,0:T(8,128)(2,1)S(1)} %get-tuple-element.663.refs_5_.refs_1_), channel_id=1, source_target_pairs={{0,2},{1,3},{2,0},{3,1},{4,6},{5,7},{6,4},{7,5},{8,10},{9,11},{10,... | collective-permute-start | bytes 786440 | tf_op jit(solution)/shard_map/ppermute | solution.py:135
  248.2 10.5 %collective-permute-start.107 = (bf16[128,1024]{1,0:T(8,128)(2,1)S(1)}, bf16[128,1024]{1,0:T(8,128)(2,1)S(1)}, u32[]{:S(2)}, u32[]{:S(2)}) collective-permute-start(bf16[128,1024]{1,0:T(8,128)(2,1)S(1)} %get-tuple-element.663.refs_5_.refs_1_), channel_id=1, source_target_pairs={{0,1},{1,0},{2,3},{3,2},{4,5},{5,4},{6,7},{7,6},{8,9},{9,8},{10,11... | collective-permute-start | bytes 786440 | tf_op jit(solution)/shard_map/ppermute | solution.py:135
  249.5 10.5 %collective-permute-start.97 = (bf16[512,256]{1,0:T(8,128)(2,1)S(1)}, bf16[512,256]{1,0:T(8,128)(2,1)S(1)}, u32[]{:S(2)}, u32[]{:S(2)}) collective-permute-start(bf16[512,256]{1,0:T(8,128)(2,1)S(1)} %get-tuple-element.667), channel_id=1, source_target_pairs={{0,8},{8,16},{16,24},{24,28},{28,20},{20,12},{12,4},{4,0},{1,9},{9... | collective-permute-start | bytes 786440 | tf_op jit(solution)/shard_map/ppermute | solution.py:436
  256.6 10.1 %collective-permute-start.103 = (bf16[512,256]{1,0:T(8,128)(2,1)S(1)}, bf16[512,256]{1,0:T(8,128)(2,1)S(1)}, u32[]{:S(2)}, u32[]{:S(2)}) collective-permute-start(bf16[512,256]{1,0:T(8,128)(2,1)S(1)} %get-tuple-element.675), channel_id=1, source_target_pairs={{0,8},{8,16},{16,24},{24,28},{28,20},{20,12},{12,4},{4,0},{1,9},{9... | collective-permute-start | bytes 786440 | tf_op jit(solution)/shard_map/ppermute | solution.py:436
  257.4 11.8 %collective-permute-start.104 = (bf16[512,256]{1,0:T(8,128)(2,1)S(1)}, bf16[512,256]{1,0:T(8,128)(2,1)S(1)}, u32[]{:S(2)}, u32[]{:S(2)}) collective-permute-start(bf16[512,256]{1,0:T(8,128)(2,1)S(1)} %get-tuple-element.676), channel_id=1, source_target_pairs={{8,0},{16,8},{24,16},{28,24},{20,28},{12,20},{4,12},{0,4},{9,1},{1... | collective-permute-start | bytes 786440 | tf_op jit(solution)/shard_map/ppermute | solution.py:436
  258.6 13.6 %collective-permute-start.109 = (bf16[128,1024]{1,0:T(8,128)(2,1)S(1)}, bf16[128,1024]{1,0:T(8,128)(2,1)S(1)}, u32[]{:S(2)}, u32[]{:S(2)}) collective-permute-start(bf16[128,1024]{1,0:T(8,128)(2,1)S(1)} %collective-permute-done.108.refs_7_.refs_3_), channel_id=1, source_target_pairs={{0,1},{1,0},{2,3},{3,2},{4,5},{5,4},{6,7},{7,6},{8,9},{9,8},{10,11... | collective-permute-start | bytes 786440 | tf_op jit(solution)/shard_map/ppermute | solution.py:135
  421.9 11.5 %collective-permute-start.160 = (bf16[512,256]{1,0:T(8,128)(2,1)S(1)}, bf16[512,256]{1,0:T(8,128)(2,1)S(1)}, u32[]{:S(2)}, u32[]{:S(2)}) collective-permute-start(bf16[512,256]{1,0:T(8,128)(2,1)S(1)} %get-tuple-element.807), channel_id=1, source_target_pairs={{8,0},{16,8},{24,16},{28,24},{20,28},{12,20},{4,12},{0,4},{9,1},{1... | collective-permute-start | bytes 786440 | tf_op jit(solution)/shard_map/ppermute | solution.py:510
  422.6 10.8 %collective-permute-start.161 = (bf16[512,256]{1,0:T(8,128)(2,1)S(1)}, bf16[512,256]{1,0:T(8,128)(2,1)S(1)}, u32[]{:S(2)}, u32[]{:S(2)}) collective-permute-start(bf16[512,256]{1,0:T(8,128)(2,1)S(1)} %get-tuple-element.808), channel_id=1, source_target_pairs={{0,8},{8,16},{16,24},{24,28},{28,20},{20,12},{12,4},{4,0},{1,9},{9... | collective-permute-start | bytes 786440 | tf_op jit(solution)/shard_map/ppermute | solution.py:510
  431.4 10.4 %collective-permute-start.158 = (bf16[608,256]{1,0:T(8,128)(2,1)S(1)}, bf16[608,256]{1,0:T(8,128)(2,1)S(1)}, u32[]{:S(2)}, u32[]{:S(2)}) collective-permute-start(bf16[608,256]{1,0:T(8,128)(2,1)S(1)} %get-tuple-element.821), channel_id=1, source_target_pairs={{8,0},{16,8},{24,16},{28,24},{20,28},{12,20},{4,12},{0,4},{9,1},{1... | collective-permute-start | bytes 933896 | tf_op jit(solution)/shard_map/ppermute | solution.py:510
  432.0 10.3 %collective-permute-start.159 = (bf16[608,256]{1,0:T(8,128)(2,1)S(1)}, bf16[608,256]{1,0:T(8,128)(2,1)S(1)}, u32[]{:S(2)}, u32[]{:S(2)}) collective-permute-start(bf16[608,256]{1,0:T(8,128)(2,1)S(1)} %get-tuple-element.822), channel_id=1, source_target_pairs={{0,8},{8,16},{16,24},{24,28},{28,20},{20,12},{12,4},{4,0},{1,9},{9... | collective-permute-start | bytes 933896 | tf_op jit(solution)/shard_map/ppermute | solution.py:510
  434.5 13.9 %collective-permute-start.164 = (bf16[608,256]{1,0:T(8,128)(2,1)S(1)}, bf16[608,256]{1,0:T(8,128)(2,1)S(1)}, u32[]{:S(2)}, u32[]{:S(2)}) collective-permute-start(bf16[608,256]{1,0:T(8,128)(2,1)S(1)} %get-tuple-element.827), channel_id=1, source_target_pairs={{8,0},{16,8},{24,16},{28,24},{20,28},{12,20},{4,12},{0,4},{9,1},{1... | collective-permute-start | bytes 933896 | tf_op jit(solution)/shard_map/ppermute | solution.py:510
  435.2 13.8 %collective-permute-start.165 = (bf16[608,256]{1,0:T(8,128)(2,1)S(1)}, bf16[608,256]{1,0:T(8,128)(2,1)S(1)}, u32[]{:S(2)}, u32[]{:S(2)}) collective-permute-start(bf16[608,256]{1,0:T(8,128)(2,1)S(1)} %get-tuple-element.828), channel_id=1, source_target_pairs={{0,8},{8,16},{16,24},{24,28},{28,20},{20,12},{12,4},{4,0},{1,9},{9... | collective-permute-start | bytes 933896 | tf_op jit(solution)/shard_map/ppermute | solution.py:510
  443.4 11.7 %collective-permute-start.162 = (bf16[608,256]{1,0:T(8,128)(2,1)S(1)}, bf16[608,256]{1,0:T(8,128)(2,1)S(1)}, u32[]{:S(2)}, u32[]{:S(2)}) collective-permute-start(bf16[608,256]{1,0:T(8,128)(2,1)S(1)} %get-tuple-element.825), channel_id=1, source_target_pairs={{8,0},{16,8},{24,16},{28,24},{20,28},{12,20},{4,12},{0,4},{9,1},{1... | collective-permute-start | bytes 933896 | tf_op jit(solution)/shard_map/ppermute | solution.py:510
  444.9 10.7 %collective-permute-start.163 = (bf16[608,256]{1,0:T(8,128)(2,1)S(1)}, bf16[608,256]{1,0:T(8,128)(2,1)S(1)}, u32[]{:S(2)}, u32[]{:S(2)}) collective-permute-start(bf16[608,256]{1,0:T(8,128)(2,1)S(1)} %get-tuple-element.826), channel_id=1, source_target_pairs={{0,8},{8,16},{16,24},{24,28},{28,20},{20,12},{12,4},{4,0},{1,9},{9... | collective-permute-start | bytes 933896 | tf_op jit(solution)/shard_map/ppermute | solution.py:510
  450.0 11.8 %collective-permute-start.168 = (bf16[608,256]{1,0:T(8,128)(2,1)S(1)}, bf16[608,256]{1,0:T(8,128)(2,1)S(1)}, u32[]{:S(2)}, u32[]{:S(2)}) collective-permute-start(bf16[608,256]{1,0:T(8,128)(2,1)S(1)} %get-tuple-element.833), channel_id=1, source_target_pairs={{8,0},{16,8},{24,16},{28,24},{20,28},{12,20},{4,12},{0,4},{9,1},{1... | collective-permute-start | bytes 933896 | tf_op jit(solution)/shard_map/ppermute | solution.py:510
  451.5 10.8 %collective-permute-start.169 = (bf16[608,256]{1,0:T(8,128)(2,1)S(1)}, bf16[608,256]{1,0:T(8,128)(2,1)S(1)}, u32[]{:S(2)}, u32[]{:S(2)}) collective-permute-start(bf16[608,256]{1,0:T(8,128)(2,1)S(1)} %get-tuple-element.834), channel_id=1, source_target_pairs={{0,8},{8,16},{16,24},{24,28},{28,20},{20,12},{12,4},{4,0},{1,9},{9... | collective-permute-start | bytes 933896 | tf_op jit(solution)/shard_map/ppermute | solution.py:510
  456.7 11.7 %collective-permute-start.166 = (bf16[608,256]{1,0:T(8,128)(2,1)S(1)}, bf16[608,256]{1,0:T(8,128)(2,1)S(1)}, u32[]{:S(2)}, u32[]{:S(2)}) collective-permute-start(bf16[608,256]{1,0:T(8,128)(2,1)S(1)} %get-tuple-element.831), channel_id=1, source_target_pairs={{8,0},{16,8},{24,16},{28,24},{20,28},{12,20},{4,12},{0,4},{9,1},{1... | collective-permute-start | bytes 933896 | tf_op jit(solution)/shard_map/ppermute | solution.py:510
  458.3 10.7 %collective-permute-start.167 = (bf16[608,256]{1,0:T(8,128)(2,1)S(1)}, bf16[608,256]{1,0:T(8,128)(2,1)S(1)}, u32[]{:S(2)}, u32[]{:S(2)}) collective-permute-start(bf16[608,256]{1,0:T(8,128)(2,1)S(1)} %get-tuple-element.832), channel_id=1, source_target_pairs={{0,8},{8,16},{16,24},{24,28},{28,20},{20,12},{12,4},{4,0},{1,9},{9... | collective-permute-start | bytes 933896 | tf_op jit(solution)/shard_map/ppermute | solution.py:510
  463.3 11.8 %collective-permute-start.172 = (bf16[608,256]{1,0:T(8,128)(2,1)S(1)}, bf16[608,256]{1,0:T(8,128)(2,1)S(1)}, u32[]{:S(2)}, u32[]{:S(2)}) collective-permute-start(bf16[608,256]{1,0:T(8,128)(2,1)S(1)} %get-tuple-element.839), channel_id=1, source_target_pairs={{8,0},{16,8},{24,16},{28,24},{20,28},{12,20},{4,12},{0,4},{9,1},{1... | collective-permute-start | bytes 933896 | tf_op jit(solution)/shard_map/ppermute | solution.py:510
  464.9 10.8 %collective-permute-start.173 = (bf16[608,256]{1,0:T(8,128)(2,1)S(1)}, bf16[608,256]{1,0:T(8,128)(2,1)S(1)}, u32[]{:S(2)}, u32[]{:S(2)}) collective-permute-start(bf16[608,256]{1,0:T(8,128)(2,1)S(1)} %get-tuple-element.840), channel_id=1, source_target_pairs={{0,8},{8,16},{16,24},{24,28},{28,20},{20,12},{12,4},{4,0},{1,9},{9... | collective-permute-start | bytes 933896 | tf_op jit(solution)/shard_map/ppermute | solution.py:510
  470.1 11.7 %collective-permute-start.170 = (bf16[608,256]{1,0:T(8,128)(2,1)S(1)}, bf16[608,256]{1,0:T(8,128)(2,1)S(1)}, u32[]{:S(2)}, u32[]{:S(2)}) collective-permute-start(bf16[608,256]{1,0:T(8,128)(2,1)S(1)} %get-tuple-element.837), channel_id=1, source_target_pairs={{8,0},{16,8},{24,16},{28,24},{20,28},{12,20},{4,12},{0,4},{9,1},{1... | collective-permute-start | bytes 933896 | tf_op jit(solution)/shard_map/ppermute | solution.py:510
  471.5 10.8 %collective-permute-start.171 = (bf16[608,256]{1,0:T(8,128)(2,1)S(1)}, bf16[608,256]{1,0:T(8,128)(2,1)S(1)}, u32[]{:S(2)}, u32[]{:S(2)}) collective-permute-start(bf16[608,256]{1,0:T(8,128)(2,1)S(1)} %get-tuple-element.838), channel_id=1, source_target_pairs={{0,8},{8,16},{16,24},{24,28},{28,20},{20,12},{12,4},{4,0},{1,9},{9... | collective-permute-start | bytes 933896 | tf_op jit(solution)/shard_map/ppermute | solution.py:510
  476.7 11.7 %collective-permute-start.176 = (bf16[608,256]{1,0:T(8,128)(2,1)S(1)}, bf16[608,256]{1,0:T(8,128)(2,1)S(1)}, u32[]{:S(2)}, u32[]{:S(2)}) collective-permute-start(bf16[608,256]{1,0:T(8,128)(2,1)S(1)} %get-tuple-element.845), channel_id=1, source_target_pairs={{8,0},{16,8},{24,16},{28,24},{20,28},{12,20},{4,12},{0,4},{9,1},{1... | collective-permute-start | bytes 933896 | tf_op jit(solution)/shard_map/ppermute | solution.py:510
  478.2 10.8 %collective-permute-start.177 = (bf16[608,256]{1,0:T(8,128)(2,1)S(1)}, bf16[608,256]{1,0:T(8,128)(2,1)S(1)}, u32[]{:S(2)}, u32[]{:S(2)}) collective-permute-start(bf16[608,256]{1,0:T(8,128)(2,1)S(1)} %get-tuple-element.846), channel_id=1, source_target_pairs={{0,8},{8,16},{16,24},{24,28},{28,20},{20,12},{12,4},{4,0},{1,9},{9... | collective-permute-start | bytes 933896 | tf_op jit(solution)/shard_map/ppermute | solution.py:510
  484.2 9.9 %collective-permute-start.174 = (bf16[512,256]{1,0:T(8,128)(2,1)S(1)}, bf16[512,256]{1,0:T(8,128)(2,1)S(1)}, u32[]{:S(2)}, u32[]{:S(2)}) collective-permute-start(bf16[512,256]{1,0:T(8,128)(2,1)S(1)} %get-tuple-element.843), channel_id=1, source_target_pairs={{8,0},{16,8},{24,16},{28,24},{20,28},{12,20},{4,12},{0,4},{9,1},{1... | collective-permute-start | bytes 786440 | tf_op jit(solution)/shard_map/ppermute | solution.py:510
  498.2 10.3 %collective-permute-start.184 = (bf16[512,256]{1,0:T(8,128)(2,1)S(1)}, bf16[512,256]{1,0:T(8,128)(2,1)S(1)}, u32[]{:S(2)}, u32[]{:S(2)}) collective-permute-start(bf16[512,256]{1,0:T(8,128)(2,1)S(1)} %get-tuple-element.874), channel_id=1, source_target_pairs={{8,0},{16,8},{24,16},{28,24},{20,28},{12,20},{4,12},{0,4},{9,1},{1... | collective-permute-start | bytes 786440 | tf_op jit(solution)/shard_map/ppermute | solution.py:510
  498.2 10.3 %collective-permute-start.185 = (bf16[512,256]{1,0:T(8,128)(2,1)S(1)}, bf16[512,256]{1,0:T(8,128)(2,1)S(1)}, u32[]{:S(2)}, u32[]{:S(2)}) collective-permute-start(bf16[512,256]{1,0:T(8,128)(2,1)S(1)} %get-tuple-element.875), channel_id=1, source_target_pairs={{0,8},{8,16},{16,24},{24,28},{28,20},{20,12},{12,4},{4,0},{1,9},{9... | collective-permute-start | bytes 786440 | tf_op jit(solution)/shard_map/ppermute | solution.py:510
  509.6 12.1 %collective-permute-start.188 = (bf16[544,256]{1,0:T(8,128)(2,1)S(1)}, bf16[544,256]{1,0:T(8,128)(2,1)S(1)}, u32[]{:S(2)}, u32[]{:S(2)}) collective-permute-start(bf16[544,256]{1,0:T(8,128)(2,1)S(1)} %get-tuple-element.881), channel_id=1, source_target_pairs={{8,0},{16,8},{24,16},{28,24},{20,28},{12,20},{4,12},{0,4},{9,1},{1... | collective-permute-start | bytes 835592 | tf_op jit(solution)/shard_map/ppermute | solution.py:510
  510.4 12.1 %collective-permute-start.189 = (bf16[544,256]{1,0:T(8,128)(2,1)S(1)}, bf16[544,256]{1,0:T(8,128)(2,1)S(1)}, u32[]{:S(2)}, u32[]{:S(2)}) collective-permute-start(bf16[544,256]{1,0:T(8,128)(2,1)S(1)} %get-tuple-element.882), channel_id=1, source_target_pairs={{0,8},{8,16},{16,24},{24,28},{28,20},{20,12},{12,4},{4,0},{1,9},{9... | collective-permute-start | bytes 835592 | tf_op jit(solution)/shard_map/ppermute | solution.py:510
  542.2 9.9 %collective-permute-start.195 = (bf16[512,256]{1,0:T(8,128)(2,1)S(1)}, bf16[512,256]{1,0:T(8,128)(2,1)S(1)}, u32[]{:S(2)}, u32[]{:S(2)}) collective-permute-start(bf16[512,256]{1,0:T(8,128)(2,1)S(1)} %get-tuple-element.892), channel_id=1, source_target_pairs={{0,8},{8,16},{16,24},{24,28},{28,20},{20,12},{12,4},{4,0},{1,9},{9... | collective-permute-start | bytes 786440 | tf_op jit(solution)/shard_map/ppermute | solution.py:510
  583.4 33.1 %collective-permute-start.210 = (f32[56,256]{1,0:T(8,128)S(1)}, f32[56,256]{1,0:T(8,128)S(1)}, u32[]{:S(2)}, u32[]{:S(2)}) collective-permute-start(f32[56,256]{1,0:T(8,128)S(1)} %select_add_fusion.2), channel_id=1, source_target_pairs={{0,4},{4,0},{8,12},{12,8},{16,20},{20,16},{24,28},{28,24},{1,5},{5... | collective-permute-start | bytes 172040 | tf_op jit(solution)/shard_map/ppermute | solution.py:135
  617.1 16.7 %collective-permute-start.211 = (f32[56,256]{1,0:T(8,128)S(1)}, f32[56,256]{1,0:T(8,128)S(1)}, u32[]{:S(2)}, u32[]{:S(2)}) collective-permute-start(f32[56,256]{1,0:T(8,128)S(1)} %add_add_fusion.1), channel_id=1, source_target_pairs={{0,8},{4,12},{8,0},{12,4},{16,24},{20,28},{24,16},{28,20},{1,9},{5... | collective-permute-start | bytes 172040 | tf_op jit(solution)/shard_map/ppermute | solution.py:135
  634.5 20.7 %collective-permute-start.212 = (f32[56,256]{1,0:T(8,128)S(1)}, f32[56,256]{1,0:T(8,128)S(1)}, u32[]{:S(2)}, u32[]{:S(2)}) collective-permute-start(f32[56,256]{1,0:T(8,128)S(1)} %add_add_fusion), channel_id=1, source_target_pairs={{0,16},{4,20},{8,24},{12,28},{16,0},{20,4},{24,8},{28,12},{1,17},{... | collective-permute-start | bytes 172040 | tf_op jit(solution)/shard_map/ppermute | solution.py:135
  (185 other events, 1722.8 us)
